TPU v7x, 32 devices: a whole 2x2x4 slice. The times are simulated.
32 devices in a mesh: dp: 4 (over z), seq: 8 (over y, x, core).
Axes of the slice: x: 2, y: 2, z: 4, core: 2. Of those that a mesh axis runs over, the one named last changes fastest.
Arguments:
- queries: bfloat16 [4096, 1024], P(('dp', 'seq')), may hold values from -6 to 6
- keys: bfloat16 [4096, 128], P(('dp', 'seq')), may hold values from -6 to 6
- values: bfloat16 [4096, 128], P(('dp', 'seq')), may hold values from -6 to 6
- d_out: bfloat16 [4096, 1024], P(('dp', 'seq')), may hold values from -6 to 6
- doc_lengths: int32 [11], replicated, may hold values from 1 to 768, as said below
Outputs:
- d_queries: bfloat16 [4096, 1024], P(('dp', 'seq'))
- key_gradient: bfloat16 [4096, 128], P(('dp', 'seq'))
- value_gradient: bfloat16 [4096, 128], P(('dp', 'seq'))
Inputs may be any that keep to these rules, and one draw needn't show every extreme that they name: `doc_lengths`: lengths of the 11 documents in order; they sum to 4096, and the longest has exactly 768 tokens.
All inputs are finite; a program needn't handle non-finite values.
Results may differ from a plain program's by a relative error of at most 0.008.
Values may be sent and summed in bfloat16 or wider, within the bound.
No kernel may reach another device: no remote copies, remote signals or barrier semaphores. Data moves between devices by JAX's collectives and lax.ppermute only.
A program may use at most 64 MiB of HBM per device.

v0:
```python
import math

import jax
import jax.numpy as jnp
from jax import lax
from jax.sharding import PartitionSpec as P

HEAD_SIZE = 128
GROUP = 8
DOC_MOST = 768


def from_behind(value, axis, steps):
    count = lax.axis_size(axis)
    leading, last = (max(0, -steps), min(count, count - steps))
    return lax.ppermute(value, axis, [(source, source + steps) for source in range(leading, last)])


def as_sent(shard):
    return jax.tree.map(lambda a: a.astype(jnp.bfloat16) if a.dtype == jnp.float32 else a, shard)


def doc_index(positions, doc_ends):
    return jnp.sum((positions[:, None] >= doc_ends[None, :]).astype(jnp.int32), axis=1)


def block_grads(q_rows, key_rows, value_rows, grad_rows, allowed, score_scale):
    scores = jnp.dot(q_rows, key_rows.T, preferred_element_type=jnp.float32) * score_scale
    scores = jnp.where(allowed, scores, -1e30)
    row_max = jnp.max(scores, axis=1, keepdims=True)
    exp_scores = jnp.exp(scores - row_max)
    attn_probs = exp_scores / jnp.sum(exp_scores, axis=1, keepdims=True)
    probs_low = attn_probs.astype(jnp.bfloat16)
    grad_probs = jnp.dot(grad_rows, value_rows.T, preferred_element_type=jnp.float32)
    row_delta = jnp.sum(attn_probs * grad_probs, axis=1, keepdims=True)
    grad_scores = (attn_probs * (grad_probs - row_delta) * score_scale).astype(jnp.bfloat16)
    grad_q = jnp.dot(grad_scores, key_rows, preferred_element_type=jnp.float32)
    grad_k = jnp.dot(grad_scores.T, q_rows, preferred_element_type=jnp.float32)
    grad_v = jnp.dot(probs_low.T, grad_rows, preferred_element_type=jnp.float32)
    return (grad_q, grad_k, grad_v)


def local(queries, keys, values, d_out, doc_lengths):
    tok_rows, q_width = queries.shape
    seq_devices = lax.axis_size("seq")
    kv_width = keys.shape[1]
    kv_heads = kv_width // HEAD_SIZE
    doc_ends = jnp.cumsum(doc_lengths)
    score_scale = 1.0 / math.sqrt(HEAD_SIZE)
    block_rows = tok_rows * seq_devices
    spread_k = jnp.broadcast_to(
        keys.reshape(tok_rows, kv_heads, 1, HEAD_SIZE), (tok_rows, kv_heads, GROUP, HEAD_SIZE)
    ).reshape(tok_rows, q_width)
    spread_v = jnp.broadcast_to(
        values.reshape(tok_rows, kv_heads, 1, HEAD_SIZE), (tok_rows, kv_heads, GROUP, HEAD_SIZE)
    ).reshape(tok_rows, q_width)
    head_q, head_g, head_k, head_v = (
        lax.all_to_all(queries, "seq", split_axis=1, concat_axis=0, tiled=True),
        lax.all_to_all(d_out, "seq", split_axis=1, concat_axis=0, tiled=True),
        lax.all_to_all(spread_k, "seq", split_axis=1, concat_axis=0, tiled=True),
        lax.all_to_all(spread_v, "seq", split_axis=1, concat_axis=0, tiled=True),
    )
    tail_pair = jnp.stack([head_k, head_v])
    prior_pair = from_behind(tail_pair, "dp", 1)
    all_k = jnp.concatenate([prior_pair[0], head_k], axis=0)
    all_v = jnp.concatenate([prior_pair[1], head_v], axis=0)
    block_start = lax.axis_index("dp") * block_rows
    query_span = min(512, block_rows)
    key_window = query_span + DOC_MOST
    steps_count = block_rows // query_span
    query_pos = block_start + jnp.arange(block_rows, dtype=jnp.int32)
    key_pos = block_start - block_rows + jnp.arange(block_rows + block_rows, dtype=jnp.int32)
    query_docs = doc_index(query_pos, doc_ends)
    key_docs = doc_index(key_pos, doc_ends)

    def step(totals, step_index):
        acc_k, acc_v = totals
        row_start = step_index * query_span
        key_start = row_start + block_rows - DOC_MOST
        q_rows = lax.dynamic_slice_in_dim(head_q, row_start, query_span, 0)
        g_rows = lax.dynamic_slice_in_dim(head_g, row_start, query_span, 0)
        key_rows = lax.dynamic_slice_in_dim(all_k, key_start, key_window, 0)
        value_rows = lax.dynamic_slice_in_dim(all_v, key_start, key_window, 0)
        q_pos = lax.dynamic_slice_in_dim(query_pos, row_start, query_span, 0)
        k_pos = lax.dynamic_slice_in_dim(key_pos, key_start, key_window, 0)
        q_docs = lax.dynamic_slice_in_dim(query_docs, row_start, query_span, 0)
        k_docs = lax.dynamic_slice_in_dim(key_docs, key_start, key_window, 0)
        allowed = (
            (q_docs[:, None] == k_docs[None, :])
            & (k_pos[None, :] <= q_pos[:, None])
            & (k_pos[None, :] >= 0)
        )
        grad_q, grad_k, grad_v = block_grads(
            q_rows, key_rows, value_rows, g_rows, allowed, score_scale
        )
        acc_k = lax.dynamic_update_slice_in_dim(
            acc_k, lax.dynamic_slice_in_dim(acc_k, key_start, key_window, 0) + grad_k, key_start, 0
        )
        acc_v = lax.dynamic_update_slice_in_dim(
            acc_v, lax.dynamic_slice_in_dim(acc_v, key_start, key_window, 0) + grad_v, key_start, 0
        )
        return ((acc_k, acc_v), grad_q.astype(jnp.bfloat16))

    empty_acc = jnp.zeros((block_rows + block_rows, HEAD_SIZE), jnp.float32)
    (acc_k, acc_v), q_blocks = lax.scan(
        step, (empty_acc, empty_acc), jnp.arange(steps_count, dtype=jnp.int32)
    )
    grads_q = q_blocks.reshape(block_rows, HEAD_SIZE)
    back_pair = from_behind(
        jnp.stack([acc_k[:block_rows], acc_v[:block_rows]]).astype(jnp.bfloat16), "dp", -1
    ).astype(jnp.float32)
    own_k = acc_k[block_rows:]
    own_v = acc_v[block_rows:]
    split_at = block_rows - block_rows
    term_k = jnp.concatenate([own_k[:split_at], own_k + back_pair[0]], axis=0)
    term_v = jnp.concatenate([own_v[:split_at], own_v + back_pair[1]], axis=0)
    tok_dq = lax.all_to_all(grads_q, "seq", split_axis=0, concat_axis=1, tiled=True)
    tok_k, tok_v = (
        lax.all_to_all(as_sent(term_k), "seq", split_axis=0, concat_axis=1, tiled=True).astype(
            term_k.dtype
        ),
        lax.all_to_all(as_sent(term_v), "seq", split_axis=0, concat_axis=1, tiled=True).astype(
            term_v.dtype
        ),
    )
    key_gradient = (
        jnp.sum(tok_k.reshape(tok_rows, kv_heads, GROUP, HEAD_SIZE), axis=2)
        .reshape(tok_rows, kv_width)
        .astype(jnp.bfloat16)
    )
    value_gradient = (
        jnp.sum(tok_v.reshape(tok_rows, kv_heads, GROUP, HEAD_SIZE), axis=2)
        .reshape(tok_rows, kv_width)
        .astype(jnp.bfloat16)
    )
    return (tok_dq, key_gradient, value_gradient)


def solution(mesh):
    in_specs = (
        P(("dp", "seq"), None),
        P(("dp", "seq"), None),
        P(("dp", "seq"), None),
        P(("dp", "seq"), None),
        P(),
    )
    out_specs = (P(("dp", "seq"), None), P(("dp", "seq"), None), P(("dp", "seq"), None))
    return jax.shard_map(local, mesh=mesh, in_specs=in_specs, out_specs=out_specs, check_vma=False)
```

profile of v0, /device:TPU:0, one launch (start us, length us, event | category | flops | bytes accessed | tf_op | source)
XLA Modules:
  0.0 109.7 jit_solution(16541012582635161159)
XLA Ops:
  0.7 1.5 %broadcast_in_dim.50 = bf16[128,8,128]{2,0,1:T(8,128)(2,1)} broadcast(bf16[128,128]{1,0:T(8,128)(2,1)} %param.8), dimensions={0,2} | broadcast | bytes 294912 | tf_op jit(solution)/shard_map/broadcast_in_dim | solution.py:51
  2.2 5.2 %all-to-all-start.1 = ((bf16[128,8,128]{2,0,1:T(8,128)(2,1)}), bf16[128,8,128]{2,0,1:T(8,128)(2,1)S(1)}, u32[]{:S(2)}, u32[]{:S(2)}) async-start(bf16[128,8,128]{2,0,1:T(8,128)(2,1)} %broadcast_in_dim.50), calls=%async_computation.1 | async-start | bytes 524288 | tf_op jit(solution)/shard_map/all_to_all | solution.py:60
  8.2 6.1 %all-to-all-done.1 = bf16[128,8,128]{2,0,1:T(8,128)(2,1)S(1)} async-done(((bf16[128,8,128]{2,0,1:T(8,128)(2,1)}), bf16[128,8,128]{2,0,1:T(8,128)(2,1)S(1)}, u32[]{:S(2)}, u32[]{:S(2)}) %all-to-all-start.1) | async-done | bytes 262176 | tf_op jit(solution)/shard_map/all_to_all | solution.py:60
  14.3 1.5 %broadcast_in_dim.51 = bf16[128,8,128]{2,0,1:T(8,128)(2,1)} broadcast(bf16[128,128]{1,0:T(8,128)(2,1)} %param.9), dimensions={0,2} | broadcast | bytes 294912 | tf_op jit(solution)/shard_map/broadcast_in_dim | solution.py:54
  15.8 3.4 %all-to-all-start.2 = ((bf16[128,8,128]{2,0,1:T(8,128)(2,1)}), bf16[128,8,128]{2,0,1:T(8,128)(2,1)S(1)}, u32[]{:S(2)}, u32[]{:S(2)}) async-start(bf16[128,8,128]{2,0,1:T(8,128)(2,1)} %broadcast_in_dim.51), calls=%async_computation.2 | async-start | bytes 524288 | tf_op jit(solution)/shard_map/all_to_all | solution.py:61
  20.0 6.1 %all-to-all-done.2 = bf16[128,8,128]{2,0,1:T(8,128)(2,1)S(1)} async-done(((bf16[128,8,128]{2,0,1:T(8,128)(2,1)}), bf16[128,8,128]{2,0,1:T(8,128)(2,1)S(1)}, u32[]{:S(2)}, u32[]{:S(2)}) %all-to-all-start.2) | async-done | bytes 262176 | tf_op jit(solution)/shard_map/all_to_all | solution.py:61
  26.0 3.4 %all-to-all-start.3 = ((bf16[128,8,128]{2,0,1:T(8,128)(2,1)}), bf16[128,8,128]{2,0,1:T(8,128)(2,1)S(1)}, u32[]{:S(2)}, u32[]{:S(2)}) async-start(bf16[128,8,128]{2,0,1:T(8,128)(2,1)} %copy_bitcast_fusion), calls=%async_computation.3 | async-start | bytes 524288 | tf_op jit(solution)/shard_map/all_to_all | solution.py:59
  29.5 3.5 %collective-permute-start = (bf16[2,1024,128]{2,1,0:T(8,128)(2,1)S(1)}, bf16[2,1024,128]{2,1,0:T(8,128)(2,1)S(1)}, u32[]{:S(2)}, u32[]{:S(2)}) collective-permute-start(bf16[2,1024,128]{2,1,0:T(8,128)(2,1)S(1)} %pad_maximum_fusion), channel_id=1, source_target_pairs={{0,8},{8,16},{16,24},{1,9},{9,17},{17,25},{2,10},{10,18},{18,26},{... | collective-permute-start | bytes 1572872 | tf_op jit(solution)/shard_map/ppermute | solution.py:16
  34.0 10.7 %collective-permute-done = bf16[2,1024,128]{2,1,0:T(8,128)(2,1)S(1)} collective-permute-done((bf16[2,1024,128]{2,1,0:T(8,128)(2,1)S(1)}, bf16[2,1024,128]{2,1,0:T(8,128)(2,1)S(1)}, u32[]{:S(2)}, u32[]{:S(2)}) %collective-permute-start) | collective-permute-done | bytes 524320 | tf_op jit(solution)/shard_map/ppermute | solution.py:16
  44.8 3.9 %all-to-all-start = ((bf16[128,8,128]{2,0,1:T(8,128)(2,1)}), bf16[128,8,128]{2,0,1:T(8,128)(2,1)S(1)}, u32[]{:S(2)}, u32[]{:S(2)}) async-start(bf16[128,8,128]{2,0,1:T(8,128)(2,1)} %copy_bitcast_fusion.1), calls=%async_computation | async-start | bytes 524288 | tf_op jit(solution)/shard_map/all_to_all | solution.py:58
  49.5 6.1 %all-to-all-done = bf16[128,8,128]{2,0,1:T(8,128)(2,1)S(1)} async-done(((bf16[128,8,128]{2,0,1:T(8,128)(2,1)}), bf16[128,8,128]{2,0,1:T(8,128)(2,1)S(1)}, u32[]{:S(2)}, u32[]{:S(2)}) %all-to-all-start) | async-done | bytes 262176 | tf_op jit(solution)/shard_map/all_to_all | solution.py:58
  55.7 14.9 %while.18 = (s32[]{:T(128)}, f32[2048,128]{1,0:T(8,128)S(1)}, f32[2048,128]{1,0:T(8,128)S(1)}, bf16[2,512,128]{2,1,0:T(8,128)(2,1)}, s32[2]{0:T(128)S(1)}, /*ind...) while((s32[]{:T(128)}, f32[2048,128]{1,0:T(8,128)S(1)}, ...), condition=%wide.region_7.8_spmd, body=%wide.region_3.7_spmd.sunk | while | flops 853671680 | bytes 28715108 | solution.py:105
  57.3 1.0 fusion.50
  62.0 1.2 %fusion.54 = bf16[2,512,128]{2,1,0:T(8,128)(2,1)} fusion(bf16[2,512,128]{2,1,0:T(8,128)(2,1)} %get-tuple-element.420, s32[]{:T(128)} %get-tuple-element.417, bf16[512,1280]{1,0:T(8,128)(2,1)S(1)} %multiply_convert_fusion.2, bf16[2048,128]{1,0:T(8,128)(2,1)S(1)} %get-tuple-element.446, s32[]{:T(128)S(6)} %select_n.41), kind=kOutput, calls=%fused_computation.14.clone.1 | convolution fusion | flops 167837696 | bytes 1769988 | tf_op jit(solution)/shard_map/while/body/eval_jaxpr/dot_general | solution.py:37
  64.7 1.0 fusion.50
  69.4 1.2 %fusion.54 = bf16[2,512,128]{2,1,0:T(8,128)(2,1)} fusion(bf16[2,512,128]{2,1,0:T(8,128)(2,1)} %get-tuple-element.420, s32[]{:T(128)} %get-tuple-element.417, bf16[512,1280]{1,0:T(8,128)(2,1)S(1)} %multiply_convert_fusion.2, bf16[2048,128]{1,0:T(8,128)(2,1)S(1)} %get-tuple-element.446, s32[]{:T(128)S(6)} %select_n.41), kind=kOutput, calls=%fused_computation.14.clone.1 | convolution fusion | flops 167837696 | bytes 1769988 | tf_op jit(solution)/shard_map/while/body/eval_jaxpr/dot_general | solution.py:37
  71.5 1.3 %collective-permute-start.1 = (bf16[2,1024,128]{2,1,0:T(8,128)(2,1)}, bf16[2,1024,128]{2,1,0:T(8,128)(2,1)}, u32[]{:S(2)}, u32[]{:S(2)}) collective-permute-start(bf16[2,1024,128]{2,1,0:T(8,128)(2,1)} %pad_maximum_fusion.3), channel_id=1, source_target_pairs={{8,0},{16,8},{24,16},{9,1},{17,9},{25,17},{10,2},{18,10},{26,18},{... | collective-permute-start | bytes 1572872 | tf_op jit(solution)/shard_map/ppermute | solution.py:16
  72.8 3.4 %all-to-all-start.4 = ((bf16[8,128,128]{2,1,0:T(8,128)(2,1)}), bf16[8,128,128]{2,1,0:T(8,128)(2,1)S(1)}, u32[]{:S(2)}, u32[]{:S(2)}) async-start(bf16[8,128,128]{2,1,0:T(8,128)(2,1)} %bitcast.16), calls=%async_computation.4 | async-start | bytes 524288 | tf_op jit(solution)/shard_map/all_to_all | solution.py:117
  76.2 11.3 %collective-permute-done.1 = bf16[2,1024,128]{2,1,0:T(8,128)(2,1)} collective-permute-done((bf16[2,1024,128]{2,1,0:T(8,128)(2,1)}, bf16[2,1024,128]{2,1,0:T(8,128)(2,1)}, u32[]{:S(2)}, u32[]{:S(2)}) %collective-permute-start.1) | collective-permute-done | bytes 524320 | tf_op jit(solution)/shard_map/ppermute | solution.py:16
  87.5 1.1 %convert_element_type.53 = f32[2,1024,128]{2,1,0:T(8,128)S(1)} convert(bf16[2,1024,128]{2,1,0:T(8,128)(2,1)} %collective-permute-done.1) | non-fusion elementwise | flops 262144 | bytes 1572864 | tf_op jit(solution)/shard_map/convert_element_type | solution.py:111
  89.5 9.3 %all_to_all.115 = bf16[8,128,128]{2,1,0:T(8,128)(2,1)S(1)} all-to-all(bf16[8,128,128]{2,1,0:T(8,128)(2,1)S(1)} %bitcast.74), channel_id=1, replica_groups=mesh['dp'=4,'seq'=8] {'seq'}, dimensions={0} | all-to-all | bytes 524288 | tf_op jit(solution)/shard_map/all_to_all | solution.py:119
  98.8 3.4 %all-to-all-start.6 = ((bf16[8,128,128]{2,1,0:T(8,128)(2,1)}), bf16[8,128,128]{2,1,0:T(8,128)(2,1)S(1)}, u32[]{:S(2)}, u32[]{:S(2)}) async-start(bf16[8,128,128]{2,1,0:T(8,128)(2,1)} %bitcast.24), calls=%async_computation.6 | async-start | bytes 524288 | tf_op jit(solution)/shard_map/all_to_all | solution.py:122
  102.4 0.9 copy.20
  103.9 5.1 %all-to-all-done.6 = bf16[8,128,128]{2,1,0:T(8,128)(2,1)S(1)} async-done(((bf16[8,128,128]{2,1,0:T(8,128)(2,1)}), bf16[8,128,128]{2,1,0:T(8,128)(2,1)S(1)}, u32[]{:S(2)}, u32[]{:S(2)}) %all-to-all-start.6) | async-done | bytes 262176 | tf_op jit(solution)/shard_map/all_to_all | solution.py:122
  (51 shorter events, 15.9 us)
Async XLA Ops:
  0.6 18.6 %copy-start = (bf16[128,1024]{1,0:T(8,128)(2,1)S(1)}, bf16[128,1024]{1,0:T(8,128)(2,1)}, u32[]{:S(2)}) copy-start(bf16[128,1024]{1,0:T(8,128)(2,1)} %param.10) | copy-start | bytes 786436
  0.6 32.6 %copy-start.2 = (bf16[128,1024]{1,0:T(8,128)(2,1)S(1)}, bf16[128,1024]{1,0:T(8,128)(2,1)}, u32[]{:S(2)}) copy-start(bf16[128,1024]{1,0:T(8,128)(2,1)} %param.7) | copy-start | bytes 786436
  2.2 12.1 %all-to-all-start.1 = ((bf16[128,8,128]{2,0,1:T(8,128)(2,1)}), bf16[128,8,128]{2,0,1:T(8,128)(2,1)S(1)}, u32[]{:S(2)}, u32[]{:S(2)}) async-start(bf16[128,8,128]{2,0,1:T(8,128)(2,1)} %broadcast_in_dim.50), calls=%async_computation.1 | async-start | bytes 524288 | tf_op jit(solution)/shard_map/all_to_all | solution.py:60
  15.8 10.3 %all-to-all-start.2 = ((bf16[128,8,128]{2,0,1:T(8,128)(2,1)}), bf16[128,8,128]{2,0,1:T(8,128)(2,1)S(1)}, u32[]{:S(2)}, u32[]{:S(2)}) async-start(bf16[128,8,128]{2,0,1:T(8,128)(2,1)} %broadcast_in_dim.51), calls=%async_computation.2 | async-start | bytes 524288 | tf_op jit(solution)/shard_map/all_to_all | solution.py:61
  26.0 18.7 %all-to-all-start.3 = ((bf16[128,8,128]{2,0,1:T(8,128)(2,1)}), bf16[128,8,128]{2,0,1:T(8,128)(2,1)S(1)}, u32[]{:S(2)}, u32[]{:S(2)}) async-start(bf16[128,8,128]{2,0,1:T(8,128)(2,1)} %copy_bitcast_fusion), calls=%async_computation.3 | async-start | bytes 524288 | tf_op jit(solution)/shard_map/all_to_all | solution.py:59
  29.5 15.2 %collective-permute-start = (bf16[2,1024,128]{2,1,0:T(8,128)(2,1)S(1)}, bf16[2,1024,128]{2,1,0:T(8,128)(2,1)S(1)}, u32[]{:S(2)}, u32[]{:S(2)}) collective-permute-start(bf16[2,1024,128]{2,1,0:T(8,128)(2,1)S(1)} %pad_maximum_fusion), channel_id=1, source_target_pairs={{0,8},{8,16},{16,24},{1,9},{9,17},{17,25},{2,10},{10,18},{18,26},{... | collective-permute-start | bytes 1572872 | tf_op jit(solution)/shard_map/ppermute | solution.py:16
  44.8 10.8 %all-to-all-start = ((bf16[128,8,128]{2,0,1:T(8,128)(2,1)}), bf16[128,8,128]{2,0,1:T(8,128)(2,1)S(1)}, u32[]{:S(2)}, u32[]{:S(2)}) async-start(bf16[128,8,128]{2,0,1:T(8,128)(2,1)} %copy_bitcast_fusion.1), calls=%async_computation | async-start | bytes 524288 | tf_op jit(solution)/shard_map/all_to_all | solution.py:58
  58.8 1.0 copy-start.1
  66.3 1.0 copy-start.1
  71.5 16.0 %collective-permute-start.1 = (bf16[2,1024,128]{2,1,0:T(8,128)(2,1)}, bf16[2,1024,128]{2,1,0:T(8,128)(2,1)}, u32[]{:S(2)}, u32[]{:S(2)}) collective-permute-start(bf16[2,1024,128]{2,1,0:T(8,128)(2,1)} %pad_maximum_fusion.3), channel_id=1, source_target_pairs={{8,0},{16,8},{24,16},{9,1},{17,9},{25,17},{10,2},{18,10},{26,18},{... | collective-permute-start | bytes 1572872 | tf_op jit(solution)/shard_map/ppermute | solution.py:16
  72.8 16.7 %all-to-all-start.4 = ((bf16[8,128,128]{2,1,0:T(8,128)(2,1)}), bf16[8,128,128]{2,1,0:T(8,128)(2,1)S(1)}, u32[]{:S(2)}, u32[]{:S(2)}) async-start(bf16[8,128,128]{2,1,0:T(8,128)(2,1)} %bitcast.16), calls=%async_computation.4 | async-start | bytes 524288 | tf_op jit(solution)/shard_map/all_to_all | solution.py:117
  98.8 10.3 %all-to-all-start.6 = ((bf16[8,128,128]{2,1,0:T(8,128)(2,1)}), bf16[8,128,128]{2,1,0:T(8,128)(2,1)S(1)}, u32[]{:S(2)}, u32[]{:S(2)}) async-start(bf16[8,128,128]{2,1,0:T(8,128)(2,1)} %bitcast.24), calls=%async_computation.6 | async-start | bytes 524288 | tf_op jit(solution)/shard_map/all_to_all | solution.py:122
where the time goes:
time: 111 us; the launch traced here: 110 us
  waiting for transfers between devices  45.4 us (41%)
  starting transfers between devices  27.5 us (25%)
  blocking collectives  9.3 us (8%)
  matrix products  8.77 us (8%)
  other arithmetic  8.72 us (8%)
  local copies, waits for them, and re-layouts  7.79 us (7%)
  loops' own time  1.39 us (1%)
    ppermute x2, waiting for transfers between devices, from_behind(): lax.ppermute(value, axis, [(source, source + steps) for source in range(l...  22.1 us
    all_to_all x1, blocking collectives, local(): lax.all_to_all(as_sent(term_k), 'seq', split_axis=0, concat_axis=1, tiled...  9.3 us
    all_to_all x1, waiting for transfers between devices, local(): lax.all_to_all(spread_v, 'seq', split_axis=1, concat_axis=0, tiled=True)  6.09 us
    all_to_all x1, waiting for transfers between devices, local(): lax.all_to_all(spread_k, 'seq', split_axis=1, concat_axis=0, tiled=True)  6.07 us
    all_to_all x1, waiting for transfers between devices, local(): lax.all_to_all(queries, 'seq', split_axis=1, concat_axis=0, tiled=True)  6.05 us
    all_to_all x1, starting transfers between devices, local(): lax.all_to_all(spread_k, 'seq', split_axis=1, concat_axis=0, tiled=True)  5.2 us
    all_to_all x1, waiting for transfers between devices, local(): lax.all_to_all(as_sent(term_v), 'seq', split_axis=0, concat_axis=1, tiled...  5.15 us
    ppermute x2, starting transfers between devices, from_behind(): lax.ppermute(value, axis, [(source, source + steps) for source in range(l...  4.79 us
  transfers between devices with their start and end apart: 8, of which 6 were waited for; matrix products, arithmetic and copies ran while one was open for 6% of the time, Pallas kernels for 0%

commit v1 on v0

v1 whole, which is shorter than its diff:
```python
import functools
import math

import jax
import jax.numpy as jnp
from jax import lax
from jax.experimental import pallas as pl
from jax.experimental.pallas import tpu as pltpu
from jax.sharding import PartitionSpec as P

HEAD_SIZE = 128
GROUP = 8
DOC_MOST = 768
AXES = ("dp", "seq")
PAIRS_BACK = 3
SLOTS = 7
NEG = -1e30
F32 = jnp.float32
BF16 = jnp.bfloat16


def permute(value, devices, source_of):
    moves = [(source_of(d), d) for d in range(devices) if 0 <= source_of(d) < devices]
    return lax.ppermute(value, AXES, moves)


def permute_back(value, devices, source_of):
    moves = [(d, source_of(d)) for d in range(devices) if 0 <= source_of(d) < devices]
    return lax.ppermute(value, AXES, moves)


def mate_of(d):
    return d ^ 1


def near_of(d):
    return d - 2 if d % 2 == 0 else d - 4


def far_of(d):
    return d - 2 * PAIRS_BACK


def dot_nt(a, b):
    return lax.dot_general(a, b, (((1,), (1,)), ((), ())), preferred_element_type=F32)


def dot_nn(a, b):
    return lax.dot_general(a, b, (((1,), (0,)), ((), ())), preferred_element_type=F32)


def attention_kernel(
    rows,
    lens_ref,
    q_ref,
    g_ref,
    full_ref,
    near_ref,
    cross_ref,
    far_ref,
    dq_ref,
    own_ref,
    mate_ref,
    dnear_ref,
    dcross_ref,
    dfar_ref,
    qs,
    gs,
    kwin,
    vwin,
    kt,
    bias,
    sc,
    gp,
    pt,
    dst,
):
    t = rows
    scale = 1.0 / math.sqrt(HEAD_SIZE)
    scale2 = scale * math.log2(math.e)
    me = lax.axis_index("dp") * lax.axis_size("seq") + lax.axis_index("seq")
    odd = lax.rem(me, 2) == 1
    first = me * t
    for h in range(GROUP):
        qs[h * t : (h + 1) * t, :] = q_ref[:, h * HEAD_SIZE : (h + 1) * HEAD_SIZE]
        gs[h * t : (h + 1) * t, :] = g_ref[:, h * HEAD_SIZE : (h + 1) * HEAD_SIZE]
    pieces = (
        (full_ref, 0, 0, 0),
        (None, 0, 5, 1),
        (near_ref, 0, 2, 4),
        (near_ref, 2, 1, 5),
        (cross_ref, 0, 3, 3),
        (cross_ref, 2, 4, 2),
        (far_ref, 0, 6, 6),
    )
    q_pos = first + lax.broadcasted_iota(jnp.int32, (1, t), 1)

    def next_doc(j, carry):
        end, low = carry
        end = end + lens_ref[j]
        return end, jnp.where(end <= q_pos, end, low)

    _, low = lax.fori_loop(
        0, lens_ref.shape[0], next_doc, (jnp.int32(0), jnp.zeros((1, t), jnp.int32))
    )
    for slot, (ref, at, even_back, odd_back) in enumerate(pieces):
        if ref is None:
            key = jnp.where(odd, full_ref[2], far_ref[2])
            value = jnp.where(odd, full_ref[3], far_ref[3])
        else:
            key, value = ref[at], ref[at + 1]
        span = slice(slot * t, (slot + 1) * t)
        kwin[span, :] = key
        vwin[span, :] = value
        kt[:, span] = key.T
        back = jnp.where(odd, odd_back, even_back)
        k_pos = first - back * t + lax.broadcasted_iota(jnp.int32, (t, t), 0)
        allowed = k_pos >= low
        if slot == 0:
            allowed = allowed & (k_pos <= q_pos)
        bias[span, :] = jnp.where(allowed, 0.0, NEG)

    for pair in range(GROUP // 2):
        cols = slice(pair * 2 * t, (pair + 1) * 2 * t)
        sc[...] = dot_nt(kwin[...], qs[cols, :])
        gp[...] = dot_nt(vwin[...], gs[cols, :])
        top = None
        for slot in range(SLOTS):
            span = slice(slot * t, (slot + 1) * t)
            b = bias[span, :]
            s = sc[span, :] * scale2 + jnp.concatenate([b, b], axis=1)
            sc[span, :] = s
            high = jnp.max(s, axis=0, keepdims=True)
            top = high if top is None else jnp.maximum(top, high)
        total = jnp.zeros((1, 2 * t), F32)
        weighted = jnp.zeros((1, 2 * t), F32)
        for slot in range(SLOTS):
            span = slice(slot * t, (slot + 1) * t)
            e = jnp.exp2(sc[span, :] - top)
            sc[span, :] = e
            total += jnp.sum(e, axis=0, keepdims=True)
            weighted += jnp.sum(e * gp[span, :], axis=0, keepdims=True)
        inverse = 1.0 / total
        delta = weighted * inverse
        for slot in range(SLOTS):
            span = slice(slot * t, (slot + 1) * t)
            p = sc[span, :] * inverse
            ds = p * (gp[span, :] - delta) * scale
            pt[span, cols] = p.astype(BF16)
            dst[span, cols] = ds.astype(BF16)

    dk = dot_nn(dst[...], qs[...])
    dv = dot_nn(pt[...], gs[...])

    def part(grad, slot):
        return grad[slot * t : (slot + 1) * t, :]

    none = jnp.zeros((t, HEAD_SIZE), F32)
    for kind, grad in enumerate((dk, dv)):
        own_ref[kind] = part(grad, 0)
        mate_ref[kind] = jnp.where(odd, part(grad, 1), none)
        dnear_ref[kind] = part(grad, 2)
        dnear_ref[kind + 2] = part(grad, 3)
        dcross_ref[kind] = part(grad, 4).astype(BF16)
        dcross_ref[kind + 2] = part(grad, 5).astype(BF16)
        dfar_ref[kind] = part(grad, 6).astype(BF16)
        dfar_ref[kind + 2] = jnp.where(odd, none, part(grad, 1)).astype(BF16)
    dqt = dot_nn(kt[...], dst[...])
    for h in range(GROUP):
        dq_ref[:, h * HEAD_SIZE : (h + 1) * HEAD_SIZE] = dqt[:, h * t : (h + 1) * t].T.astype(BF16)


def local(queries, keys, values, d_out, doc_lengths):
    rows, q_width = queries.shape
    kv_width = keys.shape[1]
    kv_heads = kv_width // HEAD_SIZE
    devices = lax.axis_size("dp") * lax.axis_size("seq")
    mine = jnp.stack([keys, values])
    mate = permute(mine, devices, mate_of)
    full = jnp.concatenate([mine, mate], axis=0)
    near = permute(full, devices, near_of)
    far = permute(full, devices, far_of)
    cross = permute(near, devices, mate_of)

    wide = GROUP * HEAD_SIZE
    window = SLOTS * rows

    def cols(count):
        return pl.BlockSpec((count, rows, HEAD_SIZE), lambda g: (0, 0, g))

    heads = pl.BlockSpec((rows, wide), lambda g: (0, g))
    shape = jax.ShapeDtypeStruct
    d_queries, own, own_mate, d_near, d_cross, d_far = pl.pallas_call(
        functools.partial(attention_kernel, rows),
        grid=(kv_heads,),
        in_specs=[
            pl.BlockSpec(memory_space=pltpu.SMEM),
            heads,
            heads,
            cols(4),
            cols(4),
            cols(4),
            cols(4),
        ],
        out_specs=[heads, cols(2), cols(2), cols(4), cols(4), cols(4)],
        out_shape=[
            shape((rows, q_width), BF16),
            shape((2, rows, kv_width), F32),
            shape((2, rows, kv_width), F32),
            shape((4, rows, kv_width), F32),
            shape((4, rows, kv_width), BF16),
            shape((4, rows, kv_width), BF16),
        ],
        scratch_shapes=[
            pltpu.VMEM((GROUP * rows, HEAD_SIZE), BF16),
            pltpu.VMEM((GROUP * rows, HEAD_SIZE), BF16),
            pltpu.VMEM((window, HEAD_SIZE), BF16),
            pltpu.VMEM((window, HEAD_SIZE), BF16),
            pltpu.VMEM((HEAD_SIZE, window), BF16),
            pltpu.VMEM((window, rows), F32),
            pltpu.VMEM((window, 2 * rows), F32),
            pltpu.VMEM((window, 2 * rows), F32),
            pltpu.VMEM((window, GROUP * rows), BF16),
            pltpu.VMEM((window, GROUP * rows), BF16),
        ],
    )(doc_lengths, queries, d_out, full, near, cross, far)

    from_cross = permute(d_cross, devices, mate_of)
    from_far = permute_back(d_far, devices, far_of)
    near_sum = (d_near + from_cross.astype(F32)).astype(BF16)
    from_near = permute_back(near_sum, devices, near_of)
    arrived = from_near.astype(F32) + from_far.astype(F32)
    from_mate = permute((own_mate + arrived[2:]).astype(BF16), devices, mate_of)
    total = (own + arrived[:2] + from_mate.astype(F32)).astype(BF16)
    return d_queries, total[0], total[1]


def solution(mesh):
    spec = P(AXES, None)
    return jax.shard_map(
        local,
        mesh=mesh,
        in_specs=(spec, spec, spec, spec, P()),
        out_specs=(spec, spec, spec),
        check_vma=False,
    )
```

time: 111 us -> 37 us (0.33)
  the two profiles are of different devices: /device:TPU:0 before, /device:TPU:23 now
where the time goes in v1:
time: 37 us; the launch traced here: 36.7 us
  starting transfers between devices  17.2 us (46%)
  waiting for transfers between devices  9.08 us (25%)
  Pallas kernels  5.82 us (16%)
  local copies, waits for them, and re-layouts  1.94 us (5%)
  other arithmetic  1.9 us (5%)
  between operations  0.76 us (2%)
    ppermute x6, starting transfers between devices, permute(): return lax.ppermute(value, AXES, moves)  11.9 us
    pallas_call x1, Pallas kernels, local(): pl.pallas_call(functools.partial(attention_kernel, rows), grid=(kv_heads,...  5.82 us
    ppermute x6, waiting for transfers between devices, permute(): return lax.ppermute(value, AXES, moves)  5.51 us
    ppermute x2, starting transfers between devices, permute_back(): return lax.ppermute(value, AXES, moves)  5.26 us
    ppermute x2, waiting for transfers between devices, permute_back(): return lax.ppermute(value, AXES, moves)  3.57 us
    unnamed x16, local copies, waits for them, and re-layouts  1.31 us
    convert_element_type x1, other arithmetic, local(): near_sum = (d_near + from_cross.astype(F32)).astype(BF16)  0.99 us
    another operation x1, other arithmetic, local(): mine = jnp.stack([keys, values])  0.83 us
  transfers between devices with their start and end apart: 8, of which 6 were waited for; matrix products, arithmetic and copies ran while one was open for 3% of the time, Pallas kernels for 0%

profile of v1, /device:TPU:23, one launch (start us, length us, event | category | flops | bytes accessed | tf_op | source)
XLA Modules:
  0.0 36.7 jit_solution(7527809901045443140)
XLA Ops:
  0.6 0.0 copy-start.3
  0.6 0.0 copy-start.4
  0.7 0.8 %pad_maximum_fusion.1 = bf16[2,128,128]{2,1,0:T(8,128)(2,1)S(1)} fusion(bf16[1,128,128]{2,1,0:T(8,128)(2,1)} %bitcast.6, bf16[1,128,128]{2,1,0:T(8,128)(2,1)} %bitcast.8), kind=kLoop, calls=%fused_computation.8 | loop fusion | flops 32768 | bytes 131072 | tf_op jit(solution)/shard_map/stack | solution.py:178
  1.5 0.7 %collective-permute-start = (bf16[2,128,128]{2,1,0:T(8,128)(2,1)S(1)}, bf16[2,128,128]{2,1,0:T(8,128)(2,1)S(1)}, u32[]{:S(2)}, u32[]{:S(2)}) collective-permute-start(bf16[2,128,128]{2,1,0:T(8,128)(2,1)S(1)} %pad_maximum_fusion.1), channel_id=1, source_target_pairs={{1,0},{0,1},{3,2},{2,3},{5,4},{4,5},{7,6},{6,7},{9,8},{8,9},{11,10... | collective-permute-start | bytes 196616 | tf_op jit(solution)/shard_map/ppermute | solution.py:24
  2.2 0.9 %collective-permute-done = bf16[2,128,128]{2,1,0:T(8,128)(2,1)S(1)} collective-permute-done((bf16[2,128,128]{2,1,0:T(8,128)(2,1)S(1)}, bf16[2,128,128]{2,1,0:T(8,128)(2,1)S(1)}, u32[]{:S(2)}, u32[]{:S(2)}) %collective-permute-start) | collective-permute-done | bytes 65568 | tf_op jit(solution)/shard_map/ppermute | solution.py:24
  3.1 3.1 %collective-permute-start.1 = (bf16[4,128,128]{2,1,0:T(8,128)(2,1)S(1)}, bf16[4,128,128]{2,1,0:T(8,128)(2,1)S(1)}, u32[]{:S(2)}, u32[]{:S(2)}) collective-permute-start(bf16[4,128,128]{2,1,0:T(8,128)(2,1)S(1)} %pad_maximum_fusion.full_ref), channel_id=1, source_target_pairs={{0,2},{2,4},{1,5},{4,6},{3,7},{6,8},{5,9},{8,10},{7,11},{10,12},{9... | collective-permute-start | bytes 393224 | tf_op jit(solution)/shard_map/ppermute | solution.py:24
  6.3 1.9 %collective-permute-start.3 = (bf16[4,128,128]{2,1,0:T(8,128)(2,1)S(1)}, bf16[4,128,128]{2,1,0:T(8,128)(2,1)S(1)}, u32[]{:S(2)}, u32[]{:S(2)}) collective-permute-start(bf16[4,128,128]{2,1,0:T(8,128)(2,1)S(1)} %pad_maximum_fusion.full_ref), channel_id=1, source_target_pairs={{0,6},{1,7},{2,8},{3,9},{4,10},{5,11},{6,12},{7,13},{8,14},{9,15},... | collective-permute-start | bytes 393224 | tf_op jit(solution)/shard_map/ppermute | solution.py:24
  8.2 0.9 %collective-permute-done.1.near_ref = bf16[4,128,128]{2,1,0:T(8,128)(2,1)S(1)} collective-permute-done((bf16[4,128,128]{2,1,0:T(8,128)(2,1)S(1)}, bf16[4,128,128]{2,1,0:T(8,128)(2,1)S(1)}, u32[]{:S(2)}, u32[]{:S(2)}) %collective-permute-start.1) | collective-permute-done | bytes 131104 | tf_op jit(solution)/shard_map/ppermute | solution.py:24
  9.2 1.6 %collective-permute-start.2 = (bf16[4,128,128]{2,1,0:T(8,128)(2,1)S(1)}, bf16[4,128,128]{2,1,0:T(8,128)(2,1)S(1)}, u32[]{:S(2)}, u32[]{:S(2)}) collective-permute-start(bf16[4,128,128]{2,1,0:T(8,128)(2,1)S(1)} %collective-permute-done.1.near_ref), channel_id=1, source_target_pairs={{1,0},{0,1},{3,2},{2,3},{5,4},{4,5},{7,6},{6,7},{9,8},{8,9},{11,10... | collective-permute-start | bytes 393224 | tf_op jit(solution)/shard_map/ppermute | solution.py:24
  10.8 2.8 %collective-permute-done.3.far_ref = bf16[4,128,128]{2,1,0:T(8,128)(2,1)S(1)} collective-permute-done((bf16[4,128,128]{2,1,0:T(8,128)(2,1)S(1)}, bf16[4,128,128]{2,1,0:T(8,128)(2,1)S(1)}, u32[]{:S(2)}, u32[]{:S(2)}) %collective-permute-start.3) | collective-permute-done | bytes 131104 | tf_op jit(solution)/shard_map/ppermute | solution.py:24
  13.6 0.0 collective-permute-done.2.cross_ref
  13.6 0.6 %copy-done.6 = bf16[4,128,128]{2,1,0:T(8,128)(2,1)} copy-done((bf16[4,128,128]{2,1,0:T(8,128)(2,1)}, bf16[4,128,128]{2,1,0:T(8,128)(2,1)S(1)}, u32[]{:S(2)}) %copy-start.6) | copy-done | bytes 131096
  14.2 0.6 %copy-done.7 = bf16[4,128,128]{2,1,0:T(8,128)(2,1)} copy-done((bf16[4,128,128]{2,1,0:T(8,128)(2,1)}, bf16[4,128,128]{2,1,0:T(8,128)(2,1)S(1)}, u32[]{:S(2)}) %copy-start.7) | copy-done | bytes 131096
  14.9 5.8 %shard_map.76 = (bf16[128,1024]{1,0:T(8,128)(2,1)}, f32[2,128,128]{2,1,0:T(8,128)}, f32[2,128,128]{2,1,0:T(8,128)}, f32[4,128,128]{2,1,0:T(8,128)}, bf16[4,128,1...) custom-call(s32[11]{0:T(128)} %lens_ref.1, bf16[128,1024]{1,0:T(8,128)(2,1)} %q_ref.1, bf16[128,1024]{1,0:T(8,128)(2,1)} %g_ref.1, ...), custom_call_target="tpu_custom_call" | custom-call | tf_op jit(solution)/shard_map/pallas_call | solution.py:193
  20.7 1.5 %collective-permute-start.4 = (bf16[4,128,128]{2,1,0:T(8,128)(2,1)}, bf16[4,128,128]{2,1,0:T(8,128)(2,1)S(1)}, u32[]{:S(2)}, u32[]{:S(2)}) collective-permute-start(bf16[4,128,128]{2,1,0:T(8,128)(2,1)} %get-tuple-element.12), channel_id=1, source_target_pairs={{1,0},{0,1},{3,2},{2,3},{5,4},{4,5},{7,6},{6,7},{9,8},{8,9},{11,10... | collective-permute-start | bytes 393224 | tf_op jit(solution)/shard_map/ppermute | solution.py:24
  22.1 2.1 %collective-permute-start.6 = (bf16[4,128,128]{2,1,0:T(8,128)(2,1)}, bf16[4,128,128]{2,1,0:T(8,128)(2,1)S(1)}, u32[]{:S(2)}, u32[]{:S(2)}) collective-permute-start(bf16[4,128,128]{2,1,0:T(8,128)(2,1)} %get-tuple-element.13), channel_id=1, source_target_pairs={{6,0},{7,1},{8,2},{9,3},{10,4},{11,5},{12,6},{13,7},{14,8},{15,9},... | collective-permute-start | bytes 393224 | tf_op jit(solution)/shard_map/ppermute | solution.py:29
  24.2 0.0 collective-permute-done.4
  24.2 1.0 %add_convert_fusion = bf16[4,128,128]{2,1,0:T(8,128)(2,1)S(1)} fusion(f32[4,128,128]{2,1,0:T(8,128)} %get-tuple-element.11, bf16[4,128,128]{2,1,0:T(8,128)(2,1)S(1)} %collective-permute-done.4), kind=kLoop, calls=%fused_computation.1 | loop fusion | flops 196608 | bytes 524288 | tf_op jit(solution)/shard_map/convert_element_type | solution.py:230
  25.2 3.2 %collective-permute-start.5 = (bf16[4,128,128]{2,1,0:T(8,128)(2,1)S(1)}, bf16[4,128,128]{2,1,0:T(8,128)(2,1)S(1)}, u32[]{:S(2)}, u32[]{:S(2)}) collective-permute-start(bf16[4,128,128]{2,1,0:T(8,128)(2,1)S(1)} %add_convert_fusion), channel_id=1, source_target_pairs={{2,0},{4,2},{5,1},{6,4},{7,3},{8,6},{9,5},{10,8},{11,7},{12,10},{1... | collective-permute-start | bytes 393224 | tf_op jit(solution)/shard_map/ppermute | solution.py:29
  28.4 1.7 %collective-permute-done.6 = bf16[4,128,128]{2,1,0:T(8,128)(2,1)S(1)} collective-permute-done((bf16[4,128,128]{2,1,0:T(8,128)(2,1)}, bf16[4,128,128]{2,1,0:T(8,128)(2,1)S(1)}, u32[]{:S(2)}, u32[]{:S(2)}) %collective-permute-start.6) | collective-permute-done | bytes 131104 | tf_op jit(solution)/shard_map/ppermute | solution.py:29
  30.2 1.8 %collective-permute-done.5 = bf16[4,128,128]{2,1,0:T(8,128)(2,1)S(1)} collective-permute-done((bf16[4,128,128]{2,1,0:T(8,128)(2,1)S(1)}, bf16[4,128,128]{2,1,0:T(8,128)(2,1)S(1)}, u32[]{:S(2)}, u32[]{:S(2)}) %collective-permute-start.5) | collective-permute-done | bytes 131104 | tf_op jit(solution)/shard_map/ppermute | solution.py:29
  32.1 3.0 %collective-permute-start.7 = (bf16[2,128,128]{2,1,0:T(8,128)(2,1)S(1)}, bf16[2,128,128]{2,1,0:T(8,128)(2,1)S(1)}, u32[]{:S(2)}, u32[]{:S(2)}) collective-permute-start(bf16[2,128,128]{2,1,0:T(8,128)(2,1)S(1)} %fusion), channel_id=1, source_target_pairs={{1,0},{0,1},{3,2},{2,3},{5,4},{4,5},{7,6},{6,7},{9,8},{8,9},{11,10... | collective-permute-start | bytes 196616 | tf_op jit(solution)/shard_map/ppermute | solution.py:24
  35.1 0.9 %collective-permute-done.7 = bf16[2,128,128]{2,1,0:T(8,128)(2,1)S(1)} collective-permute-done((bf16[2,128,128]{2,1,0:T(8,128)(2,1)S(1)}, bf16[2,128,128]{2,1,0:T(8,128)(2,1)S(1)}, u32[]{:S(2)}, u32[]{:S(2)}) %collective-permute-start.7) | collective-permute-done | bytes 65568 | tf_op jit(solution)/shard_map/ppermute | solution.py:24
  36.0 0.6 %slice_bitcast_fusion = (bf16[128,128]{1,0:T(8,128)(2,1)}, bf16[128,128]{1,0:T(8,128)(2,1)}) fusion(bf16[2,128,128]{2,1,0:T(8,128)(2,1)S(1)} %fusion.2), kind=kLoop, calls=%fused_computation.9 | loop fusion | bytes 131072 | tf_op jit(solution)/shard_map/squeeze | solution.py:235
  (16 shorter events, 0.1 us)
Async XLA Ops:
  0.6 2.5 %copy-start.3 = (bf16[128,128]{1,0:T(8,128)(2,1)S(1)}, bf16[128,128]{1,0:T(8,128)(2,1)}, u32[]{:S(2)}) copy-start(bf16[128,128]{1,0:T(8,128)(2,1)} %param.7) | copy-start | bytes 98308
  0.6 2.5 %copy-start.4 = (bf16[128,128]{1,0:T(8,128)(2,1)S(1)}, bf16[128,128]{1,0:T(8,128)(2,1)}, u32[]{:S(2)}) copy-start(bf16[128,128]{1,0:T(8,128)(2,1)} %param.6) | copy-start | bytes 98308
  1.5 1.6 %collective-permute-start = (bf16[2,128,128]{2,1,0:T(8,128)(2,1)S(1)}, bf16[2,128,128]{2,1,0:T(8,128)(2,1)S(1)}, u32[]{:S(2)}, u32[]{:S(2)}) collective-permute-start(bf16[2,128,128]{2,1,0:T(8,128)(2,1)S(1)} %pad_maximum_fusion.1), channel_id=1, source_target_pairs={{1,0},{0,1},{3,2},{2,3},{5,4},{4,5},{7,6},{6,7},{9,8},{8,9},{11,10... | collective-permute-start | bytes 196616 | tf_op jit(solution)/shard_map/ppermute | solution.py:24
  3.1 10.4 %copy-start = (bf16[4,128,128]{2,1,0:T(8,128)(2,1)}, bf16[4,128,128]{2,1,0:T(8,128)(2,1)S(1)}, u32[]{:S(2)}) copy-start(bf16[4,128,128]{2,1,0:T(8,128)(2,1)S(1)} %pad_maximum_fusion.full_ref) | copy-start | bytes 393220
  3.1 6.0 %collective-permute-start.1 = (bf16[4,128,128]{2,1,0:T(8,128)(2,1)S(1)}, bf16[4,128,128]{2,1,0:T(8,128)(2,1)S(1)}, u32[]{:S(2)}, u32[]{:S(2)}) collective-permute-start(bf16[4,128,128]{2,1,0:T(8,128)(2,1)S(1)} %pad_maximum_fusion.full_ref), channel_id=1, source_target_pairs={{0,2},{2,4},{1,5},{4,6},{3,7},{6,8},{5,9},{8,10},{7,11},{10,12},{9... | collective-permute-start | bytes 393224 | tf_op jit(solution)/shard_map/ppermute | solution.py:24
  6.3 7.2 %collective-permute-start.3 = (bf16[4,128,128]{2,1,0:T(8,128)(2,1)S(1)}, bf16[4,128,128]{2,1,0:T(8,128)(2,1)S(1)}, u32[]{:S(2)}, u32[]{:S(2)}) collective-permute-start(bf16[4,128,128]{2,1,0:T(8,128)(2,1)S(1)} %pad_maximum_fusion.full_ref), channel_id=1, source_target_pairs={{0,6},{1,7},{2,8},{3,9},{4,10},{5,11},{6,12},{7,13},{8,14},{9,15},... | collective-permute-start | bytes 393224 | tf_op jit(solution)/shard_map/ppermute | solution.py:24
  9.2 4.4 %copy-start.5 = (bf16[4,128,128]{2,1,0:T(8,128)(2,1)}, bf16[4,128,128]{2,1,0:T(8,128)(2,1)S(1)}, u32[]{:S(2)}) copy-start(bf16[4,128,128]{2,1,0:T(8,128)(2,1)S(1)} %collective-permute-done.1.near_ref) | copy-start | bytes 393220
  9.2 4.4 %collective-permute-start.2 = (bf16[4,128,128]{2,1,0:T(8,128)(2,1)S(1)}, bf16[4,128,128]{2,1,0:T(8,128)(2,1)S(1)}, u32[]{:S(2)}, u32[]{:S(2)}) collective-permute-start(bf16[4,128,128]{2,1,0:T(8,128)(2,1)S(1)} %collective-permute-done.1.near_ref), channel_id=1, source_target_pairs={{1,0},{0,1},{3,2},{2,3},{5,4},{4,5},{7,6},{6,7},{9,8},{8,9},{11,10... | collective-permute-start | bytes 393224 | tf_op jit(solution)/shard_map/ppermute | solution.py:24
  13.6 0.7 %copy-start.6 = (bf16[4,128,128]{2,1,0:T(8,128)(2,1)}, bf16[4,128,128]{2,1,0:T(8,128)(2,1)S(1)}, u32[]{:S(2)}) copy-start(bf16[4,128,128]{2,1,0:T(8,128)(2,1)S(1)} %collective-permute-done.3.far_ref) | copy-start | bytes 393220
  14.2 0.7 %copy-start.7 = (bf16[4,128,128]{2,1,0:T(8,128)(2,1)}, bf16[4,128,128]{2,1,0:T(8,128)(2,1)S(1)}, u32[]{:S(2)}) copy-start(bf16[4,128,128]{2,1,0:T(8,128)(2,1)S(1)} %collective-permute-done.2.cross_ref) | copy-start | bytes 393220
  20.7 3.6 %collective-permute-start.4 = (bf16[4,128,128]{2,1,0:T(8,128)(2,1)}, bf16[4,128,128]{2,1,0:T(8,128)(2,1)S(1)}, u32[]{:S(2)}, u32[]{:S(2)}) collective-permute-start(bf16[4,128,128]{2,1,0:T(8,128)(2,1)} %get-tuple-element.12), channel_id=1, source_target_pairs={{1,0},{0,1},{3,2},{2,3},{5,4},{4,5},{7,6},{6,7},{9,8},{8,9},{11,10... | collective-permute-start | bytes 393224 | tf_op jit(solution)/shard_map/ppermute | solution.py:24
  22.1 8.0 %collective-permute-start.6 = (bf16[4,128,128]{2,1,0:T(8,128)(2,1)}, bf16[4,128,128]{2,1,0:T(8,128)(2,1)S(1)}, u32[]{:S(2)}, u32[]{:S(2)}) collective-permute-start(bf16[4,128,128]{2,1,0:T(8,128)(2,1)} %get-tuple-element.13), channel_id=1, source_target_pairs={{6,0},{7,1},{8,2},{9,3},{10,4},{11,5},{12,6},{13,7},{14,8},{15,9},... | collective-permute-start | bytes 393224 | tf_op jit(solution)/shard_map/ppermute | solution.py:29
  25.2 6.8 %copy-start.2 = (f32[2,128,128]{2,1,0:T(8,128)S(1)}, f32[2,128,128]{2,1,0:T(8,128)}, u32[]{:S(2)}) copy-start(f32[2,128,128]{2,1,0:T(8,128)} %get-tuple-element.14) | copy-start | bytes 393220
  25.2 6.7 %collective-permute-start.5 = (bf16[4,128,128]{2,1,0:T(8,128)(2,1)S(1)}, bf16[4,128,128]{2,1,0:T(8,128)(2,1)S(1)}, u32[]{:S(2)}, u32[]{:S(2)}) collective-permute-start(bf16[4,128,128]{2,1,0:T(8,128)(2,1)S(1)} %add_convert_fusion), channel_id=1, source_target_pairs={{2,0},{4,2},{5,1},{6,4},{7,3},{8,6},{9,5},{10,8},{11,7},{12,10},{1... | collective-permute-start | bytes 393224 | tf_op jit(solution)/shard_map/ppermute | solution.py:29
  32.0 4.0 %copy-start.1 = (f32[2,128,128]{2,1,0:T(8,128)S(1)}, f32[2,128,128]{2,1,0:T(8,128)}, u32[]{:S(2)}) copy-start(f32[2,128,128]{2,1,0:T(8,128)} %get-tuple-element.10) | copy-start | bytes 393220
  32.1 3.9 %collective-permute-start.7 = (bf16[2,128,128]{2,1,0:T(8,128)(2,1)S(1)}, bf16[2,128,128]{2,1,0:T(8,128)(2,1)S(1)}, u32[]{:S(2)}, u32[]{:S(2)}) collective-permute-start(bf16[2,128,128]{2,1,0:T(8,128)(2,1)S(1)} %fusion), channel_id=1, source_target_pairs={{1,0},{0,1},{3,2},{2,3},{5,4},{4,5},{7,6},{6,7},{9,8},{8,9},{11,10... | collective-permute-start | bytes 196616 | tf_op jit(solution)/shard_map/ppermute | solution.py:24

commit v2 on v1

v2 whole, which is shorter than its diff:
```python
import functools
import math

import jax
import jax.numpy as jnp
from jax import lax
from jax.experimental import pallas as pl
from jax.experimental.pallas import tpu as pltpu
from jax.sharding import PartitionSpec as P

HEAD_SIZE = 128
GROUP = 8
DOC_MOST = 768
AXES = ("dp", "seq")
SLOTS = 7
NEG = -1e30
VMEM_BYTES = 16 << 20
F32 = jnp.float32
BF16 = jnp.bfloat16


def weave(devices, turn):
    pairs = devices // 2
    moves, sources, targets = [], [], []
    taken = set()
    for c in range(pairs):
        back = -4 if c % 4 < 2 else -8
        if c % 2 == turn:
            steps = ((0, 1, 0), (1, 2, 0))
        else:
            steps = ((0, 3, 1), (1, back, 1))
        for core, step, target_core in steps:
            target = c + step
            if 0 <= target < pairs:
                moves.append((2 * c + core, 2 * target + target_core))
                taken.add(2 * target + target_core)
            else:
                sources.append(2 * c + core)
    targets = [d for d in range(devices) if d not in taken]
    rest = list(zip(sources, targets))
    for i, (source, target) in enumerate(rest):
        if source == target:
            j = i - 1 if i else 1
            rest[i], rest[j] = (source, rest[j][1]), (rest[j][0], target)
    return moves + rest


def swap(value, devices):
    return lax.ppermute(value, AXES, [(d, d ^ 1) for d in range(devices)])


def dot_nt(a, b):
    return lax.dot_general(a, b, (((1,), (1,)), ((), ())), preferred_element_type=F32)


def dot_nn(a, b):
    return lax.dot_general(a, b, (((1,), (0,)), ((), ())), preferred_element_type=F32)


def attention_kernel(
    rows,
    lens_ref,
    q_ref,
    g_ref,
    full_ref,
    a_ref,
    ax_ref,
    b_ref,
    bx_ref,
    dq_ref,
    own_ref,
    mate_ref,
    keep2_ref,
    keep1_ref,
    give2_ref,
    give1_ref,
    qs,
    gs,
    kwin,
    vwin,
    kt,
    bias,
    sc,
    gp,
    pt,
    dst,
):
    t = rows
    scale = 1.0 / math.sqrt(HEAD_SIZE)
    scale2 = scale * math.log2(math.e)
    me = lax.axis_index("dp") * lax.axis_size("seq") + lax.axis_index("seq")
    odd = lax.rem(me, 2) == 1
    odd_pair = lax.rem(me // 2, 2) == 1
    first = me * t
    q_pos = first + lax.broadcasted_iota(jnp.int32, (1, t), 1)

    def next_doc(j, carry):
        end, low = carry
        end = end + lens_ref[j]
        return end, jnp.where(end <= q_pos, end, low)

    _, low = lax.fori_loop(
        0, lens_ref.shape[0], next_doc, (jnp.int32(0), jnp.zeros((1, t), jnp.int32))
    )
    for slot, (even_back, odd_back) in enumerate(
        ((0, 0), (6, 1), (2, 3), (1, 2), (4, 5), (3, 4), (5, 6))
    ):
        back = jnp.where(odd, odd_back, even_back)
        k_pos = first - back * t + lax.broadcasted_iota(jnp.int32, (t, t), 0)
        allowed = k_pos >= low
        if slot == 0:
            allowed = allowed & (k_pos <= q_pos)
        bias[slot * t : (slot + 1) * t, :] = jnp.where(allowed, 0.0, NEG)

    for head in range(full_ref.shape[2] // HEAD_SIZE):
        lanes = slice(head * HEAD_SIZE, (head + 1) * HEAD_SIZE)

        def q_lanes(h, head=head):
            at = (head * GROUP + h) * HEAD_SIZE
            return slice(at, at + HEAD_SIZE)

        for h in range(GROUP):
            qs[h * t : (h + 1) * t, :] = q_ref[:, q_lanes(h)]
            gs[h * t : (h + 1) * t, :] = g_ref[:, q_lanes(h)]

        def fill(core, one, two, three, lanes=lanes):
            chosen = (
                (full_ref, 2 * core),
                (full_ref, 0) if core else (three, 0),
                (one, 0),
                (one, 2),
                (two, 0),
                (two, 2),
                (three, 2),
            )
            for slot, (ref, at) in enumerate(chosen):
                span = slice(slot * t, (slot + 1) * t)
                kwin[span, :] = ref[at, :, lanes]
                vwin[span, :] = ref[at + 1, :, lanes]

        for pair_parity in (0, 1):
            for core in (0, 1):
                two_at, one_at = ((a_ref, ax_ref), (b_ref, bx_ref))
                if pair_parity:
                    two_at, one_at = one_at, two_at
                one, two, three = one_at[core], two_at[core], two_at[1 - core]

                @pl.when((odd_pair == bool(pair_parity)) & (odd == bool(core)))
                def _(core=core, one=one, two=two, three=three):
                    fill(core, one, two, three)

        for slot in range(SLOTS):
            span = slice(slot * t, (slot + 1) * t)
            kt[:, span] = kwin[span, :].T

        for pair in range(GROUP // 2):
            cols = slice(pair * 2 * t, (pair + 1) * 2 * t)
            sc[...] = dot_nt(kwin[...], qs[cols, :])
            gp[...] = dot_nt(vwin[...], gs[cols, :])
            top = None
            for slot in range(SLOTS):
                span = slice(slot * t, (slot + 1) * t)
                b = bias[span, :]
                s = sc[span, :] * scale2 + jnp.concatenate([b, b], axis=1)
                sc[span, :] = s
                high = jnp.max(s, axis=0, keepdims=True)
                top = high if top is None else jnp.maximum(top, high)
            total = jnp.zeros((1, 2 * t), F32)
            weighted = jnp.zeros((1, 2 * t), F32)
            for slot in range(SLOTS):
                span = slice(slot * t, (slot + 1) * t)
                e = jnp.exp2(sc[span, :] - top)
                sc[span, :] = e
                total += jnp.sum(e, axis=0, keepdims=True)
                weighted += jnp.sum(e * gp[span, :], axis=0, keepdims=True)
            inverse = 1.0 / total
            delta = weighted * inverse
            for slot in range(SLOTS):
                span = slice(slot * t, (slot + 1) * t)
                p = sc[span, :] * inverse
                ds = p * (gp[span, :] - delta) * scale
                pt[span, cols] = p.astype(BF16)
                dst[span, cols] = ds.astype(BF16)

        dk = dot_nn(dst[...], qs[...])
        dv = dot_nn(pt[...], gs[...])

        def part(grad, slot):
            return grad[slot * t : (slot + 1) * t, :]

        none = jnp.zeros((t, HEAD_SIZE), F32)
        for kind, grad in enumerate((dk, dv)):
            own_ref[kind, :, lanes] = part(grad, 0)
            mate_ref[kind, :, lanes] = jnp.where(odd, part(grad, 1), none)
            third_even = jnp.where(odd, none, part(grad, 1))
            two, three = (part(grad, 4), part(grad, 5)), (third_even, part(grad, 6))
            one = (part(grad, 2), part(grad, 3))
            for side in (0, 1):
                at = kind + 2 * side
                give2_ref[at, :, lanes] = jnp.where(odd, two[side], three[side]).astype(BF16)
                give1_ref[at, :, lanes] = one[side].astype(BF16)
                keep2_ref[at, :, lanes] = jnp.where(odd, three[side], two[side]).astype(BF16)
                keep1_ref[at, :, lanes] = jnp.where(odd, none, one[side]).astype(BF16)
        dqt = dot_nn(kt[...], dst[...])
        for h in range(GROUP):
            dq_ref[:, q_lanes(h)] = dqt[:, h * t : (h + 1) * t].T.astype(BF16)


def local(queries, keys, values, d_out, doc_lengths):
    rows, q_width = queries.shape
    kv_width = keys.shape[1]
    devices = lax.axis_size("dp") * lax.axis_size("seq")
    me = lax.axis_index("dp") * lax.axis_size("seq") + lax.axis_index("seq")
    odd = lax.rem(me, 2) == 1
    odd_pair = lax.rem(me // 2, 2) == 1
    a_moves, b_moves = weave(devices, 0), weave(devices, 1)

    mate_k, mate_v = swap(keys, devices), swap(values, devices)
    mine, mate = jnp.stack([keys, values]), jnp.stack([mate_k, mate_v])
    full = jnp.concatenate([jnp.where(odd, mate, mine), jnp.where(odd, mine, mate)], axis=0)
    a = lax.ppermute(full, AXES, a_moves)
    b = lax.ppermute(full, AXES, b_moves)
    ax, bx = swap(a, devices), swap(b, devices)

    window = SLOTS * rows
    shape = jax.ShapeDtypeStruct
    in_vmem = pl.BlockSpec(memory_space=pltpu.VMEM)
    piece = shape((4, rows, kv_width), BF16)
    d_queries, own, own_mate, keep2, keep1, give2, give1 = pl.pallas_call(
        functools.partial(attention_kernel, rows),
        in_specs=[pl.BlockSpec(memory_space=pltpu.SMEM)] + [in_vmem] * 7,
        out_specs=[in_vmem] * 7,
        out_shape=[
            shape((rows, q_width), BF16),
            shape((2, rows, kv_width), F32),
            shape((2, rows, kv_width), F32),
            piece,
            piece,
            piece,
            piece,
        ],
        scratch_shapes=[
            pltpu.VMEM((GROUP * rows, HEAD_SIZE), BF16),
            pltpu.VMEM((GROUP * rows, HEAD_SIZE), BF16),
            pltpu.VMEM((window, HEAD_SIZE), BF16),
            pltpu.VMEM((window, HEAD_SIZE), BF16),
            pltpu.VMEM((HEAD_SIZE, window), BF16),
            pltpu.VMEM((window, rows), F32),
            pltpu.VMEM((window, 2 * rows), F32),
            pltpu.VMEM((window, 2 * rows), F32),
            pltpu.VMEM((window, GROUP * rows), BF16),
            pltpu.VMEM((window, GROUP * rows), BF16),
        ],
        compiler_params=pltpu.CompilerParams(vmem_limit_bytes=VMEM_BYTES),
    )(doc_lengths, queries, d_out, full, a, ax, b, bx)

    got2, got1 = swap(give2, devices), swap(give1, devices)
    back2 = (keep2.astype(F32) + got2.astype(F32)).astype(BF16)
    back1 = jnp.where(odd, jnp.zeros_like(keep1), (keep1.astype(F32) + got1.astype(F32)).astype(BF16))
    home_a = lax.ppermute(jnp.where(odd_pair, back1, back2), AXES, [(d, s) for s, d in a_moves])
    home_b = lax.ppermute(jnp.where(odd_pair, back2, back1), AXES, [(d, s) for s, d in b_moves])
    arrived = home_a.astype(F32) + home_b.astype(F32)
    mine_in = jnp.where(odd, arrived[2:], arrived[:2])
    mate_in = jnp.where(odd, arrived[:2], arrived[2:])
    from_mate = swap((own_mate + mate_in).astype(BF16), devices)
    total = (own + mine_in + from_mate.astype(F32)).astype(BF16)
    return d_queries, total[0], total[1]


def solution(mesh):
    spec = P(AXES, None)
    return jax.shard_map(
        local,
        mesh=mesh,
        in_specs=(spec, spec, spec, spec, P()),
        out_specs=(spec, spec, spec),
        check_vma=False,
    )
```

time: 37 us -> 31.4 us (0.85)
  the two profiles are of different devices: /device:TPU:23 before, /device:TPU:0 now
where the time goes in v2:
time: 31.4 us; the launch traced here: 31.3 us
  waiting for transfers between devices  13.4 us (43%)
  starting transfers between devices  10.3 us (33%)
  Pallas kernels  5.17 us (16%)
  other arithmetic  1.03 us (3%)
  between operations  0.69 us (2%)
  local copies, waits for them, and re-layouts  0.65 us (2%)
    pallas_call x1, Pallas kernels, local(): pl.pallas_call(functools.partial(attention_kernel, rows), in_specs=[pl.Bl...  5.17 us
    ppermute x7, waiting for transfers between devices, swap(): return lax.ppermute(value, AXES, [(d, d ^ 1) for d in range(devices)])  4.61 us
    ppermute x1, starting transfers between devices, local(): b = lax.ppermute(full, AXES, b_moves)  3.61 us
    ppermute x7, starting transfers between devices, swap(): return lax.ppermute(value, AXES, [(d, d ^ 1) for d in range(devices)])  3.23 us
    ppermute x1, waiting for transfers between devices, local(): lax.ppermute(jnp.where(odd_pair, back1, back2), AXES, [(d, s) for s, d in...  3.2 us
    ppermute x1, waiting for transfers between devices, local(): a = lax.ppermute(full, AXES, a_moves)  2.4 us
    ppermute x1, waiting for transfers between devices, local(): b = lax.ppermute(full, AXES, b_moves)  1.94 us
    ppermute x1, starting transfers between devices, local(): lax.ppermute(jnp.where(odd_pair, back1, back2), AXES, [(d, s) for s, d in...  1.52 us
  transfers between devices with their start and end apart: 11, of which 10 were waited for; matrix products, arithmetic and copies ran while one was open for 0% of the time, Pallas kernels for 0%

profile of v2, /device:TPU:0, one launch (start us, length us, event | category | flops | bytes accessed | tf_op | source)
XLA Modules:
  0.0 31.3 jit_solution(16000230154127788952)
XLA Ops:
  0.6 0.6 %collective-permute-start = (bf16[128,128]{1,0:T(8,128)(2,1)}, bf16[128,128]{1,0:T(8,128)(2,1)S(1)}, u32[]{:S(2)}, u32[]{:S(2)}) collective-permute-start(bf16[128,128]{1,0:T(8,128)(2,1)} %param.6), channel_id=1, source_target_pairs={{0,1},{1,0},{2,3},{3,2},{4,5},{5,4},{6,7},{7,6},{8,9},{9,8},{10,11... | collective-permute-start | bytes 98312 | tf_op jit(solution)/shard_map/ppermute | solution.py:49
  1.2 0.1 collective-permute-start.1
  1.3 1.0 %collective-permute-done = bf16[128,128]{1,0:T(8,128)(2,1)S(1)} collective-permute-done((bf16[128,128]{1,0:T(8,128)(2,1)}, bf16[128,128]{1,0:T(8,128)(2,1)S(1)}, u32[]{:S(2)}, u32[]{:S(2)}) %collective-permute-start) | collective-permute-done | bytes 32800 | tf_op jit(solution)/shard_map/ppermute | solution.py:49
  2.3 0.3 %collective-permute-done.1 = bf16[128,128]{1,0:T(8,128)(2,1)S(1)} collective-permute-done((bf16[128,128]{1,0:T(8,128)(2,1)}, bf16[128,128]{1,0:T(8,128)(2,1)S(1)}, u32[]{:S(2)}, u32[]{:S(2)}) %collective-permute-start.1) | collective-permute-done | bytes 32800 | tf_op jit(solution)/shard_map/ppermute | solution.py:49
  2.6 0.8 %broadcast_select_fusion.3 = (bf16[2,128,128]{2,1,0:T(8,128)(2,1)S(1)}, bf16[2,128,128]{2,1,0:T(8,128)(2,1)S(1)}) fusion(pred[]{:T(512)S(6)} %eq.6, bf16[1,128,128]{2,1,0:T(8,128)(2,1)S(1)} %bitcast.8, bf16[1,128,128]{2,1,0:T(8,128)(2,1)} %bitcast.9, bf16[1,128,128]{2,1,0:T(8,128)(2,1)S(1)} %bitcast.11, bf16[1,128,128]{2,1,0:T(8,128)(2,1)S(1)} %bitcast.10), kind=kLoop, calls=%fused_computation.12 | loop fusion | flops 131072 | bytes 262145 | tf_op jit(solution)/shard_map/jit(_where)/select_n | solution.py:220
  3.5 0.0 copy-start.2
  3.5 3.6 %collective-permute-start.4 = (bf16[4,128,128]{2,1,0:T(8,128)(2,1)S(1)}, bf16[4,128,128]{2,1,0:T(8,128)(2,1)S(1)}, u32[]{:S(2)}, u32[]{:S(2)}) collective-permute-start(bf16[4,128,128]{2,1,0:T(8,128)(2,1)S(1)} %pad_maximum_fusion.full_ref), channel_id=1, source_target_pairs={{0,7},{2,4},{3,6},{4,11},{6,8},{7,10},{8,15},{9,1},{10,12},{11,14}... | collective-permute-start | bytes 393224 | tf_op jit(solution)/shard_map/ppermute | solution.py:222
  7.1 0.6 %collective-permute-start.2 = (bf16[4,128,128]{2,1,0:T(8,128)(2,1)S(1)}, bf16[4,128,128]{2,1,0:T(8,128)(2,1)S(1)}, u32[]{:S(2)}, u32[]{:S(2)}) collective-permute-start(bf16[4,128,128]{2,1,0:T(8,128)(2,1)S(1)} %pad_maximum_fusion.full_ref), channel_id=1, source_target_pairs={{0,2},{1,4},{2,9},{4,6},{5,8},{6,13},{8,10},{9,12},{10,17},{11,3},... | collective-permute-start | bytes 393224 | tf_op jit(solution)/shard_map/ppermute | solution.py:221
  7.7 1.9 %collective-permute-done.4.b_ref = bf16[4,128,128]{2,1,0:T(8,128)(2,1)S(1)} collective-permute-done((bf16[4,128,128]{2,1,0:T(8,128)(2,1)S(1)}, bf16[4,128,128]{2,1,0:T(8,128)(2,1)S(1)}, u32[]{:S(2)}, u32[]{:S(2)}) %collective-permute-start.4) | collective-permute-done | bytes 131104 | tf_op jit(solution)/shard_map/ppermute | solution.py:222
  9.6 2.4 %collective-permute-done.2.a_ref = bf16[4,128,128]{2,1,0:T(8,128)(2,1)S(1)} collective-permute-done((bf16[4,128,128]{2,1,0:T(8,128)(2,1)S(1)}, bf16[4,128,128]{2,1,0:T(8,128)(2,1)S(1)}, u32[]{:S(2)}, u32[]{:S(2)}) %collective-permute-start.2) | collective-permute-done | bytes 131104 | tf_op jit(solution)/shard_map/ppermute | solution.py:221
  12.0 1.3 %collective-permute-done.3.ax_ref = bf16[4,128,128]{2,1,0:T(8,128)(2,1)S(1)} collective-permute-done((bf16[4,128,128]{2,1,0:T(8,128)(2,1)S(1)}, bf16[4,128,128]{2,1,0:T(8,128)(2,1)S(1)}, u32[]{:S(2)}, u32[]{:S(2)}) %collective-permute-start.3) | collective-permute-done | bytes 131104 | tf_op jit(solution)/shard_map/ppermute | solution.py:49
  13.4 5.2 %shard_map.76 = (bf16[128,1024]{1,0:T(8,128)(2,1)}, f32[2,128,128]{2,1,0:T(8,128)S(1)}, f32[2,128,128]{2,1,0:T(8,128)S(1)}, bf16[4,128,128]{2,1,0:T(8,128)(2,1)S...) custom-call(s32[11]{0:T(128)S(1)} %copy-done.2, ...), custom_call_target="tpu_custom_call" | custom-call | tf_op jit(solution)/shard_map/pallas_call | solution.py:229
  18.6 0.1 collective-permute-start.6
  18.7 0.4 %collective-permute-start.7 = (bf16[4,128,128]{2,1,0:T(8,128)(2,1)S(1)}, bf16[4,128,128]{2,1,0:T(8,128)(2,1)S(1)}, u32[]{:S(2)}, u32[]{:S(2)}) collective-permute-start(bf16[4,128,128]{2,1,0:T(8,128)(2,1)S(1)} %get-tuple-element.15), channel_id=1, source_target_pairs={{0,1},{1,0},{2,3},{3,2},{4,5},{5,4},{6,7},{7,6},{8,9},{9,8},{10,11... | collective-permute-start | bytes 393224 | tf_op jit(solution)/shard_map/ppermute | solution.py:49
  19.1 0.8 %collective-permute-done.6 = bf16[4,128,128]{2,1,0:T(8,128)(2,1)S(1)} collective-permute-done((bf16[4,128,128]{2,1,0:T(8,128)(2,1)S(1)}, bf16[4,128,128]{2,1,0:T(8,128)(2,1)S(1)}, u32[]{:S(2)}, u32[]{:S(2)}) %collective-permute-start.6) | collective-permute-done | bytes 131104 | tf_op jit(solution)/shard_map/ppermute | solution.py:49
  19.9 0.2 collective-permute-done.7
  20.1 0.1 broadcast_select_fusion.1
  20.2 1.5 %collective-permute-start.8 = (bf16[4,128,128]{2,1,0:T(8,128)(2,1)S(1)}, bf16[4,128,128]{2,1,0:T(8,128)(2,1)S(1)}, u32[]{:S(2)}, u32[]{:S(2)}) collective-permute-start(bf16[4,128,128]{2,1,0:T(8,128)(2,1)S(1)} %get-tuple-element.17), channel_id=1, source_target_pairs={{2,0},{4,1},{9,2},{6,4},{8,5},{13,6},{10,8},{12,9},{17,10},{3,11},... | collective-permute-start | bytes 393224 | tf_op jit(solution)/shard_map/ppermute | solution.py:260
  21.7 1.4 %collective-permute-start.9 = (bf16[4,128,128]{2,1,0:T(8,128)(2,1)S(1)}, bf16[4,128,128]{2,1,0:T(8,128)(2,1)S(1)}, u32[]{:S(2)}, u32[]{:S(2)}) collective-permute-start(bf16[4,128,128]{2,1,0:T(8,128)(2,1)S(1)} %get-tuple-element.18), channel_id=1, source_target_pairs={{7,0},{4,2},{6,3},{11,4},{8,6},{10,7},{15,8},{1,9},{12,10},{14,11}... | collective-permute-start | bytes 393224 | tf_op jit(solution)/shard_map/ppermute | solution.py:261
  23.1 3.2 %collective-permute-done.8 = bf16[4,128,128]{2,1,0:T(8,128)(2,1)S(1)} collective-permute-done((bf16[4,128,128]{2,1,0:T(8,128)(2,1)S(1)}, bf16[4,128,128]{2,1,0:T(8,128)(2,1)S(1)}, u32[]{:S(2)}, u32[]{:S(2)}) %collective-permute-start.8) | collective-permute-done | bytes 131104 | tf_op jit(solution)/shard_map/ppermute | solution.py:260
  26.3 1.3 %collective-permute-done.9 = bf16[4,128,128]{2,1,0:T(8,128)(2,1)S(1)} collective-permute-done((bf16[4,128,128]{2,1,0:T(8,128)(2,1)S(1)}, bf16[4,128,128]{2,1,0:T(8,128)(2,1)S(1)}, u32[]{:S(2)}, u32[]{:S(2)}) %collective-permute-start.9) | collective-permute-done | bytes 131104 | tf_op jit(solution)/shard_map/ppermute | solution.py:261
  27.6 2.1 %collective-permute-start.10 = (bf16[2,128,128]{2,1,0:T(8,128)(2,1)S(1)}, bf16[2,128,128]{2,1,0:T(8,128)(2,1)S(1)}, u32[]{:S(2)}, u32[]{:S(2)}) collective-permute-start(bf16[2,128,128]{2,1,0:T(8,128)(2,1)S(1)} %add_convert_fusion.3), channel_id=1, source_target_pairs={{0,1},{1,0},{2,3},{3,2},{4,5},{5,4},{6,7},{7,6},{8,9},{9,8},{10,11... | collective-permute-start | bytes 196616 | tf_op jit(solution)/shard_map/ppermute | solution.py:49
  29.7 0.9 %collective-permute-done.10 = bf16[2,128,128]{2,1,0:T(8,128)(2,1)S(1)} collective-permute-done((bf16[2,128,128]{2,1,0:T(8,128)(2,1)S(1)}, bf16[2,128,128]{2,1,0:T(8,128)(2,1)S(1)}, u32[]{:S(2)}, u32[]{:S(2)}) %collective-permute-start.10) | collective-permute-done | bytes 65568 | tf_op jit(solution)/shard_map/ppermute | solution.py:49
  30.6 0.6 %slice_bitcast_fusion = (bf16[128,128]{1,0:T(8,128)(2,1)}, bf16[128,128]{1,0:T(8,128)(2,1)}) fusion(bf16[2,128,128]{2,1,0:T(8,128)(2,1)S(1)} %add_convert_fusion.2), kind=kLoop, calls=%fused_computation.13 | loop fusion | bytes 131072 | tf_op jit(solution)/shard_map/squeeze | solution.py:267
  (14 shorter events, 0.1 us)
Async XLA Ops:
  0.6 2.0 %copy-start.3 = (bf16[128,128]{1,0:T(8,128)(2,1)S(1)}, bf16[128,128]{1,0:T(8,128)(2,1)}, u32[]{:S(2)}) copy-start(bf16[128,128]{1,0:T(8,128)(2,1)} %param.7) | copy-start | bytes 98308
  0.6 1.6 %collective-permute-start = (bf16[128,128]{1,0:T(8,128)(2,1)}, bf16[128,128]{1,0:T(8,128)(2,1)S(1)}, u32[]{:S(2)}, u32[]{:S(2)}) collective-permute-start(bf16[128,128]{1,0:T(8,128)(2,1)} %param.6), channel_id=1, source_target_pairs={{0,1},{1,0},{2,3},{3,2},{4,5},{5,4},{6,7},{7,6},{8,9},{9,8},{10,11... | collective-permute-start | bytes 98312 | tf_op jit(solution)/shard_map/ppermute | solution.py:49
  1.2 1.4 %collective-permute-start.1 = (bf16[128,128]{1,0:T(8,128)(2,1)}, bf16[128,128]{1,0:T(8,128)(2,1)S(1)}, u32[]{:S(2)}, u32[]{:S(2)}) collective-permute-start(bf16[128,128]{1,0:T(8,128)(2,1)} %param.7), channel_id=1, source_target_pairs={{0,1},{1,0},{2,3},{3,2},{4,5},{5,4},{6,7},{7,6},{8,9},{9,8},{10,11... | collective-permute-start | bytes 98312 | tf_op jit(solution)/shard_map/ppermute | solution.py:49
  2.6 10.8 %copy-start = (bf16[128,1024]{1,0:T(8,128)(2,1)S(1)}, bf16[128,1024]{1,0:T(8,128)(2,1)}, u32[]{:S(2)}) copy-start(bf16[128,1024]{1,0:T(8,128)(2,1)} %q_ref.1) | copy-start | bytes 786436
  2.6 10.8 %copy-start.1 = (bf16[128,1024]{1,0:T(8,128)(2,1)S(1)}, bf16[128,1024]{1,0:T(8,128)(2,1)}, u32[]{:S(2)}) copy-start(bf16[128,1024]{1,0:T(8,128)(2,1)} %g_ref.1) | copy-start | bytes 786436
  3.5 9.9 %copy-start.2 = (s32[11]{0:T(128)S(1)}, s32[11]{0:T(128)}, u32[]{:S(2)}) copy-start(s32[11]{0:T(128)} %lens_ref.1) | copy-start | bytes 136
  3.5 6.1 %collective-permute-start.4 = (bf16[4,128,128]{2,1,0:T(8,128)(2,1)S(1)}, bf16[4,128,128]{2,1,0:T(8,128)(2,1)S(1)}, u32[]{:S(2)}, u32[]{:S(2)}) collective-permute-start(bf16[4,128,128]{2,1,0:T(8,128)(2,1)S(1)} %pad_maximum_fusion.full_ref), channel_id=1, source_target_pairs={{0,7},{2,4},{3,6},{4,11},{6,8},{7,10},{8,15},{9,1},{10,12},{11,14}... | collective-permute-start | bytes 393224 | tf_op jit(solution)/shard_map/ppermute | solution.py:222
  7.1 4.9 %collective-permute-start.2 = (bf16[4,128,128]{2,1,0:T(8,128)(2,1)S(1)}, bf16[4,128,128]{2,1,0:T(8,128)(2,1)S(1)}, u32[]{:S(2)}, u32[]{:S(2)}) collective-permute-start(bf16[4,128,128]{2,1,0:T(8,128)(2,1)S(1)} %pad_maximum_fusion.full_ref), channel_id=1, source_target_pairs={{0,2},{1,4},{2,9},{4,6},{5,8},{6,13},{8,10},{9,12},{10,17},{11,3},... | collective-permute-start | bytes 393224 | tf_op jit(solution)/shard_map/ppermute | solution.py:221
  9.6 2.4 %collective-permute-start.5 = (bf16[4,128,128]{2,1,0:T(8,128)(2,1)S(1)}, bf16[4,128,128]{2,1,0:T(8,128)(2,1)S(1)}, u32[]{:S(2)}, u32[]{:S(2)}) collective-permute-start(bf16[4,128,128]{2,1,0:T(8,128)(2,1)S(1)} %collective-permute-done.4.b_ref), channel_id=1, source_target_pairs={{0,1},{1,0},{2,3},{3,2},{4,5},{5,4},{6,7},{7,6},{8,9},{9,8},{10,11... | collective-permute-start | bytes 393224 | tf_op jit(solution)/shard_map/ppermute | solution.py:49
  12.0 1.3 %collective-permute-start.3 = (bf16[4,128,128]{2,1,0:T(8,128)(2,1)S(1)}, bf16[4,128,128]{2,1,0:T(8,128)(2,1)S(1)}, u32[]{:S(2)}, u32[]{:S(2)}) collective-permute-start(bf16[4,128,128]{2,1,0:T(8,128)(2,1)S(1)} %collective-permute-done.2.a_ref), channel_id=1, source_target_pairs={{0,1},{1,0},{2,3},{3,2},{4,5},{5,4},{6,7},{7,6},{8,9},{9,8},{10,11... | collective-permute-start | bytes 393224 | tf_op jit(solution)/shard_map/ppermute | solution.py:49
  18.6 1.3 %collective-permute-start.6 = (bf16[4,128,128]{2,1,0:T(8,128)(2,1)S(1)}, bf16[4,128,128]{2,1,0:T(8,128)(2,1)S(1)}, u32[]{:S(2)}, u32[]{:S(2)}) collective-permute-start(bf16[4,128,128]{2,1,0:T(8,128)(2,1)S(1)} %get-tuple-element.13), channel_id=1, source_target_pairs={{0,1},{1,0},{2,3},{3,2},{4,5},{5,4},{6,7},{7,6},{8,9},{9,8},{10,11... | collective-permute-start | bytes 393224 | tf_op jit(solution)/shard_map/ppermute | solution.py:49
  18.7 1.4 %collective-permute-start.7 = (bf16[4,128,128]{2,1,0:T(8,128)(2,1)S(1)}, bf16[4,128,128]{2,1,0:T(8,128)(2,1)S(1)}, u32[]{:S(2)}, u32[]{:S(2)}) collective-permute-start(bf16[4,128,128]{2,1,0:T(8,128)(2,1)S(1)} %get-tuple-element.15), channel_id=1, source_target_pairs={{0,1},{1,0},{2,3},{3,2},{4,5},{5,4},{6,7},{7,6},{8,9},{9,8},{10,11... | collective-permute-start | bytes 393224 | tf_op jit(solution)/shard_map/ppermute | solution.py:49
  20.2 6.1 %collective-permute-start.8 = (bf16[4,128,128]{2,1,0:T(8,128)(2,1)S(1)}, bf16[4,128,128]{2,1,0:T(8,128)(2,1)S(1)}, u32[]{:S(2)}, u32[]{:S(2)}) collective-permute-start(bf16[4,128,128]{2,1,0:T(8,128)(2,1)S(1)} %get-tuple-element.17), channel_id=1, source_target_pairs={{2,0},{4,1},{9,2},{6,4},{8,5},{13,6},{10,8},{12,9},{17,10},{3,11},... | collective-permute-start | bytes 393224 | tf_op jit(solution)/shard_map/ppermute | solution.py:260
  21.7 5.8 %collective-permute-start.9 = (bf16[4,128,128]{2,1,0:T(8,128)(2,1)S(1)}, bf16[4,128,128]{2,1,0:T(8,128)(2,1)S(1)}, u32[]{:S(2)}, u32[]{:S(2)}) collective-permute-start(bf16[4,128,128]{2,1,0:T(8,128)(2,1)S(1)} %get-tuple-element.18), channel_id=1, source_target_pairs={{7,0},{4,2},{6,3},{11,4},{8,6},{10,7},{15,8},{1,9},{12,10},{14,11}... | collective-permute-start | bytes 393224 | tf_op jit(solution)/shard_map/ppermute | solution.py:261
  27.6 3.0 %collective-permute-start.10 = (bf16[2,128,128]{2,1,0:T(8,128)(2,1)S(1)}, bf16[2,128,128]{2,1,0:T(8,128)(2,1)S(1)}, u32[]{:S(2)}, u32[]{:S(2)}) collective-permute-start(bf16[2,128,128]{2,1,0:T(8,128)(2,1)S(1)} %add_convert_fusion.3), channel_id=1, source_target_pairs={{0,1},{1,0},{2,3},{3,2},{4,5},{5,4},{6,7},{7,6},{8,9},{9,8},{10,11... | collective-permute-start | bytes 196616 | tf_op jit(solution)/shard_map/ppermute | solution.py:49

commit v3 on v2

v3 whole, which is shorter than its diff:
```python
import functools
import math

import jax
import jax.numpy as jnp
from jax import lax
from jax.experimental import pallas as pl
from jax.experimental.pallas import tpu as pltpu
from jax.sharding import PartitionSpec as P

HEAD_SIZE = 128
GROUP = 8
AXES = ("dp", "seq")
SLOTS = 7
NEG = -1e30
FAR = 1 << 30
WINDOW_BACK = ((0, 0), (6, 1), (2, 3), (1, 2), (4, 5), (3, 4), (5, 6))
F32 = jnp.float32
BF16 = jnp.bfloat16


def weave(devices, turn):
    pairs = devices // 2
    moves, sources, targets = [], [], []
    taken = set()
    for c in range(pairs):
        back = -4 if c % 4 < 2 else -8
        if c % 2 == turn:
            steps = ((0, 1, 0), (1, 2, 0))
        else:
            steps = ((0, 3, 1), (1, back, 1))
        for core, step, target_core in steps:
            target = c + step
            if 0 <= target < pairs:
                moves.append((2 * c + core, 2 * target + target_core))
                taken.add(2 * target + target_core)
            else:
                sources.append(2 * c + core)
    targets = [d for d in range(devices) if d not in taken]
    rest = list(zip(sources, targets))
    for i, (source, target) in enumerate(rest):
        if source == target:
            j = i - 1 if i else 1
            rest[i], rest[j] = (source, rest[j][1]), (rest[j][0], target)
    return moves + rest


def swap(value, devices):
    return lax.ppermute(value, AXES, [(d, d ^ 1) for d in range(devices)])


def dot_nt(a, b):
    return lax.dot_general(a, b, (((1,), (1,)), ((), ())), preferred_element_type=F32)


def dot_nn(a, b):
    return lax.dot_general(a, b, (((1,), (0,)), ((), ())), preferred_element_type=F32)


def prepare_kernel(rows, window_back, lens_ref, q_ref, g_ref, qa_ref, gs_ref, late_ref, sems):
    t = rows
    copies = []
    for h in range(q_ref.shape[1] // HEAD_SIZE):
        span, lanes = slice(h * t, (h + 1) * t), slice(h * HEAD_SIZE, (h + 1) * HEAD_SIZE)
        for source, target, sem in (
            (q_ref.at[:, lanes], qa_ref.at[span, :HEAD_SIZE], sems.at[0, h]),
            (g_ref.at[:, lanes], gs_ref.at[span, :], sems.at[1, h]),
        ):
            copies.append(pltpu.make_async_copy(source, target, sem))
    for copy in copies:
        copy.start()
    me = lax.axis_index("dp") * lax.axis_size("seq") + lax.axis_index("seq")
    odd = lax.rem(me, 2) == 1
    first = me * t
    lane = lax.broadcasted_iota(jnp.int32, (1, HEAD_SIZE), 1)

    def next_doc(j, carry):
        end, count, starts, stops = carry
        begin, end = end, end + lens_ref[j]
        live = end > first
        here = (lane == count) & live
        starts, stops = jnp.where(here, begin, starts), jnp.where(here, end, stops)
        return end, count + live.astype(jnp.int32), starts, stops

    far = jnp.full((1, HEAD_SIZE), FAR, jnp.int32)
    zero = jnp.int32(0)
    _, _, starts, stops = lax.fori_loop(0, lens_ref.shape[0], next_doc, (zero, zero, far, far))
    down = lax.broadcasted_iota(jnp.int32, (t, HEAD_SIZE), 0)
    q_pos = first + down
    member = jnp.where((q_pos >= starts) & (q_pos < stops), 1.0, 0.0).astype(BF16)
    for slot, (even_back, odd_back) in enumerate(window_back):
        k_pos = first - jnp.where(odd, odd_back, even_back) * t + down
        late_ref[slot * t : (slot + 1) * t, :] = jnp.where(k_pos < starts, NEG, 0.0).astype(BF16)
    for h in range(q_ref.shape[1] // HEAD_SIZE):
        qa_ref[h * t : (h + 1) * t, HEAD_SIZE:] = member
    for copy in copies:
        copy.wait()


def attention_kernel(
    rows,
    qa_ref,
    gs_ref,
    late_ref,
    full_ref,
    a_ref,
    ax_ref,
    b_ref,
    bx_ref,
    own_ref,
    mate_ref,
    keep2_ref,
    keep1_ref,
    give2_ref,
    give1_ref,
    ka_ref,
    dst_ref,
    vwin,
    sc,
    gp,
    pt,
):
    t = rows
    scale = 1.0 / math.sqrt(HEAD_SIZE)
    scale2 = scale * math.log2(math.e)
    me = lax.axis_index("dp") * lax.axis_size("seq") + lax.axis_index("seq")
    odd = lax.rem(me, 2) == 1
    odd_pair = lax.rem(me // 2, 2) == 1
    causal = lax.broadcasted_iota(jnp.int32, (t, t), 0) <= lax.broadcasted_iota(
        jnp.int32, (t, t), 1
    )
    causal = jnp.concatenate([causal, causal], axis=1)

    def spans():
        return [slice(slot * t, (slot + 1) * t) for slot in range(SLOTS)]

    def fold(x, op):
        return op(x.reshape(t // 8, 8, 2 * t), axis=0)

    for head in range(full_ref.shape[2] // HEAD_SIZE):
        lanes = slice(head * HEAD_SIZE, (head + 1) * HEAD_SIZE)
        base = head * GROUP * t

        def fill(core, one, two, three, head=head, lanes=lanes):
            chosen = (
                (full_ref, 2 * core),
                (full_ref, 0) if core else (three, 0),
                (one, 0),
                (one, 2),
                (two, 0),
                (two, 2),
                (three, 2),
            )
            for span, (ref, at) in zip(spans(), chosen):
                ka_ref[head, span, :HEAD_SIZE] = ref[at, :, lanes]
                vwin[span, :] = ref[at + 1, :, lanes]

        for pair_parity in (0, 1):
            for core in (0, 1):
                two_at, one_at = ((a_ref, ax_ref), (b_ref, bx_ref))
                if pair_parity:
                    two_at, one_at = one_at, two_at
                one, two, three = one_at[core], two_at[core], two_at[1 - core]

                @pl.when((odd_pair == bool(pair_parity)) & (odd == bool(core)))
                def _(core=core, one=one, two=two, three=three):
                    fill(core, one, two, three)

        ka_ref[head, :, HEAD_SIZE:] = late_ref[...]

        for pair in range(GROUP // 2):
            cols = slice(pair * 2 * t, (pair + 1) * 2 * t)
            pair_rows = slice(base + pair * 2 * t, base + (pair + 1) * 2 * t)
            sc[...] = dot_nt(ka_ref[head], qa_ref[pair_rows, :])
            gp[...] = dot_nt(vwin[...], gs_ref[pair_rows, :])
            top = None
            for slot, span in enumerate(spans()):
                s = sc[span, :] * scale2
                if slot == 0:
                    s = jnp.where(causal, s, NEG)
                sc[span, :] = s
                high = fold(s, jnp.max)
                top = high if top is None else jnp.maximum(top, high)
            top = jnp.max(top, axis=0, keepdims=True)
            total = jnp.zeros((8, 2 * t), F32)
            weighted = jnp.zeros((8, 2 * t), F32)
            for span in spans():
                e = jnp.exp2(sc[span, :] - top)
                total += fold(e, jnp.sum)
                weighted += fold(e * gp[span, :], jnp.sum)
            total = jnp.sum(total, axis=0, keepdims=True)
            delta = jnp.sum(weighted, axis=0, keepdims=True) / total
            level = top + jnp.log2(total)
            for span in spans():
                p = jnp.exp2(sc[span, :] - level)
                pt[span, cols] = p.astype(BF16)
                dst_ref[head, span, cols] = (p * (gp[span, :] - delta)).astype(BF16)

        all_rows = slice(base, base + GROUP * t)
        dk = dot_nn(dst_ref[head], qa_ref[all_rows, :HEAD_SIZE]) * scale
        dv = dot_nn(pt[...], gs_ref[all_rows, :])

        def part(grad, slot):
            return grad[slot * t : (slot + 1) * t, :]

        none = jnp.zeros((t, HEAD_SIZE), F32)
        for kind, grad in enumerate((dk, dv)):
            own_ref[kind, :, lanes] = part(grad, 0)
            mate_ref[kind, :, lanes] = jnp.where(odd, part(grad, 1), none)
            third_even = jnp.where(odd, none, part(grad, 1))
            two, three = (part(grad, 4), part(grad, 5)), (third_even, part(grad, 6))
            one = (part(grad, 2), part(grad, 3))
            for side in (0, 1):
                at = kind + 2 * side
                give2_ref[at, :, lanes] = jnp.where(odd, two[side], three[side]).astype(BF16)
                give1_ref[at, :, lanes] = one[side].astype(BF16)
                keep2_ref[at, :, lanes] = jnp.where(odd, three[side], two[side]).astype(BF16)
                keep1_ref[at, :, lanes] = jnp.where(odd, none, one[side]).astype(BF16)


def query_kernel(rows, ka_ref, dst_ref, dq_ref, kt):
    t = rows
    scale = 1.0 / math.sqrt(HEAD_SIZE)
    for head in range(ka_ref.shape[0]):
        for slot in range(SLOTS):
            span = slice(slot * t, (slot + 1) * t)
            kt[:, span] = ka_ref[head, span, :HEAD_SIZE].T
        dqt = dot_nn(kt[...], dst_ref[head]) * scale
        for h in range(GROUP):
            at = (head * GROUP + h) * HEAD_SIZE
            dq_ref[:, at : at + HEAD_SIZE] = dqt[:, h * t : (h + 1) * t].T.astype(BF16)


def local_grads(queries, keys, values, d_out, doc_lengths):
    rows, q_width = queries.shape
    kv_width = keys.shape[1]
    devices = lax.axis_size("dp") * lax.axis_size("seq")
    me = lax.axis_index("dp") * lax.axis_size("seq") + lax.axis_index("seq")
    odd = lax.rem(me, 2) == 1
    odd_pair = lax.rem(me // 2, 2) == 1
    a_moves, b_moves = weave(devices, 0), weave(devices, 1)

    mine = lax.optimization_barrier(jnp.stack([keys, values]))
    mate = swap(mine, devices)
    full = jnp.concatenate([jnp.where(odd, mate, mine), jnp.where(odd, mine, mate)], axis=0)
    a = lax.ppermute(full, AXES, a_moves)
    b = lax.ppermute(full, AXES, b_moves)
    ax, bx = swap(a, devices), swap(b, devices)

    window = SLOTS * rows
    kv_heads = kv_width // HEAD_SIZE
    tall = q_width // HEAD_SIZE * rows
    shape = jax.ShapeDtypeStruct
    in_vmem = pl.BlockSpec(memory_space=pltpu.VMEM)
    piece = shape((4, rows, kv_width), BF16)
    grant = pltpu.CompilerParams(vmem_limit_bytes=(12 + 5 * kv_heads) << 20)
    qa, gs, late = pl.pallas_call(
        functools.partial(prepare_kernel, rows, WINDOW_BACK),
        in_specs=[pl.BlockSpec(memory_space=pltpu.SMEM)] + [pl.BlockSpec(memory_space=pl.ANY)] * 2,
        out_specs=[in_vmem] * 3,
        out_shape=[
            shape((tall, 2 * HEAD_SIZE), BF16),
            shape((tall, HEAD_SIZE), BF16),
            shape((window, HEAD_SIZE), BF16),
        ],
        scratch_shapes=[pltpu.SemaphoreType.DMA((2, q_width // HEAD_SIZE))],
        compiler_params=grant,
        cost_estimate=pl.CostEstimate(flops=0, bytes_accessed=4 << 20, transcendentals=0),
    )(doc_lengths, queries, d_out)
    own, own_mate, keep2, keep1, give2, give1, ka, dst = pl.pallas_call(
        functools.partial(attention_kernel, rows),
        in_specs=[in_vmem] * 8,
        out_specs=[in_vmem] * 8,
        out_shape=[
            shape((2, rows, kv_width), F32),
            shape((2, rows, kv_width), F32),
            piece,
            piece,
            piece,
            piece,
            shape((kv_heads, window, 2 * HEAD_SIZE), BF16),
            shape((kv_heads, window, GROUP * rows), BF16),
        ],
        scratch_shapes=[
            pltpu.VMEM((window, HEAD_SIZE), BF16),
            pltpu.VMEM((window, 2 * rows), F32),
            pltpu.VMEM((window, 2 * rows), F32),
            pltpu.VMEM((window, GROUP * rows), BF16),
        ],
        compiler_params=grant,
    )(qa, gs, late, full, a, ax, b, bx)
    d_queries = pl.pallas_call(
        functools.partial(query_kernel, rows),
        in_specs=[in_vmem] * 2,
        out_specs=in_vmem,
        out_shape=shape((rows, q_width), BF16),
        scratch_shapes=[pltpu.VMEM((HEAD_SIZE, window), BF16)],
        compiler_params=grant,
        cost_estimate=pl.CostEstimate(flops=1 << 28, bytes_accessed=4 << 20, transcendentals=0),
    )(ka, dst)

    got2, got1 = swap(give2, devices), swap(give1, devices)
    back2 = (keep2.astype(F32) + got2.astype(F32)).astype(BF16)
    back1 = jnp.where(odd, jnp.zeros_like(keep1), (keep1.astype(F32) + got1.astype(F32)).astype(BF16))
    home_a = lax.ppermute(jnp.where(odd_pair, back1, back2), AXES, [(d, s) for s, d in a_moves])
    home_b = lax.ppermute(jnp.where(odd_pair, back2, back1), AXES, [(d, s) for s, d in b_moves])
    arrived = home_a.astype(F32) + home_b.astype(F32)
    mine_in = jnp.where(odd, arrived[2:], arrived[:2])
    mate_in = jnp.where(odd, arrived[:2], arrived[2:])
    from_mate = swap((own_mate + mate_in).astype(BF16), devices)
    total = (own + mine_in + from_mate.astype(F32)).astype(BF16)
    return d_queries, total[0], total[1]


def solution(mesh):
    spec = P(AXES, None)
    return jax.shard_map(
        local_grads,
        mesh=mesh,
        in_specs=(spec, spec, spec, spec, P()),
        out_specs=(spec, spec, spec),
        check_vma=False,
    )
```

time: 31.4 us -> 32.4 us (1.032)
  local copies, waits for them, and re-layouts: 0.65 us -> 3.18 us
  waiting for transfers between devices: 13.4 us -> 11.3 us
  Pallas kernels: 5.17 us -> 6.16 us
  starting transfers between devices: 10.3 us -> 9.82 us
    unnamed x8 -> x6, local copies, waits for them, and re-layouts: 0.02 us -> 2.55 us
    ppermute x7 -> x6, waiting for transfers between devices: 4.61 us -> 2.18 us  [swap(): return lax.ppermute(value, AXES, [(d, d ^ 1) for d in range(devices)])]
    pallas_call x1 -> x3, Pallas kernels: 5.17 us -> 6.16 us  [the longest x1 3.86 us: local_grads(): pl.pallas_call(functools.partial(attention_kernel, rows), in_specs=[in_vm...]
    select_n x2, other arithmetic: 0.93 us -> 0.11 us  [the longest x1 0.1 us: local_grads(): jnp.where(odd_pair, back1, back2)]
    another operation x0 -> x1, other arithmetic: none -> 0.78 us  [local_grads(): mine = lax.optimization_barrier(jnp.stack([keys, values]))]
    ppermute x7 -> x6, starting transfers between devices: 3.23 us -> 2.74 us  [swap(): return lax.ppermute(value, AXES, [(d, d ^ 1) for d in range(devices)])]
  transfers between devices with their start and end apart: 11 -> 10, of which waited for: 10 -> 7; matrix products, arithmetic and copies ran while one was open for 0% -> 0% of each run, Pallas kernels for 0% -> 7%
where the time goes in v3:
time: 32.4 us; the launch traced here: 32.1 us
  waiting for transfers between devices  11.3 us (35%)
  starting transfers between devices  9.82 us (30%)
  Pallas kernels  6.16 us (19%)
  local copies, waits for them, and re-layouts  3.18 us (10%)
  other arithmetic  0.99 us (3%)
  between operations  0.7 us (2%)
    pallas_call x1, Pallas kernels, local_grads(): pl.pallas_call(functools.partial(attention_kernel, rows), in_specs=[in_vm...  3.86 us
    ppermute x1, starting transfers between devices, local_grads(): b = lax.ppermute(full, AXES, b_moves)  3.61 us
    ppermute x1, waiting for transfers between devices, local_grads(): lax.ppermute(jnp.where(odd_pair, back1, back2), AXES, [(d, s) for s, d in...  2.96 us
    ppermute x6, starting transfers between devices, swap(): return lax.ppermute(value, AXES, [(d, d ^ 1) for d in range(devices)])  2.74 us
    ppermute x1, waiting for transfers between devices, local_grads(): a = lax.ppermute(full, AXES, a_moves)  2.58 us
    unnamed x6, local copies, waits for them, and re-layouts  2.55 us
    ppermute x6, waiting for transfers between devices, swap(): return lax.ppermute(value, AXES, [(d, d ^ 1) for d in range(devices)])  2.18 us
    ppermute x1, waiting for transfers between devices, local_grads(): lax.ppermute(jnp.where(odd_pair, back2, back1), AXES, [(d, s) for s, d in...  1.81 us
  transfers between devices with their start and end apart: 10, of which 7 were waited for; matrix products, arithmetic and copies ran while one was open for 0% of the time, Pallas kernels for 7%

profile of v3, /device:TPU:0, one launch (start us, length us, event | category | flops | bytes accessed | tf_op | source)
XLA Modules:
  0.0 32.1 jit_solution(6179628887451857036)
XLA Ops:
  0.6 0.8 %pad_maximum_fusion.1 = bf16[2,128,128]{2,1,0:T(8,128)(2,1)S(1)} fusion(bf16[1,128,128]{2,1,0:T(8,128)(2,1)} %bitcast.6, bf16[1,128,128]{2,1,0:T(8,128)(2,1)} %bitcast.7), kind=kLoop, calls=%fused_computation.9 | loop fusion | flops 32768 | bytes 131072 | tf_op jit(solution)/shard_map/stack | solution.py:243
  1.4 0.5 %collective-permute-start = (bf16[2,128,128]{2,1,0:T(8,128)(2,1)S(1)}, bf16[2,128,128]{2,1,0:T(8,128)(2,1)S(1)}, u32[]{:S(2)}, u32[]{:S(2)}) collective-permute-start(bf16[2,128,128]{2,1,0:T(8,128)(2,1)S(1)} %pad_maximum_fusion.1), channel_id=1, source_target_pairs={{0,1},{1,0},{2,3},{3,2},{4,5},{5,4},{6,7},{7,6},{8,9},{9,8},{10,11... | collective-permute-start | bytes 196616 | tf_op jit(solution)/shard_map/ppermute | solution.py:49
  2.0 0.9 %collective-permute-done = bf16[2,128,128]{2,1,0:T(8,128)(2,1)S(1)} collective-permute-done((bf16[2,128,128]{2,1,0:T(8,128)(2,1)S(1)}, bf16[2,128,128]{2,1,0:T(8,128)(2,1)S(1)}, u32[]{:S(2)}, u32[]{:S(2)}) %collective-permute-start) | collective-permute-done | bytes 65568 | tf_op jit(solution)/shard_map/ppermute | solution.py:49
  2.9 3.6 %collective-permute-start.3 = (bf16[4,128,128]{2,1,0:T(8,128)(2,1)S(1)}, bf16[4,128,128]{2,1,0:T(8,128)(2,1)S(1)}, u32[]{:S(2)}, u32[]{:S(2)}) collective-permute-start(bf16[4,128,128]{2,1,0:T(8,128)(2,1)S(1)} %pad_maximum_fusion.full_ref), channel_id=1, source_target_pairs={{0,7},{2,4},{3,6},{4,11},{6,8},{7,10},{8,15},{9,1},{10,12},{11,14}... | collective-permute-start | bytes 393224 | tf_op jit(solution)/shard_map/ppermute | solution.py:247
  6.5 0.8 %collective-permute-start.1 = (bf16[4,128,128]{2,1,0:T(8,128)(2,1)S(1)}, bf16[4,128,128]{2,1,0:T(8,128)(2,1)S(1)}, u32[]{:S(2)}, u32[]{:S(2)}) collective-permute-start(bf16[4,128,128]{2,1,0:T(8,128)(2,1)S(1)} %pad_maximum_fusion.full_ref), channel_id=1, source_target_pairs={{0,2},{1,4},{2,9},{4,6},{5,8},{6,13},{8,10},{9,12},{10,17},{11,3},... | collective-permute-start | bytes 393224 | tf_op jit(solution)/shard_map/ppermute | solution.py:246
  7.3 1.8 %collective-permute-done.3.b_ref = bf16[4,128,128]{2,1,0:T(8,128)(2,1)S(1)} collective-permute-done((bf16[4,128,128]{2,1,0:T(8,128)(2,1)S(1)}, bf16[4,128,128]{2,1,0:T(8,128)(2,1)S(1)}, u32[]{:S(2)}, u32[]{:S(2)}) %collective-permute-start.3) | collective-permute-done | bytes 131104 | tf_op jit(solution)/shard_map/ppermute | solution.py:247
  9.0 2.6 %collective-permute-done.1.a_ref = bf16[4,128,128]{2,1,0:T(8,128)(2,1)S(1)} collective-permute-done((bf16[4,128,128]{2,1,0:T(8,128)(2,1)S(1)}, bf16[4,128,128]{2,1,0:T(8,128)(2,1)S(1)}, u32[]{:S(2)}, u32[]{:S(2)}) %collective-permute-start.1) | collective-permute-done | bytes 131104 | tf_op jit(solution)/shard_map/ppermute | solution.py:246
  11.6 0.9 %copy-done = bf16[128,1024]{1,0:T(8,128)(2,1)S(1)} copy-done((bf16[128,1024]{1,0:T(8,128)(2,1)S(1)}, bf16[128,1024]{1,0:T(8,128)(2,1)}, u32[]{:S(2)}) %copy-start) | copy-done | bytes 262168
  12.6 0.9 %copy-done.1 = bf16[128,1024]{1,0:T(8,128)(2,1)S(1)} copy-done((bf16[128,1024]{1,0:T(8,128)(2,1)S(1)}, bf16[128,1024]{1,0:T(8,128)(2,1)}, u32[]{:S(2)}) %copy-start.1) | copy-done | bytes 262168
  13.5 0.7 %copy-done.2 = s32[11]{0:T(128)S(1)} copy-done((s32[11]{0:T(128)S(1)}, s32[11]{0:T(128)}, u32[]{:S(2)}) %copy-start.2) | copy-done | bytes 68
  14.2 1.0 %shard_map.76 = (bf16[1024,256]{1,0:T(8,128)(2,1)S(1)}, bf16[1024,128]{1,0:T(8,128)(2,1)S(1)}, bf16[896,128]{1,0:T(8,128)(2,1)S(1)}) custom-call(s32[11]{0:T(128)S(1)} %copy-done.2, bf16[128,1024]{1,0:T(8,128)(2,1)S(1)} %copy-done, bf16[128,1024]{1,0:T(8,128)(2,1)S(1)} %copy-done.1), custom_call_target="tpu_custom_call" | custom-call | bytes 4194304 | tf_op jit(solution)/shard_map/pallas_call | solution.py:257
  15.3 3.9 %shard_map.77 = (f32[2,128,128]{2,1,0:T(8,128)S(1)}, f32[2,128,128]{2,1,0:T(8,128)S(1)}, bf16[4,128,128]{2,1,0:T(8,128)(2,1)S(1)}, bf16[4,128,128]{2,1,0:T(8,128...) custom-call(bf16[1024,256]{1,0:T(8,128)(2,1)S(1)} %get-tuple-element, ...), custom_call_target="tpu_custom_call" | custom-call | tf_op jit(solution)/shard_map/pallas_call | solution.py:270
  19.1 0.6 %collective-permute-start.5 = (bf16[4,128,128]{2,1,0:T(8,128)(2,1)S(1)}, bf16[4,128,128]{2,1,0:T(8,128)(2,1)S(1)}, u32[]{:S(2)}, u32[]{:S(2)}) collective-permute-start(bf16[4,128,128]{2,1,0:T(8,128)(2,1)S(1)} %get-tuple-element.21), channel_id=1, source_target_pairs={{0,1},{1,0},{2,3},{3,2},{4,5},{5,4},{6,7},{7,6},{8,9},{9,8},{10,11... | collective-permute-start | bytes 393224 | tf_op jit(solution)/shard_map/ppermute | solution.py:49
  19.7 0.1 collective-permute-start.6
  19.8 0.9 %collective-permute-done.5 = bf16[4,128,128]{2,1,0:T(8,128)(2,1)S(1)} collective-permute-done((bf16[4,128,128]{2,1,0:T(8,128)(2,1)S(1)}, bf16[4,128,128]{2,1,0:T(8,128)(2,1)S(1)}, u32[]{:S(2)}, u32[]{:S(2)}) %collective-permute-start.5) | collective-permute-done | bytes 131104 | tf_op jit(solution)/shard_map/ppermute | solution.py:49
  20.7 0.4 %collective-permute-done.6 = bf16[4,128,128]{2,1,0:T(8,128)(2,1)S(1)} collective-permute-done((bf16[4,128,128]{2,1,0:T(8,128)(2,1)S(1)}, bf16[4,128,128]{2,1,0:T(8,128)(2,1)S(1)}, u32[]{:S(2)}, u32[]{:S(2)}) %collective-permute-start.6) | collective-permute-done | bytes 131104 | tf_op jit(solution)/shard_map/ppermute | solution.py:49
  21.0 0.1 broadcast_select_fusion.1
  21.1 1.2 %collective-permute-start.7 = (bf16[4,128,128]{2,1,0:T(8,128)(2,1)S(1)}, bf16[4,128,128]{2,1,0:T(8,128)(2,1)S(1)}, u32[]{:S(2)}, u32[]{:S(2)}) collective-permute-start(bf16[4,128,128]{2,1,0:T(8,128)(2,1)S(1)} %get-tuple-element.25), channel_id=1, source_target_pairs={{2,0},{4,1},{9,2},{6,4},{8,5},{13,6},{10,8},{12,9},{17,10},{3,11},... | collective-permute-start | bytes 393224 | tf_op jit(solution)/shard_map/ppermute | solution.py:305
  22.3 1.5 %collective-permute-start.8 = (bf16[4,128,128]{2,1,0:T(8,128)(2,1)S(1)}, bf16[4,128,128]{2,1,0:T(8,128)(2,1)S(1)}, u32[]{:S(2)}, u32[]{:S(2)}) collective-permute-start(bf16[4,128,128]{2,1,0:T(8,128)(2,1)S(1)} %get-tuple-element.26), channel_id=1, source_target_pairs={{7,0},{4,2},{6,3},{11,4},{8,6},{10,7},{15,8},{1,9},{12,10},{14,11}... | collective-permute-start | bytes 393224 | tf_op jit(solution)/shard_map/ppermute | solution.py:306
  23.8 3.0 %collective-permute-done.7 = bf16[4,128,128]{2,1,0:T(8,128)(2,1)S(1)} collective-permute-done((bf16[4,128,128]{2,1,0:T(8,128)(2,1)S(1)}, bf16[4,128,128]{2,1,0:T(8,128)(2,1)S(1)}, u32[]{:S(2)}, u32[]{:S(2)}) %collective-permute-start.7) | collective-permute-done | bytes 131104 | tf_op jit(solution)/shard_map/ppermute | solution.py:305
  26.8 1.8 %collective-permute-done.8 = bf16[4,128,128]{2,1,0:T(8,128)(2,1)S(1)} collective-permute-done((bf16[4,128,128]{2,1,0:T(8,128)(2,1)S(1)}, bf16[4,128,128]{2,1,0:T(8,128)(2,1)S(1)}, u32[]{:S(2)}, u32[]{:S(2)}) %collective-permute-start.8) | collective-permute-done | bytes 131104 | tf_op jit(solution)/shard_map/ppermute | solution.py:306
  28.7 1.6 %collective-permute-start.9 = (bf16[2,128,128]{2,1,0:T(8,128)(2,1)S(1)}, bf16[2,128,128]{2,1,0:T(8,128)(2,1)S(1)}, u32[]{:S(2)}, u32[]{:S(2)}) collective-permute-start(bf16[2,128,128]{2,1,0:T(8,128)(2,1)S(1)} %add_convert_fusion.3), channel_id=1, source_target_pairs={{0,1},{1,0},{2,3},{3,2},{4,5},{5,4},{6,7},{7,6},{8,9},{9,8},{10,11... | collective-permute-start | bytes 196616 | tf_op jit(solution)/shard_map/ppermute | solution.py:49
  30.2 1.3 %shard_map.78 = bf16[128,1024]{1,0:T(8,128)(2,1)} custom-call(bf16[1,896,256]{2,1,0:T(8,128)(2,1)S(1)} %get-tuple-element.17.ka_ref, bf16[1,896,1024]{2,1,0:T(8,128)(2,1)S(1)} %get-tuple-element.18.dst_ref), custom_call_target="tpu_custom_call" | custom-call | flops 268435456 | bytes 4194304 | tf_op jit(solution)/shard_map/pallas_call | solution.py:292
  31.5 0.6 %slice_bitcast_fusion = (bf16[128,128]{1,0:T(8,128)(2,1)}, bf16[128,128]{1,0:T(8,128)(2,1)}) fusion(bf16[2,128,128]{2,1,0:T(8,128)(2,1)S(1)} %add_convert_fusion.2), kind=kLoop, calls=%fused_computation.12 | loop fusion | bytes 131072 | tf_op jit(solution)/shard_map/squeeze | solution.py:312
  (13 shorter events, 0.1 us)
Async XLA Ops:
  1.4 1.4 %collective-permute-start = (bf16[2,128,128]{2,1,0:T(8,128)(2,1)S(1)}, bf16[2,128,128]{2,1,0:T(8,128)(2,1)S(1)}, u32[]{:S(2)}, u32[]{:S(2)}) collective-permute-start(bf16[2,128,128]{2,1,0:T(8,128)(2,1)S(1)} %pad_maximum_fusion.1), channel_id=1, source_target_pairs={{0,1},{1,0},{2,3},{3,2},{4,5},{5,4},{6,7},{7,6},{8,9},{9,8},{10,11... | collective-permute-start | bytes 196616 | tf_op jit(solution)/shard_map/ppermute | solution.py:49
  2.9 6.1 %collective-permute-start.3 = (bf16[4,128,128]{2,1,0:T(8,128)(2,1)S(1)}, bf16[4,128,128]{2,1,0:T(8,128)(2,1)S(1)}, u32[]{:S(2)}, u32[]{:S(2)}) collective-permute-start(bf16[4,128,128]{2,1,0:T(8,128)(2,1)S(1)} %pad_maximum_fusion.full_ref), channel_id=1, source_target_pairs={{0,7},{2,4},{3,6},{4,11},{6,8},{7,10},{8,15},{9,1},{10,12},{11,14}... | collective-permute-start | bytes 393224 | tf_op jit(solution)/shard_map/ppermute | solution.py:247
  6.5 5.1 %collective-permute-start.1 = (bf16[4,128,128]{2,1,0:T(8,128)(2,1)S(1)}, bf16[4,128,128]{2,1,0:T(8,128)(2,1)S(1)}, u32[]{:S(2)}, u32[]{:S(2)}) collective-permute-start(bf16[4,128,128]{2,1,0:T(8,128)(2,1)S(1)} %pad_maximum_fusion.full_ref), channel_id=1, source_target_pairs={{0,2},{1,4},{2,9},{4,6},{5,8},{6,13},{8,10},{9,12},{10,17},{11,3},... | collective-permute-start | bytes 393224 | tf_op jit(solution)/shard_map/ppermute | solution.py:246
  9.0 6.2 %collective-permute-start.4 = (bf16[4,128,128]{2,1,0:T(8,128)(2,1)S(1)}, bf16[4,128,128]{2,1,0:T(8,128)(2,1)S(1)}, u32[]{:S(2)}, u32[]{:S(2)}) collective-permute-start(bf16[4,128,128]{2,1,0:T(8,128)(2,1)S(1)} %collective-permute-done.3.b_ref), channel_id=1, source_target_pairs={{0,1},{1,0},{2,3},{3,2},{4,5},{5,4},{6,7},{7,6},{8,9},{9,8},{10,11... | collective-permute-start | bytes 393224 | tf_op jit(solution)/shard_map/ppermute | solution.py:49
  11.6 3.6 %collective-permute-start.2 = (bf16[4,128,128]{2,1,0:T(8,128)(2,1)S(1)}, bf16[4,128,128]{2,1,0:T(8,128)(2,1)S(1)}, u32[]{:S(2)}, u32[]{:S(2)}) collective-permute-start(bf16[4,128,128]{2,1,0:T(8,128)(2,1)S(1)} %collective-permute-done.1.a_ref), channel_id=1, source_target_pairs={{0,1},{1,0},{2,3},{3,2},{4,5},{5,4},{6,7},{7,6},{8,9},{9,8},{10,11... | collective-permute-start | bytes 393224 | tf_op jit(solution)/shard_map/ppermute | solution.py:49
  11.6 1.0 %copy-start = (bf16[128,1024]{1,0:T(8,128)(2,1)S(1)}, bf16[128,1024]{1,0:T(8,128)(2,1)}, u32[]{:S(2)}) copy-start(bf16[128,1024]{1,0:T(8,128)(2,1)} %q_ref.1) | copy-start | bytes 786436
  12.6 0.9 %copy-start.1 = (bf16[128,1024]{1,0:T(8,128)(2,1)S(1)}, bf16[128,1024]{1,0:T(8,128)(2,1)}, u32[]{:S(2)}) copy-start(bf16[128,1024]{1,0:T(8,128)(2,1)} %g_ref.1) | copy-start | bytes 786436
  13.5 0.7 %copy-start.2 = (s32[11]{0:T(128)S(1)}, s32[11]{0:T(128)}, u32[]{:S(2)}) copy-start(s32[11]{0:T(128)} %lens_ref.1) | copy-start | bytes 136
  19.1 1.6 %collective-permute-start.5 = (bf16[4,128,128]{2,1,0:T(8,128)(2,1)S(1)}, bf16[4,128,128]{2,1,0:T(8,128)(2,1)S(1)}, u32[]{:S(2)}, u32[]{:S(2)}) collective-permute-start(bf16[4,128,128]{2,1,0:T(8,128)(2,1)S(1)} %get-tuple-element.21), channel_id=1, source_target_pairs={{0,1},{1,0},{2,3},{3,2},{4,5},{5,4},{6,7},{7,6},{8,9},{9,8},{10,11... | collective-permute-start | bytes 393224 | tf_op jit(solution)/shard_map/ppermute | solution.py:49
  19.7 1.3 %collective-permute-start.6 = (bf16[4,128,128]{2,1,0:T(8,128)(2,1)S(1)}, bf16[4,128,128]{2,1,0:T(8,128)(2,1)S(1)}, u32[]{:S(2)}, u32[]{:S(2)}) collective-permute-start(bf16[4,128,128]{2,1,0:T(8,128)(2,1)S(1)} %get-tuple-element.23), channel_id=1, source_target_pairs={{0,1},{1,0},{2,3},{3,2},{4,5},{5,4},{6,7},{7,6},{8,9},{9,8},{10,11... | collective-permute-start | bytes 393224 | tf_op jit(solution)/shard_map/ppermute | solution.py:49
  21.1 5.7 %collective-permute-start.7 = (bf16[4,128,128]{2,1,0:T(8,128)(2,1)S(1)}, bf16[4,128,128]{2,1,0:T(8,128)(2,1)S(1)}, u32[]{:S(2)}, u32[]{:S(2)}) collective-permute-start(bf16[4,128,128]{2,1,0:T(8,128)(2,1)S(1)} %get-tuple-element.25), channel_id=1, source_target_pairs={{2,0},{4,1},{9,2},{6,4},{8,5},{13,6},{10,8},{12,9},{17,10},{3,11},... | collective-permute-start | bytes 393224 | tf_op jit(solution)/shard_map/ppermute | solution.py:305
  22.3 6.3 %collective-permute-start.8 = (bf16[4,128,128]{2,1,0:T(8,128)(2,1)S(1)}, bf16[4,128,128]{2,1,0:T(8,128)(2,1)S(1)}, u32[]{:S(2)}, u32[]{:S(2)}) collective-permute-start(bf16[4,128,128]{2,1,0:T(8,128)(2,1)S(1)} %get-tuple-element.26), channel_id=1, source_target_pairs={{7,0},{4,2},{6,3},{11,4},{8,6},{10,7},{15,8},{1,9},{12,10},{14,11}... | collective-permute-start | bytes 393224 | tf_op jit(solution)/shard_map/ppermute | solution.py:306
  28.7 2.8 %collective-permute-start.9 = (bf16[2,128,128]{2,1,0:T(8,128)(2,1)S(1)}, bf16[2,128,128]{2,1,0:T(8,128)(2,1)S(1)}, u32[]{:S(2)}, u32[]{:S(2)}) collective-permute-start(bf16[2,128,128]{2,1,0:T(8,128)(2,1)S(1)} %add_convert_fusion.3), channel_id=1, source_target_pairs={{0,1},{1,0},{2,3},{3,2},{4,5},{5,4},{6,7},{7,6},{8,9},{9,8},{10,11... | collective-permute-start | bytes 196616 | tf_op jit(solution)/shard_map/ppermute | solution.py:49

commit v4 on v2

v4 whole, which is shorter than its diff:
```python
import functools
import math

import jax
import jax.numpy as jnp
from jax import lax
from jax.experimental import pallas as pl
from jax.experimental.pallas import tpu as pltpu
from jax.sharding import PartitionSpec as P

HEAD_SIZE = 128
GROUP = 8
AXES = ("dp", "seq")
NEG = -1e30
FAR = 1 << 30
SCALE = 1.0 / math.sqrt(HEAD_SIZE)
SCALE2 = SCALE * math.log2(math.e)
F32 = jnp.float32
BF16 = jnp.bfloat16


def weave(devices, turn):
    pairs = devices // 2
    moves, sources, taken = [], [], set()
    for c in range(pairs):
        back = -4 if c % 4 < 2 else -8
        if c % 2 == turn:
            steps = ((0, 1, 0), (1, 2, 0))
        else:
            steps = ((0, 3, 1), (1, back, 1))
        for core, step, target_core in steps:
            target = c + step
            if 0 <= target < pairs:
                moves.append((2 * c + core, 2 * target + target_core))
                taken.add(2 * target + target_core)
            else:
                sources.append(2 * c + core)
    targets = [d for d in range(devices) if d not in taken]
    rest = list(zip(sources, targets))
    for i, (source, target) in enumerate(rest):
        if source == target:
            j = i - 1 if i else 1
            rest[i], rest[j] = (source, rest[j][1]), (rest[j][0], target)
    return moves + rest


def swap(value, devices):
    return lax.ppermute(value, AXES, [(d, d ^ 1) for d in range(devices)])


def dot_nt(a, b):
    return lax.dot_general(a, b, (((1,), (1,)), ((), ())), preferred_element_type=F32)


def dot_nn(a, b):
    return lax.dot_general(a, b, (((1,), (0,)), ((), ())), preferred_element_type=F32)


def where_am_i():
    me = lax.axis_index("dp") * lax.axis_size("seq") + lax.axis_index("seq")
    return me, lax.rem(me, 2) == 1, lax.rem(me // 2, 2) == 1


def holds_own(block, odd, odd_pair):
    return odd & (odd_pair if block else jnp.logical_not(odd_pair))


def prepare_kernel(
    rows, lens_hbm, q_hbm, g_hbm, q_ref, g_ref, member_ref, late_ref, lens_ref, lens_sem, q_sem, g_sem
):
    t = rows
    fetch = pltpu.make_async_copy(lens_hbm, lens_ref, lens_sem)
    fetch_q = pltpu.make_async_copy(q_hbm, q_ref, q_sem)
    fetch_g = pltpu.make_async_copy(g_hbm, g_ref, g_sem)
    fetch.start()
    fetch_q.start()
    fetch_g.start()
    me, odd, odd_pair = where_am_i()
    lane = lax.broadcasted_iota(jnp.int32, (1, HEAD_SIZE), 1)
    down = lax.broadcasted_iota(jnp.int32, (t, HEAD_SIZE), 0)
    pair_first = (me // 2) * 2 * t
    far = jnp.full((1, HEAD_SIZE), FAR, jnp.int32)
    zero = jnp.int32(0)
    fetch.wait()
    for side in (0, 1):
        first = (me if side == 0 else jnp.where(odd, me - 1, me + 1)) * t

        def next_doc(j, carry, first=first):
            end, count, starts, stops = carry
            begin, end = end, end + lens_ref[j]
            live = end > first
            here = (lane == count) & live
            starts, stops = jnp.where(here, begin, starts), jnp.where(here, end, stops)
            return end, count + live.astype(jnp.int32), starts, stops

        _, _, starts, stops = lax.fori_loop(0, lens_ref.shape[0], next_doc, (zero, zero, far, far))
        q_pos = first + down
        member = jnp.where((q_pos >= starts) & (q_pos < stops), 1.0, 0.0).astype(BF16)
        member_ref[side, :t, :] = member
        member_ref[side, t:, :] = member
        for block in (0, 1):
            one_back = jnp.where(odd, 0, -1)
            far_back = jnp.where(odd, -3, -2)
            single = odd_pair if block else jnp.logical_not(odd_pair)
            base = pair_first + jnp.where(single, one_back, far_back) * 2 * t
            for part in (0, 1):
                k_pos = base + part * t + down
                blocked = (k_pos < starts) | (k_pos >= first + t)
                late_ref[block, side, part * t : (part + 1) * t, :] = jnp.where(
                    blocked, NEG, 0.0
                ).astype(BF16)
    fetch_q.wait()
    fetch_g.wait()


def stacked(ref, first_head, count):
    return jnp.concatenate(
        [ref[:, h * HEAD_SIZE : (h + 1) * HEAD_SIZE] for h in range(first_head, first_head + count)],
        axis=0,
    )


def combine(one, two):
    high = jnp.maximum(one[0], two[0])
    keep_one, keep_two = jnp.exp2(one[0] - high), jnp.exp2(two[0] - high)
    return high, one[1] * keep_one + two[1] * keep_two, one[2] * keep_one + two[2] * keep_two


def score_kernel(rows, block, *refs):
    qs, gs = (refs[0], refs[2]), (refs[1], refs[3])
    member_ref, late_ref, full_ref, got_ref = refs[4:8]
    before_ref = refs[8] if block else None
    s_ref, g_ref, stats_ref = refs[-3:]
    t = rows
    _, odd, odd_pair = where_am_i()
    own = holds_own(block, odd, odd_pair)
    reach = jnp.where(own, 0, FAR)
    down = lax.broadcasted_iota(jnp.int32, (t, t), 0)
    across = lax.broadcasted_iota(jnp.int32, (t, t), 1)
    causal = down - across <= reach
    causal = jnp.concatenate([causal, causal], axis=1)

    def fold(x, op):
        return op(x.reshape(-1, 8, 2 * t), axis=0)

    for head in range(full_ref.shape[2] // HEAD_SIZE):
        lanes = slice(head * HEAD_SIZE, (head + 1) * HEAD_SIZE)
        key, value = (jnp.where(own, full_ref[i, :, lanes], got_ref[i, :, lanes]) for i in (0, 1))
        for side in (0, 1):
            key_late = jnp.concatenate([key, late_ref[block, side]], axis=1)
            for pair in range(GROUP // 2):
                cols = slice((side * GROUP + pair * 2) * t, (side * GROUP + pair * 2 + 2) * t)
                q_rows = stacked(qs[side], head * GROUP + pair * 2, 2)
                q_rows = jnp.concatenate([q_rows, member_ref[side]], axis=1)
                s = dot_nt(key_late, q_rows) * SCALE2
                g = dot_nt(value, stacked(gs[side], head * GROUP + pair * 2, 2))
                parts = [s[:t], s[t:]]
                parts[1 - side] = jnp.where(causal, parts[1 - side], NEG)
                s_ref[head, :t, cols] = parts[0]
                s_ref[head, t:, cols] = parts[1]
                g_ref[head, :, cols] = g
                top = jnp.maximum(fold(parts[0], jnp.max), fold(parts[1], jnp.max))
                top = jnp.max(top, axis=0, keepdims=True)
                total = jnp.zeros((8, 2 * t), F32)
                weighted = jnp.zeros((8, 2 * t), F32)
                for part in (0, 1):
                    e = jnp.exp2(parts[part] - top)
                    total += fold(e, jnp.sum)
                    weighted += fold(e * g[part * t : (part + 1) * t], jnp.sum)
                found = (
                    top,
                    jnp.sum(total, axis=0, keepdims=True),
                    jnp.sum(weighted, axis=0, keepdims=True),
                )
                if block:
                    found = combine(
                        found, [before_ref[3 * head + i : 3 * head + i + 1, cols] for i in range(3)]
                    )
                for i in range(3):
                    stats_ref[3 * head + i : 3 * head + i + 1, cols] = found[i]


def grads_kernel(rows, block, *refs):
    qs, gs = (refs[0], refs[2]), (refs[1], refs[3])
    s_ref, g_ref, stats_ref, other_ref, home_ref, own_ref, ds_ref, pt = refs[4:]
    t = rows
    _, odd, odd_pair = where_am_i()
    own = holds_own(block, odd, odd_pair)
    for head in range(s_ref.shape[0]):
        lanes = slice(head * HEAD_SIZE, (head + 1) * HEAD_SIZE)
        grads = [None, None]
        for side in (0, 1):
            for pair in range(GROUP // 2):
                cols = slice((side * GROUP + pair * 2) * t, (side * GROUP + pair * 2 + 2) * t)
                turned = slice(
                    ((1 - side) * GROUP + pair * 2) * t, ((1 - side) * GROUP + pair * 2 + 2) * t
                )
                high, total, weighted = combine(
                    [stats_ref[3 * head + i : 3 * head + i + 1, cols] for i in range(3)],
                    [other_ref[3 * head + i : 3 * head + i + 1, turned] for i in range(3)],
                )
                level, delta = high + jnp.log2(total), weighted / total
                p = jnp.exp2(s_ref[head, :, cols] - level)
                pt[:, cols] = p.astype(BF16)
                ds_ref[head, :, cols] = (p * (g_ref[head, :, cols] - delta)).astype(BF16)
            cols = slice(side * GROUP * t, (side + 1) * GROUP * t)
            dk = dot_nn(ds_ref[head, :, cols], stacked(qs[side], head * GROUP, GROUP)) * SCALE
            dv = dot_nn(pt[:, cols], stacked(gs[side], head * GROUP, GROUP))
            grads = [dk, dv] if side == 0 else [grads[0] + dk, grads[1] + dv]
        for kind, grad in enumerate(grads):
            none = jnp.zeros_like(grad)
            home_ref[kind, :, lanes] = jnp.where(own, none, grad).astype(BF16)
            own_ref[kind, :, lanes] = jnp.where(own, grad, none)


def query_kernel(rows, full_ref, b_ref, a_ref, dsb_ref, dsa_ref, mine_ref, mate_ref):
    t = rows
    _, odd, odd_pair = where_am_i()
    for head in range(dsb_ref.shape[0]):
        lanes = slice(head * HEAD_SIZE, (head + 1) * HEAD_SIZE)
        key_b, key_a = (
            jnp.where(holds_own(block, odd, odd_pair), full_ref[0, :, lanes], got[0, :, lanes]).T
            for block, got in ((0, b_ref), (1, a_ref))
        )
        for side, out_ref in ((1, mate_ref), (0, mine_ref)):
            cols = slice(side * GROUP * t, (side + 1) * GROUP * t)
            dqt = dot_nn(key_b, dsb_ref[head, :, cols]) + dot_nn(key_a, dsa_ref[head, :, cols])
            dqt = dqt * SCALE
            for h in range(GROUP):
                at = (head * GROUP + h) * HEAD_SIZE
                out_ref[:, at : at + HEAD_SIZE] = dqt[:, h * t : (h + 1) * t].T.astype(out_ref.dtype)


def local_grads(queries, keys, values, d_out, doc_lengths):
    rows, q_width = queries.shape
    kv_width = keys.shape[1]
    kv_heads = kv_width // HEAD_SIZE
    devices = lax.axis_size("dp") * lax.axis_size("seq")
    _, odd, _ = where_am_i()
    a_moves, b_moves = weave(devices, 0), weave(devices, 1)

    mine = lax.optimization_barrier(jnp.stack([keys, values]))
    mate_k, mate_v = swap(keys, devices), swap(values, devices)
    mate = jnp.stack([mate_k, mate_v])
    full = jnp.concatenate([jnp.where(odd, mate, mine), jnp.where(odd, mine, mate)], axis=1)
    full = lax.optimization_barrier(full)
    b = lax.ppermute(full, AXES, b_moves)
    a = lax.ppermute(full, AXES, a_moves)
    mate_q = swap(queries, devices)
    mate_g = swap(d_out, devices)

    shape = jax.ShapeDtypeStruct
    in_vmem = pl.BlockSpec(memory_space=pltpu.VMEM)
    grant = pltpu.CompilerParams(vmem_limit_bytes=(12 + 10 * kv_heads) << 20)

    def cost(flops):
        return pl.CostEstimate(flops=flops, bytes_accessed=1 << 20, transcendentals=0)

    width = 2 * GROUP * rows
    mine_q, mine_g, member, late = pl.pallas_call(
        functools.partial(prepare_kernel, rows),
        in_specs=[pl.BlockSpec(memory_space=pltpu.HBM)] * 3,
        out_specs=[in_vmem] * 4,
        out_shape=[
            shape((rows, q_width), BF16),
            shape((rows, q_width), BF16),
            shape((2, 2 * rows, HEAD_SIZE), BF16),
            shape((2, 2, 2 * rows, HEAD_SIZE), BF16),
        ],
        scratch_shapes=[
            pltpu.SMEM(doc_lengths.shape, jnp.int32),
            pltpu.SemaphoreType.DMA,
            pltpu.SemaphoreType.DMA,
            pltpu.SemaphoreType.DMA,
        ],
        compiler_params=grant,
        cost_estimate=cost(1 << 20),
    )(doc_lengths, queries, d_out)

    rows_of = (mine_q, mine_g, mate_q, mate_g)

    def scores(block, got, *before):
        return pl.pallas_call(
            functools.partial(score_kernel, rows, block),
            in_specs=[in_vmem] * (8 + len(before)),
            out_specs=[in_vmem] * 3,
            out_shape=[
                shape((kv_heads, 2 * rows, width), F32),
                shape((kv_heads, 2 * rows, width), F32),
                shape((3 * kv_heads, width), F32),
            ],
            compiler_params=grant,
            cost_estimate=cost(1 << 28),
        )(*rows_of, member, late, full, got, *before)

    def grads(block, s, g, stats, other):
        return pl.pallas_call(
            functools.partial(grads_kernel, rows, block),
            in_specs=[in_vmem] * 8,
            out_specs=[in_vmem] * 3,
            out_shape=[
                shape((2, 2 * rows, kv_width), BF16),
                shape((2, 2 * rows, kv_width), F32),
                shape((kv_heads, 2 * rows, width), BF16),
            ],
            scratch_shapes=[pltpu.VMEM((2 * rows, width), BF16)],
            compiler_params=grant,
            cost_estimate=cost(1 << 28),
        )(*rows_of, s, g, stats, other)

    s_b, g_b, stats_b = scores(0, b)
    s_a, g_a, stats = scores(1, a, stats_b)
    other = swap(stats, devices)
    back_b, own_b, ds_b = grads(0, s_b, g_b, stats, other)
    home_b = lax.ppermute(back_b, AXES, [(d, s) for s, d in b_moves])
    back_a, own_a, ds_a = grads(1, s_a, g_a, stats, other)
    home_a = lax.ppermute(back_a, AXES, [(d, s) for s, d in a_moves])
    dq_mine, dq_mate = pl.pallas_call(
        functools.partial(query_kernel, rows),
        in_specs=[in_vmem] * 5,
        out_specs=[in_vmem] * 2,
        out_shape=[shape((rows, q_width), F32), shape((rows, q_width), BF16)],
        compiler_params=grant,
        cost_estimate=cost(1 << 28),
    )(full, b, a, ds_b, ds_a)
    dq_other = swap(dq_mate, devices)
    d_queries = (dq_mine + dq_other.astype(F32)).astype(BF16)

    arrived = home_a.astype(F32) + home_b.astype(F32) + own_a + own_b
    mine_in = jnp.where(odd, arrived[:, rows:], arrived[:, :rows])
    mate_in = jnp.where(odd, arrived[:, :rows], arrived[:, rows:])
    from_mate = swap(mate_in.astype(BF16), devices)
    total = (mine_in + from_mate.astype(F32)).astype(BF16)
    return d_queries, total[0], total[1]


def solution(mesh):
    spec = P(AXES, None)
    return jax.shard_map(
        local_grads,
        mesh=mesh,
        in_specs=(spec, spec, spec, spec, P()),
        out_specs=(spec, spec, spec),
        check_vma=False,
    )
```

time: 31.4 us -> 27.9 us (0.89)
  the two profiles are of different devices: /device:TPU:0 before, /device:TPU:23 now
where the time goes in v4:
time: 27.9 us; the launch traced here: 27.6 us
  waiting for transfers between devices  9.29 us (33%)
  starting transfers between devices  7.32 us (26%)
  Pallas kernels  5.44 us (19%)
  local copies, waits for them, and re-layouts  3.18 us (11%)
  other arithmetic  1.65 us (6%)
  between operations  0.72 us (3%)
    ppermute x1, waiting for transfers between devices, local_grads(): home_b = lax.ppermute(back_b, AXES, [(d, s) for s, d in b_moves])  4.5 us
    ppermute x7, starting transfers between devices, swap(): return lax.ppermute(value, AXES, [(d, d ^ 1) for d in range(devices)])  3.84 us
    unnamed x6, local copies, waits for them, and re-layouts  2.55 us
    ppermute x1, waiting for transfers between devices, local_grads(): home_a = lax.ppermute(back_a, AXES, [(d, s) for s, d in a_moves])  2.32 us
    pallas_call x2, Pallas kernels, scores(): pl.pallas_call(functools.partial(score_kernel, rows, block), in_specs=[in...  2.02 us
    pallas_call x2, Pallas kernels, grads(): pl.pallas_call(functools.partial(grads_kernel, rows, block), in_specs=[in...  1.92 us
    ppermute x1, starting transfers between devices, local_grads(): home_a = lax.ppermute(back_a, AXES, [(d, s) for s, d in a_moves])  1.76 us
    ppermute x7, waiting for transfers between devices, swap(): return lax.ppermute(value, AXES, [(d, d ^ 1) for d in range(devices)])  1.68 us
  transfers between devices with their start and end apart: 11, of which 7 were waited for; matrix products, arithmetic and copies ran while one was open for 5% of the time, Pallas kernels for 13%

profile of v4, /device:TPU:23, one launch (start us, length us, event | category | flops | bytes accessed | tf_op | source)
XLA Modules:
  0.0 27.6 jit_solution(12991732978258566557)
XLA Ops:
  0.6 0.7 %collective-permute-start = (bf16[128,128]{1,0:T(8,128)(2,1)}, bf16[128,128]{1,0:T(8,128)(2,1)S(1)}, u32[]{:S(2)}, u32[]{:S(2)}) collective-permute-start(bf16[128,128]{1,0:T(8,128)(2,1)} %param.6), channel_id=1, source_target_pairs={{0,1},{1,0},{2,3},{3,2},{4,5},{5,4},{6,7},{7,6},{8,9},{9,8},{10,11... | collective-permute-start | bytes 98312 | tf_op jit(solution)/shard_map/ppermute | solution.py:48
  1.4 0.4 %collective-permute-start.4 = (bf16[128,1024]{1,0:T(8,128)(2,1)}, bf16[128,1024]{1,0:T(8,128)(2,1)S(1)}, u32[]{:S(2)}, u32[]{:S(2)}) collective-permute-start(bf16[128,1024]{1,0:T(8,128)(2,1)} %q_hbm.1), channel_id=1, source_target_pairs={{0,1},{1,0},{2,3},{3,2},{4,5},{5,4},{6,7},{7,6},{8,9},{9,8},{10,11... | collective-permute-start | bytes 786440 | tf_op jit(solution)/shard_map/ppermute | solution.py:48
  2.0 0.8 %pad_maximum_fusion.2 = bf16[2,128,128]{2,1,0:T(8,128)(2,1)S(1)} fusion(bf16[1,128,128]{2,1,0:T(8,128)(2,1)} %bitcast.9, bf16[1,128,128]{2,1,0:T(8,128)(2,1)} %bitcast.8), kind=kLoop, calls=%fused_computation.6 | loop fusion | flops 32768 | bytes 131072 | tf_op jit(solution)/shard_map/stack | solution.py:242
  2.8 1.6 %collective-permute-start.2 = (bf16[2,256,128]{2,1,0:T(8,128)(2,1)S(1)}, bf16[2,256,128]{2,1,0:T(8,128)(2,1)S(1)}, u32[]{:S(2)}, u32[]{:S(2)}) collective-permute-start(bf16[2,256,128]{2,1,0:T(8,128)(2,1)S(1)} %pad_maximum_fusion.refs_6_.full_ref), channel_id=1, source_target_pairs={{0,7},{2,4},{3,6},{4,11},{6,8},{7,10},{8,15},{9,1},{10,12},{11,14}... | collective-permute-start | bytes 393224 | tf_op jit(solution)/shard_map/ppermute | solution.py:247
  4.5 0.9 %copy-done = bf16[128,1024]{1,0:T(8,128)(2,1)S(1)} copy-done((bf16[128,1024]{1,0:T(8,128)(2,1)S(1)}, bf16[128,1024]{1,0:T(8,128)(2,1)}, u32[]{:S(2)}) %copy-start) | copy-done | bytes 262168
  5.4 0.9 %copy-done.1 = bf16[128,1024]{1,0:T(8,128)(2,1)S(1)} copy-done((bf16[128,1024]{1,0:T(8,128)(2,1)S(1)}, bf16[128,1024]{1,0:T(8,128)(2,1)}, u32[]{:S(2)}) %copy-start.1) | copy-done | bytes 262168
  6.4 0.7 %copy-done.2 = s32[11]{0:T(128)S(1)} copy-done((s32[11]{0:T(128)S(1)}, s32[11]{0:T(128)}, u32[]{:S(2)}) %copy-start.2) | copy-done | bytes 68
  7.0 0.9 %shard_map.76 = (bf16[128,1024]{1,0:T(8,128)(2,1)S(1)}, bf16[128,1024]{1,0:T(8,128)(2,1)S(1)}, bf16[2,256,128]{2,1,0:T(8,128)(2,1)S(1)}, bf16[2,2,256,128]{3,2,1,0:T(8,128)(2,1)S(1)}) custom-call(s32[11]{0:T(128)S(1)} %copy-done.2, bf16[128,1024]{1,0:T(8,128)(2,1)S(1)} %copy-done, bf16[128,1024]{1,0:T(8,128)(2,1)S(1)} %copy-done.1), custom_call_target="tpu_custom_call" | custom-call | flops 1048576 | bytes 1048576 | tf_op jit(solution)/shard_map/pallas_call | solution.py:260
  7.9 0.4 %collective-permute-done.2.refs_7_.b_ref = bf16[2,256,128]{2,1,0:T(8,128)(2,1)S(1)} collective-permute-done((bf16[2,256,128]{2,1,0:T(8,128)(2,1)S(1)}, bf16[2,256,128]{2,1,0:T(8,128)(2,1)S(1)}, u32[]{:S(2)}, u32[]{:S(2)}) %collective-permute-start.2) | collective-permute-done | bytes 131104 | tf_op jit(solution)/shard_map/ppermute | solution.py:247
  8.3 1.0 %shard_map.77 = (f32[1,256,2048]{2,1,0:T(8,128)S(1)}, f32[1,256,2048]{2,1,0:T(8,128)S(1)}, f32[3,2048]{1,0:T(4,128)S(1)}) custom-call(bf16[128,1024]{1,0:T(8,128)(2,1)S(1)} %get-tuple-element.21.refs_0_, bf16[128,1024]{1,0:T(8,128)(2,1)S(1)} %get-tuple-element.22.refs_1_, bf16[128,1024]{1,0:T(8,128)(2,1)S(1)} %collective-permute-done.4.refs_2_, ...), custom_call_target="tpu_custom_call" | custom-call | flops 268435456 | bytes 1048576 | tf_op jit(solution)/shard_map/pallas_call | solution.py:283
  9.3 0.4 %collective-permute-done.3.refs_7_.a_ref = bf16[2,256,128]{2,1,0:T(8,128)(2,1)S(1)} collective-permute-done((bf16[2,256,128]{2,1,0:T(8,128)(2,1)S(1)}, bf16[2,256,128]{2,1,0:T(8,128)(2,1)S(1)}, u32[]{:S(2)}, u32[]{:S(2)}) %collective-permute-start.3) | collective-permute-done | bytes 131104 | tf_op jit(solution)/shard_map/ppermute | solution.py:248
  9.7 1.0 %shard_map.78 = (f32[1,256,2048]{2,1,0:T(8,128)S(1)}, f32[1,256,2048]{2,1,0:T(8,128)S(1)}, f32[3,2048]{1,0:T(4,128)S(1)}) custom-call(bf16[128,1024]{1,0:T(8,128)(2,1)S(1)} %get-tuple-element.21.refs_0_, bf16[128,1024]{1,0:T(8,128)(2,1)S(1)} %get-tuple-element.22.refs_1_, bf16[128,1024]{1,0:T(8,128)(2,1)S(1)} %collective-permute-done.4.refs_2_, ...), custom_call_target="tpu_custom_call" | custom-call | flops 268435456 | bytes 1048576 | tf_op jit(solution)/shard_map/pallas_call | solution.py:283
  10.7 1.9 %collective-permute-start.6 = (f32[3,2048]{1,0:T(4,128)S(1)}, f32[3,2048]{1,0:T(4,128)S(1)}, u32[]{:S(2)}, u32[]{:S(2)}) collective-permute-start(f32[3,2048]{1,0:T(4,128)S(1)} %get-tuple-element.28.refs_6_), channel_id=1, source_target_pairs={{0,1},{1,0},{2,3},{3,2},{4,5},{5,4},{6,7},{7,6},{8,9},{9,8},{10,11... | collective-permute-start | bytes 73736 | tf_op jit(solution)/shard_map/ppermute | solution.py:48
  12.6 0.9 %collective-permute-done.6.refs_7_ = f32[3,2048]{1,0:T(4,128)S(1)} collective-permute-done((f32[3,2048]{1,0:T(4,128)S(1)}, f32[3,2048]{1,0:T(4,128)S(1)}, u32[]{:S(2)}, u32[]{:S(2)}) %collective-permute-start.6) | collective-permute-done | bytes 24608 | tf_op jit(solution)/shard_map/ppermute | solution.py:48
  13.5 1.0 %shard_map.80 = (bf16[2,256,128]{2,1,0:T(8,128)(2,1)S(1)}, f32[2,256,128]{2,1,0:T(8,128)S(1)}, bf16[1,256,2048]{2,1,0:T(8,128)(2,1)S(1)}) custom-call(bf16[128,1024]{1,0:T(8,128)(2,1)S(1)} %get-tuple-element.21.refs_0_, bf16[128,1024]{1,0:T(8,128)(2,1)S(1)} %get-tuple-element.22.refs_1_, bf16[128,1024]{1,0:T(8,128)(2,1)S(1)} %collective-permute-done.4.refs_2_, ...), custom_call_target="tpu_custom_call" | custom-call | flops 268435456 | bytes 1048576 | tf_op jit(solution)/shard_map/pallas_call | solution.py:297
  14.4 1.8 %collective-permute-start.8 = (bf16[2,256,128]{2,1,0:T(8,128)(2,1)S(1)}, bf16[2,256,128]{2,1,0:T(8,128)(2,1)S(1)}, u32[]{:S(2)}, u32[]{:S(2)}) collective-permute-start(bf16[2,256,128]{2,1,0:T(8,128)(2,1)S(1)} %get-tuple-element.35), channel_id=1, source_target_pairs={{2,0},{4,1},{9,2},{6,4},{8,5},{13,6},{10,8},{12,9},{17,10},{3,11},... | collective-permute-start | bytes 393224 | tf_op jit(solution)/shard_map/ppermute | solution.py:317
  16.2 1.0 %shard_map.79 = (bf16[2,256,128]{2,1,0:T(8,128)(2,1)S(1)}, f32[2,256,128]{2,1,0:T(8,128)S(1)}, bf16[1,256,2048]{2,1,0:T(8,128)(2,1)S(1)}) custom-call(bf16[128,1024]{1,0:T(8,128)(2,1)S(1)} %get-tuple-element.21.refs_0_, bf16[128,1024]{1,0:T(8,128)(2,1)S(1)} %get-tuple-element.22.refs_1_, bf16[128,1024]{1,0:T(8,128)(2,1)S(1)} %collective-permute-done.4.refs_2_, ...), custom_call_target="tpu_custom_call" | custom-call | flops 268435456 | bytes 1048576 | tf_op jit(solution)/shard_map/pallas_call | solution.py:297
  17.2 2.3 %collective-permute-done.8 = bf16[2,256,128]{2,1,0:T(8,128)(2,1)S(1)} collective-permute-done((bf16[2,256,128]{2,1,0:T(8,128)(2,1)S(1)}, bf16[2,256,128]{2,1,0:T(8,128)(2,1)S(1)}, u32[]{:S(2)}, u32[]{:S(2)}) %collective-permute-start.8) | collective-permute-done | bytes 131104 | tf_op jit(solution)/shard_map/ppermute | solution.py:317
  19.6 4.5 %collective-permute-done.9 = bf16[2,256,128]{2,1,0:T(8,128)(2,1)S(1)} collective-permute-done((bf16[2,256,128]{2,1,0:T(8,128)(2,1)S(1)}, bf16[2,256,128]{2,1,0:T(8,128)(2,1)S(1)}, u32[]{:S(2)}, u32[]{:S(2)}) %collective-permute-start.9) | collective-permute-done | bytes 131104 | tf_op jit(solution)/shard_map/ppermute | solution.py:315
  24.1 0.5 %collective-permute-start.10 = (bf16[2,128,128]{2,1,0:T(8,128)(2,1)S(1)}, bf16[2,128,128]{2,1,0:T(8,128)(2,1)S(1)}, u32[]{:S(2)}, u32[]{:S(2)}) collective-permute-start(bf16[2,128,128]{2,1,0:T(8,128)(2,1)S(1)} %select_convert_fusion), channel_id=1, source_target_pairs={{0,1},{1,0},{2,3},{3,2},{4,5},{5,4},{6,7},{7,6},{8,9},{9,8},{10,11... | collective-permute-start | bytes 196616 | tf_op jit(solution)/shard_map/ppermute | solution.py:48
  24.6 0.6 %shard_map.81 = (f32[128,1024]{1,0:T(8,128)S(1)}, bf16[128,1024]{1,0:T(8,128)(2,1)S(1)}) custom-call(bf16[2,256,128]{2,1,0:T(8,128)(2,1)S(1)} %pad_maximum_fusion.refs_6_.full_ref, bf16[2,256,128]{2,1,0:T(8,128)(2,1)S(1)} %collective-permute-done.2.refs_7_.b_ref, bf16[2,256,128]{2,1,0:T(8,128)(2,1)S(1)} %collective-permute-done.3.refs_7_.a_ref, ...), custom_call_target="tpu_custom_call" | custom-call | flops 268435456 | bytes 1048576 | tf_op jit(solution)/shard_map/pallas_call | solution.py:318
  25.5 0.6 %slice_bitcast_fusion = (bf16[128,128]{1,0:T(8,128)(2,1)}, bf16[128,128]{1,0:T(8,128)(2,1)}) fusion(bf16[2,128,128]{2,1,0:T(8,128)(2,1)S(1)} %add_convert_fusion.1), kind=kLoop, calls=%fused_computation.9 | loop fusion | bytes 131072 | tf_op jit(solution)/shard_map/squeeze | solution.py:334
  26.2 0.7 %collective-permute-done.7 = bf16[128,1024]{1,0:T(8,128)(2,1)S(1)} collective-permute-done((bf16[128,1024]{1,0:T(8,128)(2,1)S(1)}, bf16[128,1024]{1,0:T(8,128)(2,1)S(1)}, u32[]{:S(2)}, u32[]{:S(2)}) %collective-permute-start.7) | collective-permute-done | bytes 262176 | tf_op jit(solution)/shard_map/ppermute | solution.py:48
  26.8 0.8 %add_convert_fusion = bf16[128,1024]{1,0:T(8,128)(2,1)} fusion(f32[128,1024]{1,0:T(8,128)S(1)} %get-tuple-element.33, bf16[128,1024]{1,0:T(8,128)(2,1)S(1)} %collective-permute-done.7), kind=kLoop, calls=%fused_computation | loop fusion | flops 393216 | bytes 1048576 | tf_op jit(solution)/shard_map/convert_element_type | solution.py:327
  (18 shorter events, 0.7 us)
Async XLA Ops:
  0.6 2.1 %collective-permute-start = (bf16[128,128]{1,0:T(8,128)(2,1)}, bf16[128,128]{1,0:T(8,128)(2,1)S(1)}, u32[]{:S(2)}, u32[]{:S(2)}) collective-permute-start(bf16[128,128]{1,0:T(8,128)(2,1)} %param.6), channel_id=1, source_target_pairs={{0,1},{1,0},{2,3},{3,2},{4,5},{5,4},{6,7},{7,6},{8,9},{9,8},{10,11... | collective-permute-start | bytes 98312 | tf_op jit(solution)/shard_map/ppermute | solution.py:48
  1.4 1.4 %collective-permute-start.1 = (bf16[128,128]{1,0:T(8,128)(2,1)}, bf16[128,128]{1,0:T(8,128)(2,1)S(1)}, u32[]{:S(2)}, u32[]{:S(2)}) collective-permute-start(bf16[128,128]{1,0:T(8,128)(2,1)} %param.7), channel_id=1, source_target_pairs={{0,1},{1,0},{2,3},{3,2},{4,5},{5,4},{6,7},{7,6},{8,9},{9,8},{10,11... | collective-permute-start | bytes 98312 | tf_op jit(solution)/shard_map/ppermute | solution.py:48
  1.4 6.8 %collective-permute-start.4 = (bf16[128,1024]{1,0:T(8,128)(2,1)}, bf16[128,1024]{1,0:T(8,128)(2,1)S(1)}, u32[]{:S(2)}, u32[]{:S(2)}) collective-permute-start(bf16[128,1024]{1,0:T(8,128)(2,1)} %q_hbm.1), channel_id=1, source_target_pairs={{0,1},{1,0},{2,3},{3,2},{4,5},{5,4},{6,7},{7,6},{8,9},{9,8},{10,11... | collective-permute-start | bytes 786440 | tf_op jit(solution)/shard_map/ppermute | solution.py:48
  1.9 6.4 %collective-permute-start.5 = (bf16[128,1024]{1,0:T(8,128)(2,1)}, bf16[128,1024]{1,0:T(8,128)(2,1)S(1)}, u32[]{:S(2)}, u32[]{:S(2)}) collective-permute-start(bf16[128,1024]{1,0:T(8,128)(2,1)} %g_hbm.1), channel_id=1, source_target_pairs={{0,1},{1,0},{2,3},{3,2},{4,5},{5,4},{6,7},{7,6},{8,9},{9,8},{10,11... | collective-permute-start | bytes 786440 | tf_op jit(solution)/shard_map/ppermute | solution.py:48
  2.8 5.5 %collective-permute-start.2 = (bf16[2,256,128]{2,1,0:T(8,128)(2,1)S(1)}, bf16[2,256,128]{2,1,0:T(8,128)(2,1)S(1)}, u32[]{:S(2)}, u32[]{:S(2)}) collective-permute-start(bf16[2,256,128]{2,1,0:T(8,128)(2,1)S(1)} %pad_maximum_fusion.refs_6_.full_ref), channel_id=1, source_target_pairs={{0,7},{2,4},{3,6},{4,11},{6,8},{7,10},{8,15},{9,1},{10,12},{11,14}... | collective-permute-start | bytes 393224 | tf_op jit(solution)/shard_map/ppermute | solution.py:247
  4.4 5.3 %collective-permute-start.3 = (bf16[2,256,128]{2,1,0:T(8,128)(2,1)S(1)}, bf16[2,256,128]{2,1,0:T(8,128)(2,1)S(1)}, u32[]{:S(2)}, u32[]{:S(2)}) collective-permute-start(bf16[2,256,128]{2,1,0:T(8,128)(2,1)S(1)} %pad_maximum_fusion.refs_6_.full_ref), channel_id=1, source_target_pairs={{0,2},{1,4},{2,9},{4,6},{5,8},{6,13},{8,10},{9,12},{10,17},{11,3},... | collective-permute-start | bytes 393224 | tf_op jit(solution)/shard_map/ppermute | solution.py:248
  4.5 0.9 %copy-start = (bf16[128,1024]{1,0:T(8,128)(2,1)S(1)}, bf16[128,1024]{1,0:T(8,128)(2,1)}, u32[]{:S(2)}) copy-start(bf16[128,1024]{1,0:T(8,128)(2,1)} %q_hbm.1) | copy-start | bytes 786436
  5.4 0.9 %copy-start.1 = (bf16[128,1024]{1,0:T(8,128)(2,1)S(1)}, bf16[128,1024]{1,0:T(8,128)(2,1)}, u32[]{:S(2)}) copy-start(bf16[128,1024]{1,0:T(8,128)(2,1)} %g_hbm.1) | copy-start | bytes 786436
  6.4 0.7 %copy-start.2 = (s32[11]{0:T(128)S(1)}, s32[11]{0:T(128)}, u32[]{:S(2)}) copy-start(s32[11]{0:T(128)} %lens_hbm.1) | copy-start | bytes 136
  10.7 2.7 %collective-permute-start.6 = (f32[3,2048]{1,0:T(4,128)S(1)}, f32[3,2048]{1,0:T(4,128)S(1)}, u32[]{:S(2)}, u32[]{:S(2)}) collective-permute-start(f32[3,2048]{1,0:T(4,128)S(1)} %get-tuple-element.28.refs_6_), channel_id=1, source_target_pairs={{0,1},{1,0},{2,3},{3,2},{4,5},{5,4},{6,7},{7,6},{8,9},{9,8},{10,11... | collective-permute-start | bytes 73736 | tf_op jit(solution)/shard_map/ppermute | solution.py:48
  14.4 5.1 %collective-permute-start.8 = (bf16[2,256,128]{2,1,0:T(8,128)(2,1)S(1)}, bf16[2,256,128]{2,1,0:T(8,128)(2,1)S(1)}, u32[]{:S(2)}, u32[]{:S(2)}) collective-permute-start(bf16[2,256,128]{2,1,0:T(8,128)(2,1)S(1)} %get-tuple-element.35), channel_id=1, source_target_pairs={{2,0},{4,1},{9,2},{6,4},{8,5},{13,6},{10,8},{12,9},{17,10},{3,11},... | collective-permute-start | bytes 393224 | tf_op jit(solution)/shard_map/ppermute | solution.py:317
  17.2 6.9 %collective-permute-start.9 = (bf16[2,256,128]{2,1,0:T(8,128)(2,1)S(1)}, bf16[2,256,128]{2,1,0:T(8,128)(2,1)S(1)}, u32[]{:S(2)}, u32[]{:S(2)}) collective-permute-start(bf16[2,256,128]{2,1,0:T(8,128)(2,1)S(1)} %get-tuple-element.36), channel_id=1, source_target_pairs={{7,0},{4,2},{6,3},{11,4},{8,6},{10,7},{15,8},{1,9},{12,10},{14,11}... | collective-permute-start | bytes 393224 | tf_op jit(solution)/shard_map/ppermute | solution.py:315
  24.1 1.4 %collective-permute-start.10 = (bf16[2,128,128]{2,1,0:T(8,128)(2,1)S(1)}, bf16[2,128,128]{2,1,0:T(8,128)(2,1)S(1)}, u32[]{:S(2)}, u32[]{:S(2)}) collective-permute-start(bf16[2,128,128]{2,1,0:T(8,128)(2,1)S(1)} %select_convert_fusion), channel_id=1, source_target_pairs={{0,1},{1,0},{2,3},{3,2},{4,5},{5,4},{6,7},{7,6},{8,9},{9,8},{10,11... | collective-permute-start | bytes 196616 | tf_op jit(solution)/shard_map/ppermute | solution.py:48
  25.2 1.6 %collective-permute-start.7 = (bf16[128,1024]{1,0:T(8,128)(2,1)S(1)}, bf16[128,1024]{1,0:T(8,128)(2,1)S(1)}, u32[]{:S(2)}, u32[]{:S(2)}) collective-permute-start(bf16[128,1024]{1,0:T(8,128)(2,1)S(1)} %get-tuple-element.34), channel_id=1, source_target_pairs={{0,1},{1,0},{2,3},{3,2},{4,5},{5,4},{6,7},{7,6},{8,9},{9,8},{10,11... | collective-permute-start | bytes 786440 | tf_op jit(solution)/shard_map/ppermute | solution.py:48

commit v5 on v4

v5 whole, which is shorter than its diff:
```python
import functools
import itertools
import math

import jax
import jax.numpy as jnp
from jax import lax
from jax.experimental import pallas as pl
from jax.experimental.pallas import tpu as pltpu
from jax.sharding import PartitionSpec as P

HEAD_SIZE = 128
GROUP = 8
AXES = ("dp", "seq")
NEG = -1e30
FAR = 1 << 30
NEAR_STEPS = (1, 2)
FAR_STEP = 3
SCALE = 1.0 / math.sqrt(HEAD_SIZE)
SCALE2 = SCALE * math.log2(math.e)
F32 = jnp.float32
BF16 = jnp.bfloat16


def ring(devices, steps):
    moves = [(d, d + 2 * steps[d % 2]) for d in range(devices)]
    inside = [(s, t) for s, t in moves if t < devices]
    sources = [s for s, t in moves if t >= devices]
    targets = sorted(set(range(devices)) - {t for _, t in inside})

    def turns(s, t):
        return bin((s // 2 ^ t // 2) & 3).count("1")

    def cost(order):
        found = [turns(s, t) for s, t in zip(sources, order)]
        return max(found), sum(found)

    return inside + list(zip(sources, min(itertools.permutations(targets), key=cost)))


def swap(value, devices):
    return lax.ppermute(value, AXES, [(d, d ^ 1) for d in range(devices)])


def dot_nt(a, b):
    return lax.dot_general(a, b, (((1,), (1,)), ((), ())), preferred_element_type=F32)


def dot_nn(a, b):
    return lax.dot_general(a, b, (((1,), (0,)), ((), ())), preferred_element_type=F32)


def where_am_i():
    me = lax.axis_index("dp") * lax.axis_size("seq") + lax.axis_index("seq")
    return me, lax.rem(me, 2) == 1


def prepare_kernel(
    rows, lens_hbm, q_hbm, g_hbm, q_ref, g_ref, member_ref, late_ref, lens_ref, lens_sem, q_sem, g_sem
):
    t = rows
    fetch = pltpu.make_async_copy(lens_hbm, lens_ref, lens_sem)
    fetch.start()
    stacks = []
    for h in range(q_hbm.shape[1] // HEAD_SIZE):
        span, lanes = slice(h * t, (h + 1) * t), slice(h * HEAD_SIZE, (h + 1) * HEAD_SIZE)
        for source, target, sem in ((q_hbm, q_ref, q_sem), (g_hbm, g_ref, g_sem)):
            stacks.append(pltpu.make_async_copy(source.at[:, lanes], target.at[span, :], sem.at[h]))
    for stack in stacks:
        stack.start()
    me, odd = where_am_i()
    lane = lax.broadcasted_iota(jnp.int32, (1, HEAD_SIZE), 1)
    down = lax.broadcasted_iota(jnp.int32, (t, HEAD_SIZE), 0)
    near = (me // 2 - jnp.where(odd, 2, 1)) * 2 * t
    starts_of_parts = (((me - 2 * FAR_STEP) * t, me * t), (near, near + t))
    far = jnp.full((1, HEAD_SIZE), FAR, jnp.int32)
    zero = jnp.int32(0)
    fetch.wait()
    for side in (0, 1):
        first = (me if side == 0 else jnp.where(odd, me - 1, me + 1)) * t

        def next_doc(j, carry, first=first):
            end, count, starts, stops = carry
            begin, end = end, end + lens_ref[j]
            live = end > first
            here = (lane == count) & live
            starts, stops = jnp.where(here, begin, starts), jnp.where(here, end, stops)
            return end, count + live.astype(jnp.int32), starts, stops

        _, _, starts, stops = lax.fori_loop(0, lens_ref.shape[0], next_doc, (zero, zero, far, far))
        q_pos = first + down
        member = jnp.where((q_pos >= starts) & (q_pos < stops), 1.0, 0.0).astype(BF16)
        member_ref[side, :t, :] = member
        member_ref[side, t:, :] = member
        for block in (0, 1):
            for part in (0, 1):
                k_pos = starts_of_parts[block][part] + down
                blocked = (k_pos < starts) | (k_pos >= first + t)
                late_ref[block, side, part * t : (part + 1) * t, :] = jnp.where(
                    blocked, NEG, 0.0
                ).astype(BF16)
    for stack in stacks:
        stack.wait()


def stacked(ref, rows, first_head, count):
    return ref[first_head * rows : (first_head + count) * rows, :]


def block_rows(block, kind, mine_ref, got_ref, lanes):
    if block:
        return got_ref[kind, :, lanes]
    return jnp.concatenate([got_ref[kind, :, lanes], mine_ref[kind, :, lanes]], axis=0)


def combine(one, two):
    high = jnp.maximum(one[0], two[0])
    keep_one, keep_two = jnp.exp2(one[0] - high), jnp.exp2(two[0] - high)
    return high, one[1] * keep_one + two[1] * keep_two, one[2] * keep_one + two[2] * keep_two


def score_kernel(rows, block, *refs):
    qs, gs = (refs[0], refs[2]), (refs[1], refs[3])
    member_ref, late_ref, mine_ref, got_ref = refs[4:8]
    before_ref = refs[8] if block else None
    s_ref, g_ref, stats_ref = refs[-3:]
    t = rows
    causal = lax.broadcasted_iota(jnp.int32, (t, t), 0) <= lax.broadcasted_iota(
        jnp.int32, (t, t), 1
    )
    causal = jnp.concatenate([causal, causal], axis=1)

    def fold(x, op):
        return op(x.reshape(-1, 8, 2 * t), axis=0)

    for head in range(mine_ref.shape[2] // HEAD_SIZE):
        lanes = slice(head * HEAD_SIZE, (head + 1) * HEAD_SIZE)
        key, value = (block_rows(block, kind, mine_ref, got_ref, lanes) for kind in (0, 1))
        for side in (0, 1):
            key_late = jnp.concatenate([key, late_ref[block, side]], axis=1)
            for pair in range(GROUP // 2):
                cols = slice((side * GROUP + pair * 2) * t, (side * GROUP + pair * 2 + 2) * t)
                q_rows = stacked(qs[side], t, head * GROUP + pair * 2, 2)
                q_rows = jnp.concatenate([q_rows, member_ref[side]], axis=1)
                s = dot_nt(key_late, q_rows) * SCALE2
                g = dot_nt(value, stacked(gs[side], t, head * GROUP + pair * 2, 2))
                parts = [s[:t], s[t:]]
                if block == 0 and side == 0:
                    parts[1] = jnp.where(causal, parts[1], NEG)
                s_ref[head, :t, cols] = parts[0]
                s_ref[head, t:, cols] = parts[1]
                g_ref[head, :, cols] = g
                top = jnp.maximum(fold(parts[0], jnp.max), fold(parts[1], jnp.max))
                top = jnp.max(top, axis=0, keepdims=True)
                total = jnp.zeros((8, 2 * t), F32)
                weighted = jnp.zeros((8, 2 * t), F32)
                for part in (0, 1):
                    e = jnp.exp2(parts[part] - top)
                    total += fold(e, jnp.sum)
                    weighted += fold(e * g[part * t : (part + 1) * t], jnp.sum)
                turn = side * (GROUP // 2) + pair
                for i, found in enumerate((total, weighted)):
                    stats_ref[3 * head + 1 + i, turn : turn + 1, :] = jnp.sum(
                        found, axis=0, keepdims=True
                    )
                stats_ref[3 * head, turn : turn + 1, :] = top
        if block:
            found = combine(*([ref[3 * head + i] for i in range(3)] for ref in (stats_ref, before_ref)))
            for i in range(3):
                stats_ref[3 * head + i] = found[i]


def grads_kernel(rows, block, *refs):
    qs, gs = (refs[0], refs[2]), (refs[1], refs[3])
    s_ref, g_ref, stats_ref, other_ref, ds_ref, home_ref = refs[4:10]
    t = rows
    for head in range(s_ref.shape[0]):
        lanes = slice(head * HEAD_SIZE, (head + 1) * HEAD_SIZE)
        mine = [stats_ref[3 * head + i] for i in range(3)]
        half = GROUP // 2
        mates = [other_ref[3 * head + i] for i in range(3)]
        mates = [jnp.concatenate([x[half:], x[:half]], axis=0) for x in mates]
        high, total, weighted = combine(mine, mates)
        levels, deltas = high + jnp.log2(total), weighted / total
        grads = [None, None]
        for side in (0, 1):
            for pair in range(half):
                turn = side * half + pair
                cols = slice(turn * 2 * t, (turn + 1) * 2 * t)
                level, delta = levels[turn : turn + 1], deltas[turn : turn + 1]
                p = jnp.exp2(s_ref[head, :, cols] - level)
                ds = (p * (g_ref[head, :, cols] - delta)).astype(BF16)
                ds_ref[head, :, cols] = ds
                at = head * GROUP + pair * 2
                dk = dot_nn(ds, stacked(qs[side], t, at, 2))
                dv = dot_nn(p.astype(BF16), stacked(gs[side], t, at, 2))
                grads = [dk, dv] if turn == 0 else [grads[0] + dk, grads[1] + dv]
        grads[0] = grads[0] * SCALE
        for kind, grad in enumerate(grads):
            if block:
                home_ref[kind, :, lanes] = grad.astype(BF16)
            else:
                home_ref[kind, :, lanes] = grad[:t].astype(BF16)
                refs[10][kind, :, lanes] = grad[t:]


def query_kernel(rows, kv_ref, b_ref, a_ref, dsb_ref, dsa_ref, mine_ref, mate_ref):
    t = rows
    for head in range(dsb_ref.shape[0]):
        lanes = slice(head * HEAD_SIZE, (head + 1) * HEAD_SIZE)
        key_b, key_a = (
            block_rows(block, 0, kv_ref, got, lanes).T for block, got in ((0, b_ref), (1, a_ref))
        )
        for side, out_ref in ((1, mate_ref), (0, mine_ref)):
            cols = slice(side * GROUP * t, (side + 1) * GROUP * t)
            dqt = dot_nn(key_b, dsb_ref[head, :, cols]) + dot_nn(key_a, dsa_ref[head, :, cols])
            dqt = dqt * SCALE
            for h in range(GROUP):
                at = (head * GROUP + h) * HEAD_SIZE
                out_ref[:, at : at + HEAD_SIZE] = dqt[:, h * t : (h + 1) * t].T.astype(out_ref.dtype)


def local_grads(queries, keys, values, d_out, doc_lengths):
    rows, q_width = queries.shape
    kv_width = keys.shape[1]
    kv_heads = kv_width // HEAD_SIZE
    devices = lax.axis_size("dp") * lax.axis_size("seq")
    _, odd = where_am_i()
    a_moves, b_moves = ring(devices, NEAR_STEPS), ring(devices, (FAR_STEP, FAR_STEP))

    mine = lax.optimization_barrier(jnp.stack([keys, values]))
    mate = swap(mine, devices)
    b = lax.ppermute(mine, AXES, b_moves)
    full = jnp.concatenate([jnp.where(odd, mate, mine), jnp.where(odd, mine, mate)], axis=1)
    a = lax.ppermute(full, AXES, a_moves)

    shape = jax.ShapeDtypeStruct
    in_vmem = pl.BlockSpec(memory_space=pltpu.VMEM)
    grant = pltpu.CompilerParams(vmem_limit_bytes=(12 + 10 * kv_heads) << 20)

    def cost(flops):
        return pl.CostEstimate(flops=flops, bytes_accessed=1 << 20, transcendentals=0)

    width = 2 * GROUP * rows
    mine_q, mine_g, member, late = pl.pallas_call(
        functools.partial(prepare_kernel, rows),
        in_specs=[pl.BlockSpec(memory_space=pltpu.HBM)] * 3,
        out_specs=[in_vmem] * 4,
        out_shape=[
            shape((q_width // HEAD_SIZE * rows, HEAD_SIZE), BF16),
            shape((q_width // HEAD_SIZE * rows, HEAD_SIZE), BF16),
            shape((2, 2 * rows, HEAD_SIZE), BF16),
            shape((2, 2, 2 * rows, HEAD_SIZE), BF16),
        ],
        scratch_shapes=[
            pltpu.SMEM(doc_lengths.shape, jnp.int32),
            pltpu.SemaphoreType.DMA,
            *[pltpu.SemaphoreType.DMA((q_width // HEAD_SIZE,))] * 2,
        ],
        compiler_params=grant,
        cost_estimate=cost(1 << 20),
    )(*(pltpu.with_memory_space_constraint(x, pltpu.HBM) for x in (doc_lengths, queries, d_out)))

    mate_q = swap(mine_q, devices)
    mate_g = swap(mine_g, devices)

    rows_of = (mine_q, mine_g, mate_q, mate_g)

    def scores(block, got, *before):
        return pl.pallas_call(
            functools.partial(score_kernel, rows, block),
            in_specs=[in_vmem] * (8 + len(before)),
            out_specs=[in_vmem] * 3,
            out_shape=[
                shape((kv_heads, 2 * rows, width), F32),
                shape((kv_heads, 2 * rows, width), F32),
                shape((3 * kv_heads, GROUP, 2 * rows), F32),
            ],
            compiler_params=grant,
            cost_estimate=cost(1 << 28),
        )(*rows_of, member, late, mine, got, *before)

    def grads(block, s, g, stats, other):
        out_shape = [shape((kv_heads, 2 * rows, width), BF16)]
        if block:
            out_shape += [shape((2, 2 * rows, kv_width), BF16)]
        else:
            out_shape += [shape((2, rows, kv_width), BF16), shape((2, rows, kv_width), F32)]
        return pl.pallas_call(
            functools.partial(grads_kernel, rows, block),
            in_specs=[in_vmem] * 8,
            out_specs=[in_vmem] * len(out_shape),
            out_shape=out_shape,
            compiler_params=grant,
            cost_estimate=cost(1 << 28),
        )(*rows_of, s, g, stats, other)

    s_b, g_b, stats_b = scores(0, b)
    s_a, g_a, stats = scores(1, a, stats_b)
    other = swap(stats, devices)
    ds_a, back_a = grads(1, s_a, g_a, stats, other)
    home_a = lax.ppermute(back_a, AXES, [(d, s) for s, d in a_moves])
    ds_b, back_b, own = grads(0, s_b, g_b, stats, other)
    home_b = lax.ppermute(back_b, AXES, [(d, s) for s, d in b_moves])
    dq_mine, dq_mate = pl.pallas_call(
        functools.partial(query_kernel, rows),
        in_specs=[in_vmem] * 5,
        out_specs=[in_vmem] * 2,
        out_shape=[shape((rows, q_width), F32), shape((rows, q_width), BF16)],
        compiler_params=grant,
        cost_estimate=cost(1 << 28),
    )(mine, b, a, ds_b, ds_a)
    dq_other = swap(dq_mate, devices)
    d_queries = (dq_mine + dq_other.astype(F32)).astype(BF16)

    first, second = home_a[:, :rows].astype(F32), home_a[:, rows:].astype(F32)
    from_mate = swap(jnp.where(odd, first, second).astype(BF16), devices)
    total = own + home_b.astype(F32) + jnp.where(odd, second, first) + from_mate.astype(F32)
    total = total.astype(BF16)
    return d_queries, total[0], total[1]


def solution(mesh):
    spec = P(AXES, None)
    return jax.shard_map(
        local_grads,
        mesh=mesh,
        in_specs=(spec, spec, spec, spec, P()),
        out_specs=(spec, spec, spec),
        check_vma=False,
    )
```

time: 27.9 us -> 29.2 us (1.047)
  the two profiles are of different devices: /device:TPU:23 before, /device:TPU:0 now
where the time goes in v5:
time: 29.2 us; the launch traced here: 29 us
  starting transfers between devices  11.2 us (38%)
  waiting for transfers between devices  9.35 us (32%)
  Pallas kernels  5.42 us (19%)
  other arithmetic  1.65 us (6%)
  between operations  0.72 us (2%)
  local copies, waits for them, and re-layouts  0.63 us (2%)
    ppermute x1, waiting for transfers between devices, local_grads(): b = lax.ppermute(mine, AXES, b_moves)  4.52 us
    ppermute x1, starting transfers between devices, local_grads(): home_a = lax.ppermute(back_a, AXES, [(d, s) for s, d in a_moves])  4.03 us
    ppermute x1, starting transfers between devices, local_grads(): a = lax.ppermute(full, AXES, a_moves)  2.61 us
    ppermute x1, waiting for transfers between devices, local_grads(): home_a = lax.ppermute(back_a, AXES, [(d, s) for s, d in a_moves])  2.52 us
    ppermute x1, starting transfers between devices, local_grads(): b = lax.ppermute(mine, AXES, b_moves)  2.45 us
    ppermute x6, starting transfers between devices, swap(): return lax.ppermute(value, AXES, [(d, d ^ 1) for d in range(devices)])  2.06 us
    pallas_call x2, Pallas kernels, scores(): pl.pallas_call(functools.partial(score_kernel, rows, block), in_specs=[in...  1.88 us
    pallas_call x2, Pallas kernels, grads(): pl.pallas_call(functools.partial(grads_kernel, rows, block), in_specs=[in...  1.64 us
  transfers between devices with their start and end apart: 10, of which 4 were waited for; matrix products, arithmetic and copies ran while one was open for 2% of the time, Pallas kernels for 12%

profile of v5, /device:TPU:0, one launch (start us, length us, event | category | flops | bytes accessed | tf_op | source)
XLA Modules:
  0.0 29.0 jit_solution(11940275645493556565)
XLA Ops:
  0.6 0.8 %pad_maximum_fusion.1.refs_6_.kv_ref = bf16[2,128,128]{2,1,0:T(8,128)(2,1)S(1)} fusion(bf16[1,128,128]{2,1,0:T(8,128)(2,1)} %bitcast.6, bf16[1,128,128]{2,1,0:T(8,128)(2,1)} %bitcast.7), kind=kLoop, calls=%fused_computation.8 | loop fusion | flops 32768 | bytes 131072 | tf_op jit(solution)/shard_map/stack | solution.py:231
  1.4 0.5 %collective-permute-start.1 = (bf16[2,128,128]{2,1,0:T(8,128)(2,1)S(1)}, bf16[2,128,128]{2,1,0:T(8,128)(2,1)S(1)}, u32[]{:S(2)}, u32[]{:S(2)}) collective-permute-start(bf16[2,128,128]{2,1,0:T(8,128)(2,1)S(1)} %pad_maximum_fusion.1.refs_6_.kv_ref), channel_id=1, source_target_pairs={{0,1},{1,0},{2,3},{3,2},{4,5},{5,4},{6,7},{7,6},{8,9},{9,8},{10,11... | collective-permute-start | bytes 196616 | tf_op jit(solution)/shard_map/ppermute | solution.py:42
  2.0 1.3 %shard_map.76 = (bf16[1024,128]{1,0:T(8,128)(2,1)S(1)}, bf16[1024,128]{1,0:T(8,128)(2,1)S(1)}, bf16[2,256,128]{2,1,0:T(8,128)(2,1)S(1)}, bf16[2,2,256,128]{3,2,1,0:T(8,128)(2,1)S(1)}) custom-call(s32[11]{0:T(128)} %lens_hbm.1, bf16[128,1024]{1,0:T(8,128)(2,1)} %q_hbm.1, bf16[128,1024]{1,0:T(8,128)(2,1)} %g_hbm.1), custom_call_target="tpu_custom_call" | custom-call | flops 1048576 | bytes 1048576 | tf_op jit(solution)/shard_map/pallas_call | solution.py:245
  3.2 0.1 collective-permute-start.3
  3.3 0.5 %collective-permute-start.4 = (bf16[1024,128]{1,0:T(8,128)(2,1)S(1)}, bf16[1024,128]{1,0:T(8,128)(2,1)S(1)}, u32[]{:S(2)}, u32[]{:S(2)}) collective-permute-start(bf16[1024,128]{1,0:T(8,128)(2,1)S(1)} %get-tuple-element.21.refs_1_), channel_id=1, source_target_pairs={{0,1},{1,0},{2,3},{3,2},{4,5},{5,4},{6,7},{7,6},{8,9},{9,8},{10,11... | collective-permute-start | bytes 786440 | tf_op jit(solution)/shard_map/ppermute | solution.py:42
  3.9 2.6 %collective-permute-start.2 = (bf16[2,256,128]{2,1,0:T(8,128)(2,1)S(1)}, bf16[2,256,128]{2,1,0:T(8,128)(2,1)S(1)}, u32[]{:S(2)}, u32[]{:S(2)}) collective-permute-start(bf16[2,256,128]{2,1,0:T(8,128)(2,1)S(1)} %pad_maximum_fusion), channel_id=1, source_target_pairs={{0,2},{1,5},{2,4},{3,7},{4,6},{5,9},{6,8},{7,11},{8,10},{9,13},{10... | collective-permute-start | bytes 393224 | tf_op jit(solution)/shard_map/ppermute | solution.py:235
  6.5 2.4 %collective-permute-start = (bf16[2,128,128]{2,1,0:T(8,128)(2,1)S(1)}, bf16[2,128,128]{2,1,0:T(8,128)(2,1)S(1)}, u32[]{:S(2)}, u32[]{:S(2)}) collective-permute-start(bf16[2,128,128]{2,1,0:T(8,128)(2,1)S(1)} %pad_maximum_fusion.1.refs_6_.kv_ref), channel_id=1, source_target_pairs={{0,6},{1,7},{2,8},{3,9},{4,10},{5,11},{6,12},{7,13},{8,14},{9,15},... | collective-permute-start | bytes 196616 | tf_op jit(solution)/shard_map/ppermute | solution.py:233
  8.9 4.5 %collective-permute-done.refs_7_.b_ref = bf16[2,128,128]{2,1,0:T(8,128)(2,1)S(1)} collective-permute-done((bf16[2,128,128]{2,1,0:T(8,128)(2,1)S(1)}, bf16[2,128,128]{2,1,0:T(8,128)(2,1)S(1)}, u32[]{:S(2)}, u32[]{:S(2)}) %collective-permute-start) | collective-permute-done | bytes 65568 | tf_op jit(solution)/shard_map/ppermute | solution.py:233
  13.4 0.9 %shard_map.77 = (f32[1,256,2048]{2,1,0:T(8,128)S(1)}, f32[1,256,2048]{2,1,0:T(8,128)S(1)}, f32[3,8,256]{2,1,0:T(8,128)S(1)}) custom-call(bf16[1024,128]{1,0:T(8,128)(2,1)S(1)} %get-tuple-element.20.refs_0_, bf16[1024,128]{1,0:T(8,128)(2,1)S(1)} %get-tuple-element.21.refs_1_, bf16[1024,128]{1,0:T(8,128)(2,1)S(1)} %collective-permute-done.3.refs_2_, ...), custom_call_target="tpu_custom_call" | custom-call | flops 268435456 | bytes 1048576 | tf_op jit(solution)/shard_map/pallas_call | solution.py:270
  14.4 1.0 %shard_map.78 = (f32[1,256,2048]{2,1,0:T(8,128)S(1)}, f32[1,256,2048]{2,1,0:T(8,128)S(1)}, f32[3,8,256]{2,1,0:T(8,128)S(1)}) custom-call(bf16[1024,128]{1,0:T(8,128)(2,1)S(1)} %get-tuple-element.20.refs_0_, bf16[1024,128]{1,0:T(8,128)(2,1)S(1)} %get-tuple-element.21.refs_1_, bf16[1024,128]{1,0:T(8,128)(2,1)S(1)} %collective-permute-done.3.refs_2_, ...), custom_call_target="tpu_custom_call" | custom-call | flops 268435456 | bytes 1048576 | tf_op jit(solution)/shard_map/pallas_call | solution.py:270
  15.3 0.3 %collective-permute-start.5 = (f32[3,8,256]{2,1,0:T(8,128)S(1)}, f32[3,8,256]{2,1,0:T(8,128)S(1)}, u32[]{:S(2)}, u32[]{:S(2)}) collective-permute-start(f32[3,8,256]{2,1,0:T(8,128)S(1)} %get-tuple-element.27.refs_6_), channel_id=1, source_target_pairs={{0,1},{1,0},{2,3},{3,2},{4,5},{5,4},{6,7},{7,6},{8,9},{9,8},{10,11... | collective-permute-start | bytes 73736 | tf_op jit(solution)/shard_map/ppermute | solution.py:42
  15.7 0.9 %collective-permute-done.5.refs_7_ = f32[3,8,256]{2,1,0:T(8,128)S(1)} collective-permute-done((f32[3,8,256]{2,1,0:T(8,128)S(1)}, f32[3,8,256]{2,1,0:T(8,128)S(1)}, u32[]{:S(2)}, u32[]{:S(2)}) %collective-permute-start.5) | collective-permute-done | bytes 24608 | tf_op jit(solution)/shard_map/ppermute | solution.py:42
  16.6 0.8 %shard_map.80 = (bf16[1,256,2048]{2,1,0:T(8,128)(2,1)S(1)}, bf16[2,256,128]{2,1,0:T(8,128)(2,1)S(1)}) custom-call(bf16[1024,128]{1,0:T(8,128)(2,1)S(1)} %get-tuple-element.20.refs_0_, bf16[1024,128]{1,0:T(8,128)(2,1)S(1)} %get-tuple-element.21.refs_1_, bf16[1024,128]{1,0:T(8,128)(2,1)S(1)} %collective-permute-done.3.refs_2_, ...), custom_call_target="tpu_custom_call" | custom-call | flops 268435456 | bytes 1048576 | tf_op jit(solution)/shard_map/pallas_call | solution.py:289
  17.5 4.0 %collective-permute-start.8 = (bf16[2,256,128]{2,1,0:T(8,128)(2,1)S(1)}, bf16[2,256,128]{2,1,0:T(8,128)(2,1)S(1)}, u32[]{:S(2)}, u32[]{:S(2)}) collective-permute-start(bf16[2,256,128]{2,1,0:T(8,128)(2,1)S(1)} %get-tuple-element.36), channel_id=1, source_target_pairs={{2,0},{5,1},{4,2},{7,3},{6,4},{9,5},{8,6},{11,7},{10,8},{13,9},{12... | collective-permute-start | bytes 393224 | tf_op jit(solution)/shard_map/ppermute | solution.py:302
  21.5 0.8 %shard_map.79 = (bf16[1,256,2048]{2,1,0:T(8,128)(2,1)S(1)}, bf16[2,128,128]{2,1,0:T(8,128)(2,1)S(1)}, f32[2,128,128]{2,1,0:T(8,128)S(1)}) custom-call(bf16[1024,128]{1,0:T(8,128)(2,1)S(1)} %get-tuple-element.20.refs_0_, bf16[1024,128]{1,0:T(8,128)(2,1)S(1)} %get-tuple-element.21.refs_1_, bf16[1024,128]{1,0:T(8,128)(2,1)S(1)} %collective-permute-done.3.refs_2_, ...), custom_call_target="tpu_custom_call" | custom-call | flops 268435456 | bytes 1048576 | tf_op jit(solution)/shard_map/pallas_call | solution.py:289
  22.3 0.1 collective-permute-start.7
  22.4 2.5 %collective-permute-done.8 = bf16[2,256,128]{2,1,0:T(8,128)(2,1)S(1)} collective-permute-done((bf16[2,256,128]{2,1,0:T(8,128)(2,1)S(1)}, bf16[2,256,128]{2,1,0:T(8,128)(2,1)S(1)}, u32[]{:S(2)}, u32[]{:S(2)}) %collective-permute-start.8) | collective-permute-done | bytes 131104 | tf_op jit(solution)/shard_map/ppermute | solution.py:302
  24.9 0.1 collective-permute-start.9
  25.0 0.6 %shard_map.81 = (f32[128,1024]{1,0:T(8,128)S(1)}, bf16[128,1024]{1,0:T(8,128)(2,1)S(1)}) custom-call(bf16[2,128,128]{2,1,0:T(8,128)(2,1)S(1)} %pad_maximum_fusion.1.refs_6_.kv_ref, bf16[2,128,128]{2,1,0:T(8,128)(2,1)S(1)} %collective-permute-done.refs_7_.b_ref, bf16[2,256,128]{2,1,0:T(8,128)(2,1)S(1)} %collective-permute-done.2.refs_7_.a_ref, ...), custom_call_target="tpu_custom_call" | custom-call | flops 268435456 | bytes 1048576 | tf_op jit(solution)/shard_map/pallas_call | solution.py:305
  25.6 0.6 %collective-permute-start.6 = (bf16[128,1024]{1,0:T(8,128)(2,1)S(1)}, bf16[128,1024]{1,0:T(8,128)(2,1)S(1)}, u32[]{:S(2)}, u32[]{:S(2)}) collective-permute-start(bf16[128,1024]{1,0:T(8,128)(2,1)S(1)} %get-tuple-element.33), channel_id=1, source_target_pairs={{0,1},{1,0},{2,3},{3,2},{4,5},{5,4},{6,7},{7,6},{8,9},{9,8},{10,11... | collective-permute-start | bytes 786440 | tf_op jit(solution)/shard_map/ppermute | solution.py:42
  26.2 1.3 %collective-permute-done.7 = bf16[2,128,128]{2,1,0:T(8,128)(2,1)S(1)} collective-permute-done((bf16[2,128,128]{2,1,0:T(8,128)(2,1)S(1)}, bf16[2,128,128]{2,1,0:T(8,128)(2,1)S(1)}, u32[]{:S(2)}, u32[]{:S(2)}) %collective-permute-start.7) | collective-permute-done | bytes 65568 | tf_op jit(solution)/shard_map/ppermute | solution.py:304
  27.6 0.6 %slice_bitcast_fusion = (bf16[128,128]{1,0:T(8,128)(2,1)}, bf16[128,128]{1,0:T(8,128)(2,1)}) fusion(bf16[2,128,128]{2,1,0:T(8,128)(2,1)S(1)} %fusion.2), kind=kLoop, calls=%fused_computation.11 | loop fusion | bytes 131072 | tf_op jit(solution)/shard_map/squeeze | solution.py:320
  28.2 0.0 collective-permute-done.6
  28.2 0.8 %add_convert_fusion = bf16[128,1024]{1,0:T(8,128)(2,1)} fusion(f32[128,1024]{1,0:T(8,128)S(1)} %get-tuple-element.32, bf16[128,1024]{1,0:T(8,128)(2,1)S(1)} %collective-permute-done.6), kind=kLoop, calls=%fused_computation | loop fusion | flops 393216 | bytes 1048576 | tf_op jit(solution)/shard_map/convert_element_type | solution.py:314
  (9 shorter events, 0.1 us)
Async XLA Ops:
  1.4 2.4 %collective-permute-start.1 = (bf16[2,128,128]{2,1,0:T(8,128)(2,1)S(1)}, bf16[2,128,128]{2,1,0:T(8,128)(2,1)S(1)}, u32[]{:S(2)}, u32[]{:S(2)}) collective-permute-start(bf16[2,128,128]{2,1,0:T(8,128)(2,1)S(1)} %pad_maximum_fusion.1.refs_6_.kv_ref), channel_id=1, source_target_pairs={{0,1},{1,0},{2,3},{3,2},{4,5},{5,4},{6,7},{7,6},{8,9},{9,8},{10,11... | collective-permute-start | bytes 196616 | tf_op jit(solution)/shard_map/ppermute | solution.py:42
  3.2 10.2 %collective-permute-start.3 = (bf16[1024,128]{1,0:T(8,128)(2,1)S(1)}, bf16[1024,128]{1,0:T(8,128)(2,1)S(1)}, u32[]{:S(2)}, u32[]{:S(2)}) collective-permute-start(bf16[1024,128]{1,0:T(8,128)(2,1)S(1)} %get-tuple-element.20.refs_0_), channel_id=1, source_target_pairs={{0,1},{1,0},{2,3},{3,2},{4,5},{5,4},{6,7},{7,6},{8,9},{9,8},{10,11... | collective-permute-start | bytes 786440 | tf_op jit(solution)/shard_map/ppermute | solution.py:42
  3.3 10.1 %collective-permute-start.4 = (bf16[1024,128]{1,0:T(8,128)(2,1)S(1)}, bf16[1024,128]{1,0:T(8,128)(2,1)S(1)}, u32[]{:S(2)}, u32[]{:S(2)}) collective-permute-start(bf16[1024,128]{1,0:T(8,128)(2,1)S(1)} %get-tuple-element.21.refs_1_), channel_id=1, source_target_pairs={{0,1},{1,0},{2,3},{3,2},{4,5},{5,4},{6,7},{7,6},{8,9},{9,8},{10,11... | collective-permute-start | bytes 786440 | tf_op jit(solution)/shard_map/ppermute | solution.py:42
  3.9 10.5 %collective-permute-start.2 = (bf16[2,256,128]{2,1,0:T(8,128)(2,1)S(1)}, bf16[2,256,128]{2,1,0:T(8,128)(2,1)S(1)}, u32[]{:S(2)}, u32[]{:S(2)}) collective-permute-start(bf16[2,256,128]{2,1,0:T(8,128)(2,1)S(1)} %pad_maximum_fusion), channel_id=1, source_target_pairs={{0,2},{1,5},{2,4},{3,7},{4,6},{5,9},{6,8},{7,11},{8,10},{9,13},{10... | collective-permute-start | bytes 393224 | tf_op jit(solution)/shard_map/ppermute | solution.py:235
  6.5 7.0 %collective-permute-start = (bf16[2,128,128]{2,1,0:T(8,128)(2,1)S(1)}, bf16[2,128,128]{2,1,0:T(8,128)(2,1)S(1)}, u32[]{:S(2)}, u32[]{:S(2)}) collective-permute-start(bf16[2,128,128]{2,1,0:T(8,128)(2,1)S(1)} %pad_maximum_fusion.1.refs_6_.kv_ref), channel_id=1, source_target_pairs={{0,6},{1,7},{2,8},{3,9},{4,10},{5,11},{6,12},{7,13},{8,14},{9,15},... | collective-permute-start | bytes 196616 | tf_op jit(solution)/shard_map/ppermute | solution.py:233
  15.3 1.3 %collective-permute-start.5 = (f32[3,8,256]{2,1,0:T(8,128)S(1)}, f32[3,8,256]{2,1,0:T(8,128)S(1)}, u32[]{:S(2)}, u32[]{:S(2)}) collective-permute-start(f32[3,8,256]{2,1,0:T(8,128)S(1)} %get-tuple-element.27.refs_6_), channel_id=1, source_target_pairs={{0,1},{1,0},{2,3},{3,2},{4,5},{5,4},{6,7},{7,6},{8,9},{9,8},{10,11... | collective-permute-start | bytes 73736 | tf_op jit(solution)/shard_map/ppermute | solution.py:42
  17.5 7.4 %collective-permute-start.8 = (bf16[2,256,128]{2,1,0:T(8,128)(2,1)S(1)}, bf16[2,256,128]{2,1,0:T(8,128)(2,1)S(1)}, u32[]{:S(2)}, u32[]{:S(2)}) collective-permute-start(bf16[2,256,128]{2,1,0:T(8,128)(2,1)S(1)} %get-tuple-element.36), channel_id=1, source_target_pairs={{2,0},{5,1},{4,2},{7,3},{6,4},{9,5},{8,6},{11,7},{10,8},{13,9},{12... | collective-permute-start | bytes 393224 | tf_op jit(solution)/shard_map/ppermute | solution.py:302
  22.3 5.2 %collective-permute-start.7 = (bf16[2,128,128]{2,1,0:T(8,128)(2,1)S(1)}, bf16[2,128,128]{2,1,0:T(8,128)(2,1)S(1)}, u32[]{:S(2)}, u32[]{:S(2)}) collective-permute-start(bf16[2,128,128]{2,1,0:T(8,128)(2,1)S(1)} %get-tuple-element.35), channel_id=1, source_target_pairs={{6,0},{7,1},{8,2},{9,3},{10,4},{11,5},{12,6},{13,7},{14,8},{15,9},... | collective-permute-start | bytes 196616 | tf_op jit(solution)/shard_map/ppermute | solution.py:304
  24.9 2.6 %collective-permute-start.9 = (bf16[2,128,128]{2,1,0:T(8,128)(2,1)S(1)}, bf16[2,128,128]{2,1,0:T(8,128)(2,1)S(1)}, u32[]{:S(2)}, u32[]{:S(2)}) collective-permute-start(bf16[2,128,128]{2,1,0:T(8,128)(2,1)S(1)} %fusion.3), channel_id=1, source_target_pairs={{0,1},{1,0},{2,3},{3,2},{4,5},{5,4},{6,7},{7,6},{8,9},{9,8},{10,11... | collective-permute-start | bytes 196616 | tf_op jit(solution)/shard_map/ppermute | solution.py:42
  25.6 2.6 %collective-permute-start.6 = (bf16[128,1024]{1,0:T(8,128)(2,1)S(1)}, bf16[128,1024]{1,0:T(8,128)(2,1)S(1)}, u32[]{:S(2)}, u32[]{:S(2)}) collective-permute-start(bf16[128,1024]{1,0:T(8,128)(2,1)S(1)} %get-tuple-element.33), channel_id=1, source_target_pairs={{0,1},{1,0},{2,3},{3,2},{4,5},{5,4},{6,7},{7,6},{8,9},{9,8},{10,11... | collective-permute-start | bytes 786440 | tf_op jit(solution)/shard_map/ppermute | solution.py:42

commit v6 on v5

--- a/solution.py
+++ b/solution.py
@@ -14,8 +14,8 @@
 AXES = ("dp", "seq")
 NEG = -1e30
 FAR = 1 << 30
-NEAR_STEPS = (1, 2)
-FAR_STEP = 3
+NEAR_STEPS = (1, 3)
+FAR_STEP = 2
 SCALE = 1.0 / math.sqrt(HEAD_SIZE)
 SCALE2 = SCALE * math.log2(math.e)
 F32 = jnp.float32
@@ -71,7 +71,7 @@
     me, odd = where_am_i()
     lane = lax.broadcasted_iota(jnp.int32, (1, HEAD_SIZE), 1)
     down = lax.broadcasted_iota(jnp.int32, (t, HEAD_SIZE), 0)
-    near = (me // 2 - jnp.where(odd, 2, 1)) * 2 * t
+    near = (me // 2 - jnp.where(odd, NEAR_STEPS[1], NEAR_STEPS[0])) * 2 * t
     starts_of_parts = (((me - 2 * FAR_STEP) * t, me * t), (near, near + t))
     far = jnp.full((1, HEAD_SIZE), FAR, jnp.int32)
     zero = jnp.int32(0)

time: 29.2 us -> 28.3 us (0.969)
  waiting for transfers between devices: 9.35 us -> 8.38 us
    ppermute x1, waiting for transfers between devices: 2.52 us -> 0.64 us  [local_grads(): home_a = lax.ppermute(back_a, AXES, [(d, s) for s, d in a_moves])]
    ppermute x1, starting transfers between devices: 0.06 us -> 1.75 us  [local_grads(): home_b = lax.ppermute(back_b, AXES, [(d, s) for s, d in b_moves])]
    ppermute x1, waiting for transfers between devices: 4.52 us -> 6 us  [local_grads(): b = lax.ppermute(mine, AXES, b_moves)]
    ppermute x1, starting transfers between devices: 2.45 us -> 1.52 us  [local_grads(): b = lax.ppermute(mine, AXES, b_moves)]
    ppermute x1, waiting for transfers between devices: 1.34 us -> 0.65 us  [local_grads(): home_b = lax.ppermute(back_b, AXES, [(d, s) for s, d in b_moves])]
    ppermute x1, starting transfers between devices: 4.03 us -> 3.5 us  [local_grads(): home_a = lax.ppermute(back_a, AXES, [(d, s) for s, d in a_moves])]
  transfers between devices with their start and end apart: 10 -> 10, of which waited for: 4 -> 4; matrix products, arithmetic and copies ran while one was open for 2% -> 3% of each run, Pallas kernels for 12% -> 13%
where the time goes in v6:
time: 28.3 us; the launch traced here: 28.1 us
  starting transfers between devices  11.3 us (40%)
  waiting for transfers between devices  8.38 us (30%)
  Pallas kernels  5.4 us (19%)
  other arithmetic  1.65 us (6%)
  between operations  0.71 us (3%)
  local copies, waits for them, and re-layouts  0.63 us (2%)
    ppermute x1, waiting for transfers between devices, local_grads(): b = lax.ppermute(mine, AXES, b_moves)  6 us
    ppermute x1, starting transfers between devices, local_grads(): home_a = lax.ppermute(back_a, AXES, [(d, s) for s, d in a_moves])  3.5 us
    ppermute x1, starting transfers between devices, local_grads(): a = lax.ppermute(full, AXES, a_moves)  2.61 us
    ppermute x6, starting transfers between devices, swap(): return lax.ppermute(value, AXES, [(d, d ^ 1) for d in range(devices)])  1.95 us
    pallas_call x2, Pallas kernels, scores(): pl.pallas_call(functools.partial(score_kernel, rows, block), in_specs=[in...  1.88 us
    ppermute x1, starting transfers between devices, local_grads(): home_b = lax.ppermute(back_b, AXES, [(d, s) for s, d in b_moves])  1.75 us
    pallas_call x2, Pallas kernels, grads(): pl.pallas_call(functools.partial(grads_kernel, rows, block), in_specs=[in...  1.63 us
    ppermute x1, starting transfers between devices, local_grads(): b = lax.ppermute(mine, AXES, b_moves)  1.52 us
  transfers between devices with their start and end apart: 10, of which 4 were waited for; matrix products, arithmetic and copies ran while one was open for 3% of the time, Pallas kernels for 13%

profile of v6, /device:TPU:0, one launch (start us, length us, event | category | flops | bytes accessed | tf_op | source)
XLA Modules:
  0.0 28.1 jit_solution(6765472189669656550)
XLA Ops:
  0.6 0.8 %pad_maximum_fusion.1.refs_6_.kv_ref = bf16[2,128,128]{2,1,0:T(8,128)(2,1)S(1)} fusion(bf16[1,128,128]{2,1,0:T(8,128)(2,1)} %bitcast.6, bf16[1,128,128]{2,1,0:T(8,128)(2,1)} %bitcast.7), kind=kLoop, calls=%fused_computation.8 | loop fusion | flops 32768 | bytes 131072 | tf_op jit(solution)/shard_map/stack | solution.py:231
  1.4 0.5 %collective-permute-start.1 = (bf16[2,128,128]{2,1,0:T(8,128)(2,1)S(1)}, bf16[2,128,128]{2,1,0:T(8,128)(2,1)S(1)}, u32[]{:S(2)}, u32[]{:S(2)}) collective-permute-start(bf16[2,128,128]{2,1,0:T(8,128)(2,1)S(1)} %pad_maximum_fusion.1.refs_6_.kv_ref), channel_id=1, source_target_pairs={{0,1},{1,0},{2,3},{3,2},{4,5},{5,4},{6,7},{7,6},{8,9},{9,8},{10,11... | collective-permute-start | bytes 196616 | tf_op jit(solution)/shard_map/ppermute | solution.py:42
  2.0 1.3 %shard_map.76 = (bf16[1024,128]{1,0:T(8,128)(2,1)S(1)}, bf16[1024,128]{1,0:T(8,128)(2,1)S(1)}, bf16[2,256,128]{2,1,0:T(8,128)(2,1)S(1)}, bf16[2,2,256,128]{3,2,1,0:T(8,128)(2,1)S(1)}) custom-call(s32[11]{0:T(128)} %lens_hbm.1, bf16[128,1024]{1,0:T(8,128)(2,1)} %q_hbm.1, bf16[128,1024]{1,0:T(8,128)(2,1)} %g_hbm.1), custom_call_target="tpu_custom_call" | custom-call | flops 1048576 | bytes 1048576 | tf_op jit(solution)/shard_map/pallas_call | solution.py:245
  3.2 0.1 collective-permute-start.3
  3.3 0.5 %collective-permute-start.4 = (bf16[1024,128]{1,0:T(8,128)(2,1)S(1)}, bf16[1024,128]{1,0:T(8,128)(2,1)S(1)}, u32[]{:S(2)}, u32[]{:S(2)}) collective-permute-start(bf16[1024,128]{1,0:T(8,128)(2,1)S(1)} %get-tuple-element.21.refs_1_), channel_id=1, source_target_pairs={{0,1},{1,0},{2,3},{3,2},{4,5},{5,4},{6,7},{7,6},{8,9},{9,8},{10,11... | collective-permute-start | bytes 786440 | tf_op jit(solution)/shard_map/ppermute | solution.py:42
  3.9 2.6 %collective-permute-start.2 = (bf16[2,256,128]{2,1,0:T(8,128)(2,1)S(1)}, bf16[2,256,128]{2,1,0:T(8,128)(2,1)S(1)}, u32[]{:S(2)}, u32[]{:S(2)}) collective-permute-start(bf16[2,256,128]{2,1,0:T(8,128)(2,1)S(1)} %pad_maximum_fusion), channel_id=1, source_target_pairs={{0,2},{1,7},{2,4},{3,9},{4,6},{5,11},{6,8},{7,13},{8,10},{9,15},{1... | collective-permute-start | bytes 393224 | tf_op jit(solution)/shard_map/ppermute | solution.py:235
  6.5 1.5 %collective-permute-start = (bf16[2,128,128]{2,1,0:T(8,128)(2,1)S(1)}, bf16[2,128,128]{2,1,0:T(8,128)(2,1)S(1)}, u32[]{:S(2)}, u32[]{:S(2)}) collective-permute-start(bf16[2,128,128]{2,1,0:T(8,128)(2,1)S(1)} %pad_maximum_fusion.1.refs_6_.kv_ref), channel_id=1, source_target_pairs={{0,4},{1,5},{2,6},{3,7},{4,8},{5,9},{6,10},{7,11},{8,12},{9,13},{1... | collective-permute-start | bytes 196616 | tf_op jit(solution)/shard_map/ppermute | solution.py:233
  8.0 6.0 %collective-permute-done.refs_7_.b_ref = bf16[2,128,128]{2,1,0:T(8,128)(2,1)S(1)} collective-permute-done((bf16[2,128,128]{2,1,0:T(8,128)(2,1)S(1)}, bf16[2,128,128]{2,1,0:T(8,128)(2,1)S(1)}, u32[]{:S(2)}, u32[]{:S(2)}) %collective-permute-start) | collective-permute-done | bytes 65568 | tf_op jit(solution)/shard_map/ppermute | solution.py:233
  14.0 0.9 %shard_map.77 = (f32[1,256,2048]{2,1,0:T(8,128)S(1)}, f32[1,256,2048]{2,1,0:T(8,128)S(1)}, f32[3,8,256]{2,1,0:T(8,128)S(1)}) custom-call(bf16[1024,128]{1,0:T(8,128)(2,1)S(1)} %get-tuple-element.20.refs_0_, bf16[1024,128]{1,0:T(8,128)(2,1)S(1)} %get-tuple-element.21.refs_1_, bf16[1024,128]{1,0:T(8,128)(2,1)S(1)} %collective-permute-done.3.refs_2_, ...), custom_call_target="tpu_custom_call" | custom-call | flops 268435456 | bytes 1048576 | tf_op jit(solution)/shard_map/pallas_call | solution.py:270
  14.9 1.0 %shard_map.78 = (f32[1,256,2048]{2,1,0:T(8,128)S(1)}, f32[1,256,2048]{2,1,0:T(8,128)S(1)}, f32[3,8,256]{2,1,0:T(8,128)S(1)}) custom-call(bf16[1024,128]{1,0:T(8,128)(2,1)S(1)} %get-tuple-element.20.refs_0_, bf16[1024,128]{1,0:T(8,128)(2,1)S(1)} %get-tuple-element.21.refs_1_, bf16[1024,128]{1,0:T(8,128)(2,1)S(1)} %collective-permute-done.3.refs_2_, ...), custom_call_target="tpu_custom_call" | custom-call | flops 268435456 | bytes 1048576 | tf_op jit(solution)/shard_map/pallas_call | solution.py:270
  15.9 0.2 collective-permute-start.5
  16.1 1.1 %collective-permute-done.5.refs_7_ = f32[3,8,256]{2,1,0:T(8,128)S(1)} collective-permute-done((f32[3,8,256]{2,1,0:T(8,128)S(1)}, f32[3,8,256]{2,1,0:T(8,128)S(1)}, u32[]{:S(2)}, u32[]{:S(2)}) %collective-permute-start.5) | collective-permute-done | bytes 24608 | tf_op jit(solution)/shard_map/ppermute | solution.py:42
  17.2 0.8 %shard_map.80 = (bf16[1,256,2048]{2,1,0:T(8,128)(2,1)S(1)}, bf16[2,256,128]{2,1,0:T(8,128)(2,1)S(1)}) custom-call(bf16[1024,128]{1,0:T(8,128)(2,1)S(1)} %get-tuple-element.20.refs_0_, bf16[1024,128]{1,0:T(8,128)(2,1)S(1)} %get-tuple-element.21.refs_1_, bf16[1024,128]{1,0:T(8,128)(2,1)S(1)} %collective-permute-done.3.refs_2_, ...), custom_call_target="tpu_custom_call" | custom-call | flops 268435456 | bytes 1048576 | tf_op jit(solution)/shard_map/pallas_call | solution.py:289
  18.0 3.5 %collective-permute-start.8 = (bf16[2,256,128]{2,1,0:T(8,128)(2,1)S(1)}, bf16[2,256,128]{2,1,0:T(8,128)(2,1)S(1)}, u32[]{:S(2)}, u32[]{:S(2)}) collective-permute-start(bf16[2,256,128]{2,1,0:T(8,128)(2,1)S(1)} %get-tuple-element.36), channel_id=1, source_target_pairs={{2,0},{7,1},{4,2},{9,3},{6,4},{11,5},{8,6},{13,7},{10,8},{15,9},{1... | collective-permute-start | bytes 393224 | tf_op jit(solution)/shard_map/ppermute | solution.py:302
  21.5 0.8 %shard_map.79 = (bf16[1,256,2048]{2,1,0:T(8,128)(2,1)S(1)}, bf16[2,128,128]{2,1,0:T(8,128)(2,1)S(1)}, f32[2,128,128]{2,1,0:T(8,128)S(1)}) custom-call(bf16[1024,128]{1,0:T(8,128)(2,1)S(1)} %get-tuple-element.20.refs_0_, bf16[1024,128]{1,0:T(8,128)(2,1)S(1)} %get-tuple-element.21.refs_1_, bf16[1024,128]{1,0:T(8,128)(2,1)S(1)} %collective-permute-done.3.refs_2_, ...), custom_call_target="tpu_custom_call" | custom-call | flops 268435456 | bytes 1048576 | tf_op jit(solution)/shard_map/pallas_call | solution.py:289
  22.3 1.7 %collective-permute-start.7 = (bf16[2,128,128]{2,1,0:T(8,128)(2,1)S(1)}, bf16[2,128,128]{2,1,0:T(8,128)(2,1)S(1)}, u32[]{:S(2)}, u32[]{:S(2)}) collective-permute-start(bf16[2,128,128]{2,1,0:T(8,128)(2,1)S(1)} %get-tuple-element.35), channel_id=1, source_target_pairs={{4,0},{5,1},{6,2},{7,3},{8,4},{9,5},{10,6},{11,7},{12,8},{13,9},{1... | collective-permute-start | bytes 196616 | tf_op jit(solution)/shard_map/ppermute | solution.py:304
  24.1 0.6 %collective-permute-done.8 = bf16[2,256,128]{2,1,0:T(8,128)(2,1)S(1)} collective-permute-done((bf16[2,256,128]{2,1,0:T(8,128)(2,1)S(1)}, bf16[2,256,128]{2,1,0:T(8,128)(2,1)S(1)}, u32[]{:S(2)}, u32[]{:S(2)}) %collective-permute-start.8) | collective-permute-done | bytes 131104 | tf_op jit(solution)/shard_map/ppermute | solution.py:302
  24.7 0.1 collective-permute-start.9
  24.8 0.6 %shard_map.81 = (f32[128,1024]{1,0:T(8,128)S(1)}, bf16[128,1024]{1,0:T(8,128)(2,1)S(1)}) custom-call(bf16[2,128,128]{2,1,0:T(8,128)(2,1)S(1)} %pad_maximum_fusion.1.refs_6_.kv_ref, bf16[2,128,128]{2,1,0:T(8,128)(2,1)S(1)} %collective-permute-done.refs_7_.b_ref, bf16[2,256,128]{2,1,0:T(8,128)(2,1)S(1)} %collective-permute-done.2.refs_7_.a_ref, ...), custom_call_target="tpu_custom_call" | custom-call | flops 268435456 | bytes 1048576 | tf_op jit(solution)/shard_map/pallas_call | solution.py:305
  25.4 0.6 %collective-permute-start.6 = (bf16[128,1024]{1,0:T(8,128)(2,1)S(1)}, bf16[128,1024]{1,0:T(8,128)(2,1)S(1)}, u32[]{:S(2)}, u32[]{:S(2)}) collective-permute-start(bf16[128,1024]{1,0:T(8,128)(2,1)S(1)} %get-tuple-element.33), channel_id=1, source_target_pairs={{0,1},{1,0},{2,3},{3,2},{4,5},{5,4},{6,7},{7,6},{8,9},{9,8},{10,11... | collective-permute-start | bytes 786440 | tf_op jit(solution)/shard_map/ppermute | solution.py:42
  26.0 0.6 %collective-permute-done.7 = bf16[2,128,128]{2,1,0:T(8,128)(2,1)S(1)} collective-permute-done((bf16[2,128,128]{2,1,0:T(8,128)(2,1)S(1)}, bf16[2,128,128]{2,1,0:T(8,128)(2,1)S(1)}, u32[]{:S(2)}, u32[]{:S(2)}) %collective-permute-start.7) | collective-permute-done | bytes 65568 | tf_op jit(solution)/shard_map/ppermute | solution.py:304
  26.7 0.6 %slice_bitcast_fusion = (bf16[128,128]{1,0:T(8,128)(2,1)}, bf16[128,128]{1,0:T(8,128)(2,1)}) fusion(bf16[2,128,128]{2,1,0:T(8,128)(2,1)S(1)} %fusion.2), kind=kLoop, calls=%fused_computation.11 | loop fusion | bytes 131072 | tf_op jit(solution)/shard_map/squeeze | solution.py:320
  27.3 0.0 collective-permute-done.6
  27.3 0.8 %add_convert_fusion = bf16[128,1024]{1,0:T(8,128)(2,1)} fusion(f32[128,1024]{1,0:T(8,128)S(1)} %get-tuple-element.32, bf16[128,1024]{1,0:T(8,128)(2,1)S(1)} %collective-permute-done.6), kind=kLoop, calls=%fused_computation | loop fusion | flops 393216 | bytes 1048576 | tf_op jit(solution)/shard_map/convert_element_type | solution.py:314
  (9 shorter events, 0.1 us)
Async XLA Ops:
  1.4 2.4 %collective-permute-start.1 = (bf16[2,128,128]{2,1,0:T(8,128)(2,1)S(1)}, bf16[2,128,128]{2,1,0:T(8,128)(2,1)S(1)}, u32[]{:S(2)}, u32[]{:S(2)}) collective-permute-start(bf16[2,128,128]{2,1,0:T(8,128)(2,1)S(1)} %pad_maximum_fusion.1.refs_6_.kv_ref), channel_id=1, source_target_pairs={{0,1},{1,0},{2,3},{3,2},{4,5},{5,4},{6,7},{7,6},{8,9},{9,8},{10,11... | collective-permute-start | bytes 196616 | tf_op jit(solution)/shard_map/ppermute | solution.py:42
  3.2 10.8 %collective-permute-start.3 = (bf16[1024,128]{1,0:T(8,128)(2,1)S(1)}, bf16[1024,128]{1,0:T(8,128)(2,1)S(1)}, u32[]{:S(2)}, u32[]{:S(2)}) collective-permute-start(bf16[1024,128]{1,0:T(8,128)(2,1)S(1)} %get-tuple-element.20.refs_0_), channel_id=1, source_target_pairs={{0,1},{1,0},{2,3},{3,2},{4,5},{5,4},{6,7},{7,6},{8,9},{9,8},{10,11... | collective-permute-start | bytes 786440 | tf_op jit(solution)/shard_map/ppermute | solution.py:42
  3.3 10.7 %collective-permute-start.4 = (bf16[1024,128]{1,0:T(8,128)(2,1)S(1)}, bf16[1024,128]{1,0:T(8,128)(2,1)S(1)}, u32[]{:S(2)}, u32[]{:S(2)}) collective-permute-start(bf16[1024,128]{1,0:T(8,128)(2,1)S(1)} %get-tuple-element.21.refs_1_), channel_id=1, source_target_pairs={{0,1},{1,0},{2,3},{3,2},{4,5},{5,4},{6,7},{7,6},{8,9},{9,8},{10,11... | collective-permute-start | bytes 786440 | tf_op jit(solution)/shard_map/ppermute | solution.py:42
  3.9 11.1 %collective-permute-start.2 = (bf16[2,256,128]{2,1,0:T(8,128)(2,1)S(1)}, bf16[2,256,128]{2,1,0:T(8,128)(2,1)S(1)}, u32[]{:S(2)}, u32[]{:S(2)}) collective-permute-start(bf16[2,256,128]{2,1,0:T(8,128)(2,1)S(1)} %pad_maximum_fusion), channel_id=1, source_target_pairs={{0,2},{1,7},{2,4},{3,9},{4,6},{5,11},{6,8},{7,13},{8,10},{9,15},{1... | collective-permute-start | bytes 393224 | tf_op jit(solution)/shard_map/ppermute | solution.py:235
  6.5 7.5 %collective-permute-start = (bf16[2,128,128]{2,1,0:T(8,128)(2,1)S(1)}, bf16[2,128,128]{2,1,0:T(8,128)(2,1)S(1)}, u32[]{:S(2)}, u32[]{:S(2)}) collective-permute-start(bf16[2,128,128]{2,1,0:T(8,128)(2,1)S(1)} %pad_maximum_fusion.1.refs_6_.kv_ref), channel_id=1, source_target_pairs={{0,4},{1,5},{2,6},{3,7},{4,8},{5,9},{6,10},{7,11},{8,12},{9,13},{1... | collective-permute-start | bytes 196616 | tf_op jit(solution)/shard_map/ppermute | solution.py:233
  15.9 1.3 %collective-permute-start.5 = (f32[3,8,256]{2,1,0:T(8,128)S(1)}, f32[3,8,256]{2,1,0:T(8,128)S(1)}, u32[]{:S(2)}, u32[]{:S(2)}) collective-permute-start(f32[3,8,256]{2,1,0:T(8,128)S(1)} %get-tuple-element.27.refs_6_), channel_id=1, source_target_pairs={{0,1},{1,0},{2,3},{3,2},{4,5},{5,4},{6,7},{7,6},{8,9},{9,8},{10,11... | collective-permute-start | bytes 73736 | tf_op jit(solution)/shard_map/ppermute | solution.py:42
  18.0 6.7 %collective-permute-start.8 = (bf16[2,256,128]{2,1,0:T(8,128)(2,1)S(1)}, bf16[2,256,128]{2,1,0:T(8,128)(2,1)S(1)}, u32[]{:S(2)}, u32[]{:S(2)}) collective-permute-start(bf16[2,256,128]{2,1,0:T(8,128)(2,1)S(1)} %get-tuple-element.36), channel_id=1, source_target_pairs={{2,0},{7,1},{4,2},{9,3},{6,4},{11,5},{8,6},{13,7},{10,8},{15,9},{1... | collective-permute-start | bytes 393224 | tf_op jit(solution)/shard_map/ppermute | solution.py:302
  22.3 4.3 %collective-permute-start.7 = (bf16[2,128,128]{2,1,0:T(8,128)(2,1)S(1)}, bf16[2,128,128]{2,1,0:T(8,128)(2,1)S(1)}, u32[]{:S(2)}, u32[]{:S(2)}) collective-permute-start(bf16[2,128,128]{2,1,0:T(8,128)(2,1)S(1)} %get-tuple-element.35), channel_id=1, source_target_pairs={{4,0},{5,1},{6,2},{7,3},{8,4},{9,5},{10,6},{11,7},{12,8},{13,9},{1... | collective-permute-start | bytes 196616 | tf_op jit(solution)/shard_map/ppermute | solution.py:304
  24.7 1.9 %collective-permute-start.9 = (bf16[2,128,128]{2,1,0:T(8,128)(2,1)S(1)}, bf16[2,128,128]{2,1,0:T(8,128)(2,1)S(1)}, u32[]{:S(2)}, u32[]{:S(2)}) collective-permute-start(bf16[2,128,128]{2,1,0:T(8,128)(2,1)S(1)} %fusion.3), channel_id=1, source_target_pairs={{0,1},{1,0},{2,3},{3,2},{4,5},{5,4},{6,7},{7,6},{8,9},{9,8},{10,11... | collective-permute-start | bytes 196616 | tf_op jit(solution)/shard_map/ppermute | solution.py:42
  25.4 1.9 %collective-permute-start.6 = (bf16[128,1024]{1,0:T(8,128)(2,1)S(1)}, bf16[128,1024]{1,0:T(8,128)(2,1)S(1)}, u32[]{:S(2)}, u32[]{:S(2)}) collective-permute-start(bf16[128,1024]{1,0:T(8,128)(2,1)S(1)} %get-tuple-element.33), channel_id=1, source_target_pairs={{0,1},{1,0},{2,3},{3,2},{4,5},{5,4},{6,7},{7,6},{8,9},{9,8},{10,11... | collective-permute-start | bytes 786440 | tf_op jit(solution)/shard_map/ppermute | solution.py:42

commit v7 on v6

--- a/solution.py
+++ b/solution.py
@@ -170,9 +170,9 @@
                 stats_ref[3 * head + i] = found[i]
 
 
-def grads_kernel(rows, block, *refs):
+def grads_kernel(rows, span, *refs):
     qs, gs = (refs[0], refs[2]), (refs[1], refs[3])
-    s_ref, g_ref, stats_ref, other_ref, ds_ref, home_ref = refs[4:10]
+    s_ref, g_ref, stats_ref, other_ref, ds_ref, home_ref = refs[4:]
     t = rows
     for head in range(s_ref.shape[0]):
         lanes = slice(head * HEAD_SIZE, (head + 1) * HEAD_SIZE)
@@ -188,8 +188,8 @@
                 turn = side * half + pair
                 cols = slice(turn * 2 * t, (turn + 1) * 2 * t)
                 level, delta = levels[turn : turn + 1], deltas[turn : turn + 1]
-                p = jnp.exp2(s_ref[head, :, cols] - level)
-                ds = (p * (g_ref[head, :, cols] - delta)).astype(BF16)
+                p = jnp.exp2(s_ref[head, span, cols] - level)
+                ds = (p * (g_ref[head, span, cols] - delta)).astype(BF16)
                 ds_ref[head, :, cols] = ds
                 at = head * GROUP + pair * 2
                 dk = dot_nn(ds, stacked(qs[side], t, at, 2))
@@ -197,27 +197,20 @@
                 grads = [dk, dv] if turn == 0 else [grads[0] + dk, grads[1] + dv]
         grads[0] = grads[0] * SCALE
         for kind, grad in enumerate(grads):
-            if block:
-                home_ref[kind, :, lanes] = grad.astype(BF16)
-            else:
-                home_ref[kind, :, lanes] = grad[:t].astype(BF16)
-                refs[10][kind, :, lanes] = grad[t:]
-
-
-def query_kernel(rows, kv_ref, b_ref, a_ref, dsb_ref, dsa_ref, mine_ref, mate_ref):
+            home_ref[kind, :, lanes] = grad.astype(home_ref.dtype)
+
+
+def query_kernel(rows, side, *refs):
     t = rows
-    for head in range(dsb_ref.shape[0]):
+    keys, scores, out_ref = refs[:3], refs[3:6], refs[6]
+    cols = slice(side * GROUP * t, (side + 1) * GROUP * t)
+    for head in range(scores[0].shape[0]):
         lanes = slice(head * HEAD_SIZE, (head + 1) * HEAD_SIZE)
-        key_b, key_a = (
-            block_rows(block, 0, kv_ref, got, lanes).T for block, got in ((0, b_ref), (1, a_ref))
-        )
-        for side, out_ref in ((1, mate_ref), (0, mine_ref)):
-            cols = slice(side * GROUP * t, (side + 1) * GROUP * t)
-            dqt = dot_nn(key_b, dsb_ref[head, :, cols]) + dot_nn(key_a, dsa_ref[head, :, cols])
-            dqt = dqt * SCALE
-            for h in range(GROUP):
-                at = (head * GROUP + h) * HEAD_SIZE
-                out_ref[:, at : at + HEAD_SIZE] = dqt[:, h * t : (h + 1) * t].T.astype(out_ref.dtype)
+        dqt = sum(dot_nn(key[0, :, lanes].T, ds[head, :, cols]) for key, ds in zip(keys, scores))
+        dqt = dqt * SCALE
+        for h in range(GROUP):
+            at = (head * GROUP + h) * HEAD_SIZE
+            out_ref[:, at : at + HEAD_SIZE] = dqt[:, h * t : (h + 1) * t].T.astype(out_ref.dtype)
 
 
 def local_grads(queries, keys, values, d_out, doc_lengths):
@@ -280,37 +273,43 @@
             cost_estimate=cost(1 << 28),
         )(*rows_of, member, late, mine, got, *before)
 
-    def grads(block, s, g, stats, other):
-        out_shape = [shape((kv_heads, 2 * rows, width), BF16)]
-        if block:
-            out_shape += [shape((2, 2 * rows, kv_width), BF16)]
-        else:
-            out_shape += [shape((2, rows, kv_width), BF16), shape((2, rows, kv_width), F32)]
+    s_b, g_b, stats_b = scores(0, b)
+    s_a, g_a, stats = scores(1, a, stats_b)
+    other = swap(stats, devices)
+
+    def grads(span, dtype, s, g):
+        count = span.stop - span.start
         return pl.pallas_call(
-            functools.partial(grads_kernel, rows, block),
+            functools.partial(grads_kernel, rows, span),
             in_specs=[in_vmem] * 8,
-            out_specs=[in_vmem] * len(out_shape),
-            out_shape=out_shape,
+            out_specs=[in_vmem] * 2,
+            out_shape=[
+                shape((kv_heads, count, width), BF16),
+                shape((2, count, kv_width), dtype),
+            ],
             compiler_params=grant,
             cost_estimate=cost(1 << 28),
         )(*rows_of, s, g, stats, other)
 
-    s_b, g_b, stats_b = scores(0, b)
-    s_a, g_a, stats = scores(1, a, stats_b)
-    other = swap(stats, devices)
-    ds_a, back_a = grads(1, s_a, g_a, stats, other)
+    ds_a, back_a = grads(slice(0, 2 * rows), BF16, s_a, g_a)
     home_a = lax.ppermute(back_a, AXES, [(d, s) for s, d in a_moves])
-    ds_b, back_b, own = grads(0, s_b, g_b, stats, other)
+    ds_b, back_b = grads(slice(0, rows), BF16, s_b, g_b)
     home_b = lax.ppermute(back_b, AXES, [(d, s) for s, d in b_moves])
-    dq_mine, dq_mate = pl.pallas_call(
-        functools.partial(query_kernel, rows),
-        in_specs=[in_vmem] * 5,
-        out_specs=[in_vmem] * 2,
-        out_shape=[shape((rows, q_width), F32), shape((rows, q_width), BF16)],
-        compiler_params=grant,
-        cost_estimate=cost(1 << 28),
-    )(mine, b, a, ds_b, ds_a)
+    ds_own, own = grads(slice(rows, 2 * rows), F32, s_b, g_b)
+
+    def query(side, dtype):
+        return pl.pallas_call(
+            functools.partial(query_kernel, rows, side),
+            in_specs=[in_vmem] * 6,
+            out_specs=in_vmem,
+            out_shape=shape((rows, q_width), dtype),
+            compiler_params=grant,
+            cost_estimate=cost(1 << 27),
+        )(mine, b, a, ds_own, ds_b, ds_a)
+
+    dq_mate = query(1, BF16)
     dq_other = swap(dq_mate, devices)
+    dq_mine = query(0, F32)
     d_queries = (dq_mine + dq_other.astype(F32)).astype(BF16)
 
     first, second = home_a[:, :rows].astype(F32), home_a[:, rows:].astype(F32)

time: 28.3 us -> 28.4 us (level)
  Pallas kernels: 5.4 us -> 5.94 us
  waiting for transfers between devices: 8.38 us -> 7.9 us
    ppermute x1, waiting for transfers between devices: 0.65 us -> 0.01 us  [local_grads(): home_b = lax.ppermute(back_b, AXES, [(d, s) for s, d in b_moves])]
    pallas_call x3 -> x5, Pallas kernels: 2.24 us -> 2.78 us  [the longest x3 1.8 us: grads(): pl.pallas_call(functools.partial(grads_kernel, rows, span), in_specs=[in_...]
  transfers between devices with their start and end apart: 10 -> 10, of which waited for: 4 -> 3; matrix products, arithmetic and copies ran while one was open for 3% -> 3% of each run, Pallas kernels for 13% -> 15%
where the time goes in v7:
time: 28.4 us; the launch traced here: 28.2 us
  starting transfers between devices  11.3 us (40%)
  waiting for transfers between devices  7.9 us (28%)
  Pallas kernels  5.94 us (21%)
  other arithmetic  1.63 us (6%)
  between operations  0.74 us (3%)
  local copies, waits for them, and re-layouts  0.63 us (2%)
    ppermute x1, waiting for transfers between devices, local_grads(): b = lax.ppermute(mine, AXES, b_moves)  6 us
    ppermute x1, starting transfers between devices, local_grads(): home_a = lax.ppermute(back_a, AXES, [(d, s) for s, d in a_moves])  3.51 us
    ppermute x1, starting transfers between devices, local_grads(): a = lax.ppermute(full, AXES, a_moves)  2.61 us
    ppermute x6, starting transfers between devices, swap(): return lax.ppermute(value, AXES, [(d, d ^ 1) for d in range(devices)])  1.93 us
    pallas_call x2, Pallas kernels, scores(): pl.pallas_call(functools.partial(score_kernel, rows, block), in_specs=[in...  1.88 us
    pallas_call x3, Pallas kernels, grads(): pl.pallas_call(functools.partial(grads_kernel, rows, span), in_specs=[in_...  1.8 us
    ppermute x1, starting transfers between devices, local_grads(): home_b = lax.ppermute(back_b, AXES, [(d, s) for s, d in b_moves])  1.74 us
    ppermute x1, starting transfers between devices, local_grads(): b = lax.ppermute(mine, AXES, b_moves)  1.52 us
  transfers between devices with their start and end apart: 10, of which 3 were waited for; matrix products, arithmetic and copies ran while one was open for 3% of the time, Pallas kernels for 15%

profile of v7, /device:TPU:0, one launch (start us, length us, event | category | flops | bytes accessed | tf_op | source)
XLA Modules:
  0.0 28.2 jit_solution(8701398738651323259)
XLA Ops:
  0.6 0.8 %pad_maximum_fusion.1.refs_6_.refs_0_ = bf16[2,128,128]{2,1,0:T(8,128)(2,1)S(1)} fusion(bf16[1,128,128]{2,1,0:T(8,128)(2,1)} %bitcast.6, bf16[1,128,128]{2,1,0:T(8,128)(2,1)} %bitcast.7), kind=kLoop, calls=%fused_computation.8 | loop fusion | flops 32768 | bytes 131072 | tf_op jit(solution)/shard_map/stack | solution.py:224
  1.4 0.5 %collective-permute-start.1 = (bf16[2,128,128]{2,1,0:T(8,128)(2,1)S(1)}, bf16[2,128,128]{2,1,0:T(8,128)(2,1)S(1)}, u32[]{:S(2)}, u32[]{:S(2)}) collective-permute-start(bf16[2,128,128]{2,1,0:T(8,128)(2,1)S(1)} %pad_maximum_fusion.1.refs_6_.refs_0_), channel_id=1, source_target_pairs={{0,1},{1,0},{2,3},{3,2},{4,5},{5,4},{6,7},{7,6},{8,9},{9,8},{10,11... | collective-permute-start | bytes 196616 | tf_op jit(solution)/shard_map/ppermute | solution.py:42
  2.0 1.3 %shard_map.76 = (bf16[1024,128]{1,0:T(8,128)(2,1)S(1)}, bf16[1024,128]{1,0:T(8,128)(2,1)S(1)}, bf16[2,256,128]{2,1,0:T(8,128)(2,1)S(1)}, bf16[2,2,256,128]{3,2,1,0:T(8,128)(2,1)S(1)}) custom-call(s32[11]{0:T(128)} %lens_hbm.1, bf16[128,1024]{1,0:T(8,128)(2,1)} %q_hbm.1, bf16[128,1024]{1,0:T(8,128)(2,1)} %g_hbm.1), custom_call_target="tpu_custom_call" | custom-call | flops 1048576 | bytes 1048576 | tf_op jit(solution)/shard_map/pallas_call | solution.py:238
  3.2 0.1 collective-permute-start.3
  3.3 0.5 %collective-permute-start.4 = (bf16[1024,128]{1,0:T(8,128)(2,1)S(1)}, bf16[1024,128]{1,0:T(8,128)(2,1)S(1)}, u32[]{:S(2)}, u32[]{:S(2)}) collective-permute-start(bf16[1024,128]{1,0:T(8,128)(2,1)S(1)} %get-tuple-element.20.refs_1_), channel_id=1, source_target_pairs={{0,1},{1,0},{2,3},{3,2},{4,5},{5,4},{6,7},{7,6},{8,9},{9,8},{10,11... | collective-permute-start | bytes 786440 | tf_op jit(solution)/shard_map/ppermute | solution.py:42
  3.9 2.6 %collective-permute-start.2 = (bf16[2,256,128]{2,1,0:T(8,128)(2,1)S(1)}, bf16[2,256,128]{2,1,0:T(8,128)(2,1)S(1)}, u32[]{:S(2)}, u32[]{:S(2)}) collective-permute-start(bf16[2,256,128]{2,1,0:T(8,128)(2,1)S(1)} %pad_maximum_fusion), channel_id=1, source_target_pairs={{0,2},{1,7},{2,4},{3,9},{4,6},{5,11},{6,8},{7,13},{8,10},{9,15},{1... | collective-permute-start | bytes 393224 | tf_op jit(solution)/shard_map/ppermute | solution.py:228
  6.5 1.5 %collective-permute-start = (bf16[2,128,128]{2,1,0:T(8,128)(2,1)S(1)}, bf16[2,128,128]{2,1,0:T(8,128)(2,1)S(1)}, u32[]{:S(2)}, u32[]{:S(2)}) collective-permute-start(bf16[2,128,128]{2,1,0:T(8,128)(2,1)S(1)} %pad_maximum_fusion.1.refs_6_.refs_0_), channel_id=1, source_target_pairs={{0,4},{1,5},{2,6},{3,7},{4,8},{5,9},{6,10},{7,11},{8,12},{9,13},{1... | collective-permute-start | bytes 196616 | tf_op jit(solution)/shard_map/ppermute | solution.py:226
  8.0 6.0 %collective-permute-done.refs_7_.refs_1_ = bf16[2,128,128]{2,1,0:T(8,128)(2,1)S(1)} collective-permute-done((bf16[2,128,128]{2,1,0:T(8,128)(2,1)S(1)}, bf16[2,128,128]{2,1,0:T(8,128)(2,1)S(1)}, u32[]{:S(2)}, u32[]{:S(2)}) %collective-permute-start) | collective-permute-done | bytes 65568 | tf_op jit(solution)/shard_map/ppermute | solution.py:226
  14.0 0.9 %shard_map.77 = (f32[1,256,2048]{2,1,0:T(8,128)S(1)}, f32[1,256,2048]{2,1,0:T(8,128)S(1)}, f32[3,8,256]{2,1,0:T(8,128)S(1)}) custom-call(bf16[1024,128]{1,0:T(8,128)(2,1)S(1)} %get-tuple-element.19.refs_0_, bf16[1024,128]{1,0:T(8,128)(2,1)S(1)} %get-tuple-element.20.refs_1_, bf16[1024,128]{1,0:T(8,128)(2,1)S(1)} %collective-permute-done.3.refs_2_, ...), custom_call_target="tpu_custom_call" | custom-call | flops 268435456 | bytes 1048576 | tf_op jit(solution)/shard_map/pallas_call | solution.py:263
  14.9 0.9 %shard_map.78 = (f32[1,256,2048]{2,1,0:T(8,128)S(1)}, f32[1,256,2048]{2,1,0:T(8,128)S(1)}, f32[3,8,256]{2,1,0:T(8,128)S(1)}) custom-call(bf16[1024,128]{1,0:T(8,128)(2,1)S(1)} %get-tuple-element.19.refs_0_, bf16[1024,128]{1,0:T(8,128)(2,1)S(1)} %get-tuple-element.20.refs_1_, bf16[1024,128]{1,0:T(8,128)(2,1)S(1)} %collective-permute-done.3.refs_2_, ...), custom_call_target="tpu_custom_call" | custom-call | flops 268435456 | bytes 1048576 | tf_op jit(solution)/shard_map/pallas_call | solution.py:263
  15.9 0.2 collective-permute-start.5
  16.1 1.1 %collective-permute-done.5.refs_7_ = f32[3,8,256]{2,1,0:T(8,128)S(1)} collective-permute-done((f32[3,8,256]{2,1,0:T(8,128)S(1)}, f32[3,8,256]{2,1,0:T(8,128)S(1)}, u32[]{:S(2)}, u32[]{:S(2)}) %collective-permute-start.5) | collective-permute-done | bytes 24608 | tf_op jit(solution)/shard_map/ppermute | solution.py:42
  17.2 0.8 %shard_map.81 = (bf16[1,256,2048]{2,1,0:T(8,128)(2,1)S(1)}, bf16[2,256,128]{2,1,0:T(8,128)(2,1)S(1)}) custom-call(bf16[1024,128]{1,0:T(8,128)(2,1)S(1)} %get-tuple-element.19.refs_0_, bf16[1024,128]{1,0:T(8,128)(2,1)S(1)} %get-tuple-element.20.refs_1_, bf16[1024,128]{1,0:T(8,128)(2,1)S(1)} %collective-permute-done.3.refs_2_, ...), custom_call_target="tpu_custom_call" | custom-call | flops 268435456 | bytes 1048576 | tf_op jit(solution)/shard_map/pallas_call | solution.py:282
  18.0 3.5 %collective-permute-start.8 = (bf16[2,256,128]{2,1,0:T(8,128)(2,1)S(1)}, bf16[2,256,128]{2,1,0:T(8,128)(2,1)S(1)}, u32[]{:S(2)}, u32[]{:S(2)}) collective-permute-start(bf16[2,256,128]{2,1,0:T(8,128)(2,1)S(1)} %get-tuple-element.34), channel_id=1, source_target_pairs={{2,0},{7,1},{4,2},{9,3},{6,4},{11,5},{8,6},{13,7},{10,8},{15,9},{1... | collective-permute-start | bytes 393224 | tf_op jit(solution)/shard_map/ppermute | solution.py:295
  21.5 0.5 %shard_map.80 = (bf16[1,128,2048]{2,1,0:T(8,128)(2,1)S(1)}, bf16[2,128,128]{2,1,0:T(8,128)(2,1)S(1)}) custom-call(bf16[1024,128]{1,0:T(8,128)(2,1)S(1)} %get-tuple-element.19.refs_0_, bf16[1024,128]{1,0:T(8,128)(2,1)S(1)} %get-tuple-element.20.refs_1_, bf16[1024,128]{1,0:T(8,128)(2,1)S(1)} %collective-permute-done.3.refs_2_, ...), custom_call_target="tpu_custom_call" | custom-call | flops 268435456 | bytes 1048576 | tf_op jit(solution)/shard_map/pallas_call | solution.py:282
  22.0 1.7 %collective-permute-start.7 = (bf16[2,128,128]{2,1,0:T(8,128)(2,1)S(1)}, bf16[2,128,128]{2,1,0:T(8,128)(2,1)S(1)}, u32[]{:S(2)}, u32[]{:S(2)}) collective-permute-start(bf16[2,128,128]{2,1,0:T(8,128)(2,1)S(1)} %get-tuple-element.33), channel_id=1, source_target_pairs={{4,0},{5,1},{6,2},{7,3},{8,4},{9,5},{10,6},{11,7},{12,8},{13,9},{1... | collective-permute-start | bytes 196616 | tf_op jit(solution)/shard_map/ppermute | solution.py:297
  23.7 0.8 %collective-permute-done.8 = bf16[2,256,128]{2,1,0:T(8,128)(2,1)S(1)} collective-permute-done((bf16[2,256,128]{2,1,0:T(8,128)(2,1)S(1)}, bf16[2,256,128]{2,1,0:T(8,128)(2,1)S(1)}, u32[]{:S(2)}, u32[]{:S(2)}) %collective-permute-start.8) | collective-permute-done | bytes 131104 | tf_op jit(solution)/shard_map/ppermute | solution.py:295
  24.6 0.1 collective-permute-start.9
  24.6 0.5 %shard_map.79 = (bf16[1,128,2048]{2,1,0:T(8,128)(2,1)S(1)}, f32[2,128,128]{2,1,0:T(8,128)S(1)}) custom-call(bf16[1024,128]{1,0:T(8,128)(2,1)S(1)} %get-tuple-element.19.refs_0_, bf16[1024,128]{1,0:T(8,128)(2,1)S(1)} %get-tuple-element.20.refs_1_, bf16[1024,128]{1,0:T(8,128)(2,1)S(1)} %collective-permute-done.3.refs_2_, ...), custom_call_target="tpu_custom_call" | custom-call | flops 268435456 | bytes 1048576 | tf_op jit(solution)/shard_map/pallas_call | solution.py:282
  25.1 0.5 %shard_map.83 = bf16[128,1024]{1,0:T(8,128)(2,1)S(1)} custom-call(bf16[2,128,128]{2,1,0:T(8,128)(2,1)S(1)} %pad_maximum_fusion.1.refs_6_.refs_0_, bf16[2,128,128]{2,1,0:T(8,128)(2,1)S(1)} %collective-permute-done.refs_7_.refs_1_, bf16[2,256,128]{2,1,0:T(8,128)(2,1)S(1)} %collective-permute-done.2.refs_7_.refs_2_, ...), custom_call_target="tpu_custom_call" | custom-call | flops 134217728 | bytes 1048576 | tf_op jit(solution)/shard_map/pallas_call | solution.py:301
  25.6 0.6 %collective-permute-start.6 = (bf16[128,1024]{1,0:T(8,128)(2,1)S(1)}, bf16[128,1024]{1,0:T(8,128)(2,1)S(1)}, u32[]{:S(2)}, u32[]{:S(2)}) collective-permute-start(bf16[128,1024]{1,0:T(8,128)(2,1)S(1)} %shard_map.83), channel_id=1, source_target_pairs={{0,1},{1,0},{2,3},{3,2},{4,5},{5,4},{6,7},{7,6},{8,9},{9,8},{10,11... | collective-permute-start | bytes 786440 | tf_op jit(solution)/shard_map/ppermute | solution.py:42
  26.2 0.5 %shard_map.82 = f32[128,1024]{1,0:T(8,128)S(1)} custom-call(bf16[2,128,128]{2,1,0:T(8,128)(2,1)S(1)} %pad_maximum_fusion.1.refs_6_.refs_0_, bf16[2,128,128]{2,1,0:T(8,128)(2,1)S(1)} %collective-permute-done.refs_7_.refs_1_, bf16[2,256,128]{2,1,0:T(8,128)(2,1)S(1)} %collective-permute-done.2.refs_7_.refs_2_, ...), custom_call_target="tpu_custom_call" | custom-call | flops 134217728 | bytes 1048576 | tf_op jit(solution)/shard_map/pallas_call | solution.py:301
  26.8 0.6 %slice_bitcast_fusion = (bf16[128,128]{1,0:T(8,128)(2,1)}, bf16[128,128]{1,0:T(8,128)(2,1)}) fusion(bf16[2,128,128]{2,1,0:T(8,128)(2,1)S(1)} %fusion.2), kind=kLoop, calls=%fused_computation.11 | loop fusion | bytes 131072 | tf_op jit(solution)/shard_map/squeeze | solution.py:319
  27.4 0.8 %add_convert_fusion = bf16[128,1024]{1,0:T(8,128)(2,1)} fusion(f32[128,1024]{1,0:T(8,128)S(1)} %shard_map.82, bf16[128,1024]{1,0:T(8,128)(2,1)S(1)} %collective-permute-done.6), kind=kLoop, calls=%fused_computation | loop fusion | flops 393216 | bytes 1048576 | tf_op jit(solution)/shard_map/convert_element_type | solution.py:313
  (11 shorter events, 0.1 us)
Async XLA Ops:
  1.4 2.4 %collective-permute-start.1 = (bf16[2,128,128]{2,1,0:T(8,128)(2,1)S(1)}, bf16[2,128,128]{2,1,0:T(8,128)(2,1)S(1)}, u32[]{:S(2)}, u32[]{:S(2)}) collective-permute-start(bf16[2,128,128]{2,1,0:T(8,128)(2,1)S(1)} %pad_maximum_fusion.1.refs_6_.refs_0_), channel_id=1, source_target_pairs={{0,1},{1,0},{2,3},{3,2},{4,5},{5,4},{6,7},{7,6},{8,9},{9,8},{10,11... | collective-permute-start | bytes 196616 | tf_op jit(solution)/shard_map/ppermute | solution.py:42
  3.2 10.8 %collective-permute-start.3 = (bf16[1024,128]{1,0:T(8,128)(2,1)S(1)}, bf16[1024,128]{1,0:T(8,128)(2,1)S(1)}, u32[]{:S(2)}, u32[]{:S(2)}) collective-permute-start(bf16[1024,128]{1,0:T(8,128)(2,1)S(1)} %get-tuple-element.19.refs_0_), channel_id=1, source_target_pairs={{0,1},{1,0},{2,3},{3,2},{4,5},{5,4},{6,7},{7,6},{8,9},{9,8},{10,11... | collective-permute-start | bytes 786440 | tf_op jit(solution)/shard_map/ppermute | solution.py:42
  3.3 10.7 %collective-permute-start.4 = (bf16[1024,128]{1,0:T(8,128)(2,1)S(1)}, bf16[1024,128]{1,0:T(8,128)(2,1)S(1)}, u32[]{:S(2)}, u32[]{:S(2)}) collective-permute-start(bf16[1024,128]{1,0:T(8,128)(2,1)S(1)} %get-tuple-element.20.refs_1_), channel_id=1, source_target_pairs={{0,1},{1,0},{2,3},{3,2},{4,5},{5,4},{6,7},{7,6},{8,9},{9,8},{10,11... | collective-permute-start | bytes 786440 | tf_op jit(solution)/shard_map/ppermute | solution.py:42
  3.9 11.1 %collective-permute-start.2 = (bf16[2,256,128]{2,1,0:T(8,128)(2,1)S(1)}, bf16[2,256,128]{2,1,0:T(8,128)(2,1)S(1)}, u32[]{:S(2)}, u32[]{:S(2)}) collective-permute-start(bf16[2,256,128]{2,1,0:T(8,128)(2,1)S(1)} %pad_maximum_fusion), channel_id=1, source_target_pairs={{0,2},{1,7},{2,4},{3,9},{4,6},{5,11},{6,8},{7,13},{8,10},{9,15},{1... | collective-permute-start | bytes 393224 | tf_op jit(solution)/shard_map/ppermute | solution.py:228
  6.5 7.5 %collective-permute-start = (bf16[2,128,128]{2,1,0:T(8,128)(2,1)S(1)}, bf16[2,128,128]{2,1,0:T(8,128)(2,1)S(1)}, u32[]{:S(2)}, u32[]{:S(2)}) collective-permute-start(bf16[2,128,128]{2,1,0:T(8,128)(2,1)S(1)} %pad_maximum_fusion.1.refs_6_.refs_0_), channel_id=1, source_target_pairs={{0,4},{1,5},{2,6},{3,7},{4,8},{5,9},{6,10},{7,11},{8,12},{9,13},{1... | collective-permute-start | bytes 196616 | tf_op jit(solution)/shard_map/ppermute | solution.py:226
  15.9 1.3 %collective-permute-start.5 = (f32[3,8,256]{2,1,0:T(8,128)S(1)}, f32[3,8,256]{2,1,0:T(8,128)S(1)}, u32[]{:S(2)}, u32[]{:S(2)}) collective-permute-start(f32[3,8,256]{2,1,0:T(8,128)S(1)} %get-tuple-element.26.refs_6_), channel_id=1, source_target_pairs={{0,1},{1,0},{2,3},{3,2},{4,5},{5,4},{6,7},{7,6},{8,9},{9,8},{10,11... | collective-permute-start | bytes 73736 | tf_op jit(solution)/shard_map/ppermute | solution.py:42
  18.0 6.5 %collective-permute-start.8 = (bf16[2,256,128]{2,1,0:T(8,128)(2,1)S(1)}, bf16[2,256,128]{2,1,0:T(8,128)(2,1)S(1)}, u32[]{:S(2)}, u32[]{:S(2)}) collective-permute-start(bf16[2,256,128]{2,1,0:T(8,128)(2,1)S(1)} %get-tuple-element.34), channel_id=1, source_target_pairs={{2,0},{7,1},{4,2},{9,3},{6,4},{11,5},{8,6},{13,7},{10,8},{15,9},{1... | collective-permute-start | bytes 393224 | tf_op jit(solution)/shard_map/ppermute | solution.py:295
  22.0 4.7 %collective-permute-start.7 = (bf16[2,128,128]{2,1,0:T(8,128)(2,1)S(1)}, bf16[2,128,128]{2,1,0:T(8,128)(2,1)S(1)}, u32[]{:S(2)}, u32[]{:S(2)}) collective-permute-start(bf16[2,128,128]{2,1,0:T(8,128)(2,1)S(1)} %get-tuple-element.33), channel_id=1, source_target_pairs={{4,0},{5,1},{6,2},{7,3},{8,4},{9,5},{10,6},{11,7},{12,8},{13,9},{1... | collective-permute-start | bytes 196616 | tf_op jit(solution)/shard_map/ppermute | solution.py:297
  24.6 2.1 %collective-permute-start.9 = (bf16[2,128,128]{2,1,0:T(8,128)(2,1)S(1)}, bf16[2,128,128]{2,1,0:T(8,128)(2,1)S(1)}, u32[]{:S(2)}, u32[]{:S(2)}) collective-permute-start(bf16[2,128,128]{2,1,0:T(8,128)(2,1)S(1)} %fusion.3), channel_id=1, source_target_pairs={{0,1},{1,0},{2,3},{3,2},{4,5},{5,4},{6,7},{7,6},{8,9},{9,8},{10,11... | collective-permute-start | bytes 196616 | tf_op jit(solution)/shard_map/ppermute | solution.py:42
  25.6 1.8 %collective-permute-start.6 = (bf16[128,1024]{1,0:T(8,128)(2,1)S(1)}, bf16[128,1024]{1,0:T(8,128)(2,1)S(1)}, u32[]{:S(2)}, u32[]{:S(2)}) collective-permute-start(bf16[128,1024]{1,0:T(8,128)(2,1)S(1)} %shard_map.83), channel_id=1, source_target_pairs={{0,1},{1,0},{2,3},{3,2},{4,5},{5,4},{6,7},{7,6},{8,9},{9,8},{10,11... | collective-permute-start | bytes 786440 | tf_op jit(solution)/shard_map/ppermute | solution.py:42
